TPU v7x, 1024 devices: a whole 4x4x32 slice. The times are simulated.
1024 devices in a mesh: dp: 16 (over z_lo, core), px: 4 (over x), py: 16 (over y, z_hi).
Axes of the slice: x: 4, y: 4, z: 32 (z_hi: 4, z_lo: 8; z = z_hi * 8 + z_lo), core: 2. Of those that a mesh axis runs over, the one named last changes fastest.
Arguments:
- activations: bfloat16 [16, 64, 16, 64, 128], P('dp', None, 'px', 'py'), may hold values from -6 to 6
- grad_out: bfloat16 [16, 64, 16, 64, 128], P('dp', None, 'px', 'py'), may hold values from -6 to 6
- kernel: bfloat16 [64, 1728], replicated, may hold values from -0.15625 to 0.15625
Outputs:
- grad_input: bfloat16 [16, 64, 16, 64, 128], P('dp', None, 'px', 'py')
- grad_kernel: float32 [64, 1728], P('dp')
All inputs are finite; a program needn't handle non-finite values.
Results may differ from a plain program's by a relative error of at most 0.001.
Values may be sent and summed in bfloat16 or wider, within the bound.
No kernel may reach another device: no remote copies, remote signals or barrier semaphores. Data moves between devices by JAX's collectives and lax.ppermute only.
A program may use at most 32 MiB of HBM per device.

v0:
```python
import math

import jax
import jax.numpy as jnp
from jax import lax
from jax.sharding import PartitionSpec as P


def padded_2(x, sides, width):
    for axis, dim in sides:
        count, length = (lax.axis_size(axis), x.shape[dim])
        up = [(i, (i + 1) % count) for i in range(count - 1)]
        down = [(j, i) for i, j in up]
        last = lax.slice_in_dim(x, length - width, length, axis=dim)
        leading = lax.slice_in_dim(x, 0, width, axis=dim)
        before = lax.ppermute(last, axis, up)
        after = lax.ppermute(leading, axis, down)
        x = jnp.concatenate([before, x, after], axis=dim)
    return x


def local(activations, grad_out, kernel):
    in_channels = activations.shape[1]
    out_channels = grad_out.shape[1]
    size_x = activations.shape[2]
    size_y = activations.shape[3]
    size_z = activations.shape[4]
    cells = size_x * size_y * size_z
    rimmed = padded_2(grad_out, (("px", 2), ("py", 3)), 1)
    padded = jnp.pad(rimmed[0], ((0, 0), (0, 0), (0, 0), (1, 1)))
    flat_activ = activations[0].reshape(in_channels, cells)
    total = jnp.zeros((in_channels, cells), jnp.float32)
    pieces = []
    for offset_a in range(3):
        slices = []
        for offset_b in range(3):
            for offset_c in range(3):
                slices.append(
                    padded[
                        :,
                        2 - offset_a : 2 - offset_a + size_x,
                        2 - offset_b : 2 - offset_b + size_y,
                        2 - offset_c : 2 - offset_c + size_z,
                    ].reshape(out_channels, cells)
                )
        stacked = jnp.concatenate(slices, axis=0)
        block = kernel[:, offset_a * 9 * in_channels : (offset_a + 1) * 9 * in_channels]
        weights = (
            block.reshape(out_channels, 9, in_channels)
            .transpose(1, 0, 2)
            .reshape(9 * out_channels, in_channels)
        )
        total = total + lax.dot_general(
            weights, stacked, (((0,), (0,)), ((), ())), preferred_element_type=jnp.float32
        )
        product = lax.dot_general(
            stacked, flat_activ, (((1,), (1,)), ((), ())), preferred_element_type=jnp.float32
        )
        pieces.append(
            product.reshape(9, out_channels, in_channels)
            .transpose(1, 0, 2)
            .reshape(out_channels, 9 * in_channels)
        )
    grad_input = total.astype(jnp.bfloat16).reshape(1, in_channels, size_x, size_y, size_z)
    local_terms = jnp.concatenate(pieces, axis=1)
    plane = lax.psum(local_terms, ("px", "py"))
    summed = lax.psum_scatter(plane, "dp", scatter_dimension=0, tiled=True)
    whole_cells = lax.axis_size("dp") * lax.axis_size("px") * lax.axis_size("py") * cells
    grad_kernel = summed * (1.0 / math.sqrt(whole_cells))
    return (grad_input, grad_kernel)


def solution(mesh):
    in_specs = (P("dp", None, "px", "py", None), P("dp", None, "px", "py", None), P())
    out_specs = (P("dp", None, "px", "py", None), P("dp", None))
    return jax.shard_map(local, mesh=mesh, in_specs=in_specs, out_specs=out_specs, check_vma=False)
```

profile of v0, /device:TPU:32, one launch (start us, length us, event | category | flops | bytes accessed | tf_op | source)
XLA Modules:
  0.0 978.4 jit_solution(5959970542486395269)
XLA Ops:
  8.2 3.4 collective-permute-start
  11.6 1.3 collective-permute-start.1
  13.5 1.1 constant_dynamic-update-slice_fusion.1
  14.6 3.2 collective-permute-done.1
  18.1 15.7 %collective-permute-start.2 = (bf16[1,64,6,1,128]{4,3,2,1,0:T(2,128)(2,1)S(1)}, bf16[1,64,6,1,128]{4,3,2,1,0:T(2,128)(2,1)S(1)}, u32[]{:S(2)}, u32[]{:S(2)}) collective-permute-start(bf16[1,64,6,1,128]{4,3,2,1,0:T(2,128)(2,1)S(1)} %get-tuple-element.33), channel_id=1, source_target_pairs={{0,1},{1,2},{2,3},{3,4},{4,5},{5,6},{6,7},{7,8},{8,9},{9,10},{10,1... | collective-permute-start | bytes 294920 | tf_op jit(solution)/shard_map/ppermute | solution.py:16
  33.8 1.3 collective-permute-start.3
  35.1 1.1 fusion.5
  39.2 1.3 dynamic-slice
  41.1 3.7 collective-permute-done.2
  44.8 33.4 %collective-permute-done.3 = bf16[1,64,6,1,128]{4,3,2,1,0:T(2,128)(2,1)S(1)} collective-permute-done((bf16[1,64,6,1,128]{4,3,2,1,0:T(2,128)(2,1)S(1)}, bf16[1,64,6,1,128]{4,3,2,1,0:T(2,128)(2,1)S(1)}, u32[]{:S(2)}, u32[]{:S(2)}) %collective-permute-start.3) | collective-permute-done | bytes 98336 | tf_op jit(solution)/shard_map/ppermute | solution.py:17
  79.8 4.2 pad_slice_fusion
  92.0 1.8 reshape.151
  93.8 1.8 reshape.123
  95.6 1.8 reshape.124
  97.4 1.8 reshape.126
  99.3 1.8 reshape.127
  101.1 1.8 reshape.129
  102.9 1.8 reshape.132
  104.8 1.8 reshape.134
  106.6 1.8 reshape.135
  108.4 1.8 reshape.137
  110.3 1.8 reshape.138
  112.1 1.8 reshape.140
  113.9 1.8 reshape.143
  115.7 1.8 reshape.145
  117.6 1.8 reshape.146
  119.4 1.9 reshape.148
  123.9 1.0 constant_dynamic-update-slice_fusion.10
  124.9 1.0 constant_dynamic-update-slice_fusion.9
  125.9 1.0 constant_dynamic-update-slice_fusion.8
  126.9 1.0 constant_dynamic-update-slice_fusion.7
  127.8 1.0 constant_dynamic-update-slice_fusion.6
  129.9 1.6 fusion.6
  132.8 1.5 convolution_bitcast_fusion
  134.2 1.8 copy.23
  136.0 1.1 constant_dynamic-update-slice_fusion.20
  137.1 1.0 constant_dynamic-update-slice_fusion.19
  138.1 1.0 constant_dynamic-update-slice_fusion.18
  139.0 1.0 constant_dynamic-update-slice_fusion.17
  140.0 1.0 constant_dynamic-update-slice_fusion.16
  141.1 1.4 copy-done
  142.5 1.5 convolution_bitcast_fusion.1
  144.0 1.9 copy.22
  145.9 2.0 pad_maximum_fusion
  147.9 2.3 convolution_add_fusion.1
  151.8 207.7 %all-reduce.4.cloned.1.call-done = f32[64,1728]{0,1:T(8,128)} async-done(((f32[64,1728]{0,1:T(8,128)}), f32[64,1728]{0,1:T(8,128)}) %all-reduce.4.cloned.1.call-update) | async-done | bytes 442384
  359.5 1.5 constant_dynamic-slice_fusion
  360.9 609.6 %psum.8 = f32[4,1728]{0,1:T(8,128)S(1)} all-reduce(f32[4,1728]{0,1:T(8,128)S(1)} %constant_dynamic-slice_fusion), channel_id=1, replica_groups=mesh['dp'=16,'px'=4,'py'=16] {'px','py'}, use_global_device_ids=true, to_apply=%region_0.1 | all-reduce | flops 6912 | bytes 55296 | tf_op jit(solution)/shard_map/psum | solution.py:66
  (89 shorter events, 21.8 us)
Async XLA Ops:
  7.2 31.8 %copy-start.19 = (bf16[1,64,4,4,128]{4,3,2,1,0:T(4,128)(2,1)S(1)}, bf16[1,64,4,4,128]{4,3,2,1,0:T(4,128)(2,1)}, u32[]{:S(2)}) copy-start(bf16[1,64,4,4,128]{4,3,2,1,0:T(4,128)(2,1)} %param.3) | copy-start | bytes 786436
  7.2 352.3 %all-reduce.4.cloned.1.call-start = ((), (), s32[]{:S(2)}) async-start(), calls=%async_computation | async-start | bytes 1769472
  8.2 5.3 collective-permute-start
  11.6 6.2 collective-permute-start.1
  18.1 26.7 %collective-permute-start.2 = (bf16[1,64,6,1,128]{4,3,2,1,0:T(2,128)(2,1)S(1)}, bf16[1,64,6,1,128]{4,3,2,1,0:T(2,128)(2,1)S(1)}, u32[]{:S(2)}, u32[]{:S(2)}) collective-permute-start(bf16[1,64,6,1,128]{4,3,2,1,0:T(2,128)(2,1)S(1)} %get-tuple-element.33), channel_id=1, source_target_pairs={{0,1},{1,2},{2,3},{3,4},{4,5},{5,6},{6,7},{7,8},{8,9},{9,10},{10,1... | collective-permute-start | bytes 294920 | tf_op jit(solution)/shard_map/ppermute | solution.py:16
  33.8 44.3 %collective-permute-start.3 = (bf16[1,64,6,1,128]{4,3,2,1,0:T(2,128)(2,1)S(1)}, bf16[1,64,6,1,128]{4,3,2,1,0:T(2,128)(2,1)S(1)}, u32[]{:S(2)}, u32[]{:S(2)}) collective-permute-start(bf16[1,64,6,1,128]{4,3,2,1,0:T(2,128)(2,1)S(1)} %get-tuple-element.34), channel_id=1, source_target_pairs={{1,0},{2,1},{3,2},{4,3},{5,4},{6,5},{7,6},{8,7},{9,8},{10,9},{11,1... | collective-permute-start | bytes 294920 | tf_op jit(solution)/shard_map/ppermute | solution.py:17
  122.1 6.7 copy-start.7
  123.0 5.9 copy-start.11
  123.9 4.9 copy-start.14
  129.9 1.7 copy-start.15
  129.9 1.7 copy-start.6
  129.9 1.8 copy-start.13
  129.9 1.8 copy-start.12
  129.9 1.8 copy-start.16
  131.5 1.0 copy-start.10
  131.6 1.0 copy-start.9
  131.6 1.1 copy-start.8
  131.6 1.2 copy-start.5
  136.0 5.0 copy-start.4
  136.0 5.0 copy-start.3
  136.0 5.0 copy-start.1
  136.0 5.1 copy-start.2
  141.1 1.4 copy-start
  144.0 3.9 copy-start.18
  147.9 2.3 copy-start.17
Sparse Core Ops, SparseCore 0:
  148.0 211.3 all-reduce.3
where the time goes:
time: 980 us; the launch traced here: 978 us
  blocking collectives  610 us (62%)
  waiting for transfers between devices  249 us (25%)
  local copies, waits for them, and re-layouts  72.3 us (7%)
  starting transfers between devices  21.7 us (2%)
  between operations  15.2 us (2%)
    psum x1, blocking collectives, local(): plane = lax.psum(local_terms, ('px', 'py'))  610 us
    unnamed x2, waiting for transfers between devices  208 us
    reshape x27, local copies, waits for them, and re-layouts, local(): slices.append(padded[:, 2 - offset_a:2 - offset_a + size_x, 2 - offset_b:...  39 us
    ppermute x2, waiting for transfers between devices, padded_2(): after = lax.ppermute(leading, axis, down)  36.5 us
  transfers between devices with their start and end apart: 5, of which 5 were waited for; matrix products, arithmetic and copies ran while one was open for 1% of the time, Pallas kernels for 0%

commit v1 on v0

v1 whole, which is shorter than its diff:
```python
import math

import jax
import jax.numpy as jnp
from jax import lax
from jax.experimental import pallas as pl
from jax.experimental.pallas import tpu as pltpu
from jax.sharding import Mesh, PartitionSpec as P

LANES = 128
CH = 64
NX = 4
NY = 4
CELLS = NX * NY * LANES
F32 = jnp.float32
BF16 = jnp.bfloat16
ROWS = 3 * CH


def plane(ref, index):
    return ref[:, index * LANES : (index + 1) * LANES]


def shift_z(x, by):
    lane = lax.broadcasted_iota(jnp.int32, x.shape, 1)
    if by == 1:
        return jnp.where(lane == 0, 0.0, pltpu.roll(x, 1, 1))
    return jnp.where(lane == LANES - 1, 0.0, pltpu.roll(x, LANES - 1, 1))


def collect_z(t):
    return shift_z(t[0:CH], -1) + t[CH : 2 * CH] + shift_z(t[2 * CH : ROWS], 1)


def over_x(get, y):
    return [
        jnp.concatenate([get(x - (a - 1), y) for x in range(NX)], axis=1) for a in range(3)
    ]


def dot_nt(x, y):
    return lax.dot_general(x, y, (((1,), (1,)), ((), ())), preferred_element_type=F32)


def inner_kernel(g_ref, a_ref, below_ref, above_ref, w_ref, gk_ref, gi_ref, edge_ref, a3_ref):
    def get(x, y):
        if x < 0:
            return plane(below_ref, y)
        if x >= NX:
            return plane(above_ref, y)
        return plane(g_ref, x * NY + y)

    for y in range(NY):
        for x in range(NX):
            cells = plane(a_ref, x * NY + y).astype(F32)
            a3_ref[:, x * LANES : (x + 1) * LANES] = jnp.concatenate(
                [shift_z(cells, 1), cells, shift_z(cells, -1)], axis=0
            ).astype(BF16)
        if y == 0:
            edge_ref[:, 0 : NX * LANES] = a3_ref[...]
        if y == NY - 1:
            edge_ref[:, NX * LANES : 2 * NX * LANES] = a3_ref[...]
        taps = [b for b in range(3) if 0 <= y - (b - 1) < NY]
        rows = []
        for b in taps:
            rows += over_x(get, y - (b - 1))
        stack = jnp.concatenate(rows, axis=0)
        first, last = (taps[0] * ROWS, (taps[-1] + 1) * ROWS)
        terms = dot_nt(stack, a3_ref[...])
        if y == 0:
            gk_ref[first:last, :] = terms
            gk_ref[last:, :] = jnp.zeros((3 * ROWS - last, ROWS), F32)
        else:
            gk_ref[first:last, :] += terms
        t = jnp.dot(w_ref[:, first:last], stack, preferred_element_type=F32)
        for x in range(NX):
            lanes = (x * NY + y) * LANES
            gi_ref[:, lanes : lanes + LANES] = collect_z(t[:, x * LANES : (x + 1) * LANES])


def outer_kernel(
    gk_ref, gi_ref, edge_ref, w_ref, low_rim_ref, low_mid_ref, high_rim_ref, high_mid_ref,
    below_ref, above_ref, msg_ref, out_ref, wide_ref,
):
    def get(x, y):
        side = 0 if y < 0 else 1
        if x < 0:
            return plane(below_ref, side)
        if x >= NX:
            return plane(above_ref, side)
        rim, mid = ((low_rim_ref, low_mid_ref), (high_rim_ref, high_mid_ref))[side]
        if x == 0 or x == NX - 1:
            return plane(rim, x // (NX - 1))
        return plane(mid, x - 1)

    low = jnp.concatenate(over_x(get, -1), axis=0)
    high = jnp.concatenate(over_x(get, NY), axis=0)
    half = NX * LANES
    of_low = gk_ref[2 * ROWS : 3 * ROWS, :] + dot_nt(low, edge_ref[:, 0:half])
    of_high = gk_ref[0:ROWS, :] + dot_nt(high, edge_ref[:, half : 2 * half])

    def block(a, b):
        if b == 0:
            return of_high[a * CH : (a + 1) * CH]
        if b == 2:
            return of_low[a * CH : (a + 1) * CH]
        return gk_ref[ROWS + a * CH : ROWS + (a + 1) * CH, :]

    pad = jnp.zeros((CH, 2 * LANES - ROWS), F32)
    lane = lax.broadcasted_iota(jnp.int32, (CH, LANES), 1)
    for m in range(5):
        even = jnp.concatenate([block(*divmod(2 * m, 3)), pad], axis=1)
        wide_ref[3 * m] = even[:, 0:LANES]
        if m == 4:
            wide_ref[3 * m + 1] = even[:, LANES:]
            wide_ref[3 * m + 2] = jnp.zeros((CH, LANES), F32)
            wide_ref[3 * m + 3] = jnp.zeros((CH, LANES), F32)
            break
        odd = jnp.concatenate([block(*divmod(2 * m + 1, 3)), pad], axis=1)
        odd = pltpu.roll(odd, CH, 1)
        wide_ref[3 * m + 1] = jnp.where(lane < CH, even[:, LANES:], odd[:, 0:LANES])
        wide_ref[3 * m + 2] = odd[:, LANES:]
    for s in range(8):
        for column in range(16):
            at = column % 4 * LANES
            msg_ref[s * 4 + column // 4, :, at : at + LANES] = wide_ref[
                column, pl.ds(s, 8, stride=8), :
            ]

    t_low = jnp.dot(w_ref[:, 2 * ROWS : 3 * ROWS], low, preferred_element_type=F32)
    t_high = jnp.dot(w_ref[:, 0:ROWS], high, preferred_element_type=F32)
    for x in range(NX):
        for y in range(NY):
            lanes = (x * NY + y) * LANES
            value = gi_ref[:, lanes : lanes + LANES]
            if y == 0:
                value = value + collect_z(t_low[:, x * LANES : (x + 1) * LANES])
            if y == NY - 1:
                value = value + collect_z(t_high[:, x * LANES : (x + 1) * LANES])
            out_ref[:, lanes : lanes + LANES] = value.astype(BF16)


def call(body, out_shape, scratch):
    return pl.pallas_call(
        body,
        out_shape=out_shape,
        scratch_shapes=scratch,
        compiler_params=pltpu.CompilerParams(vmem_limit_bytes=48 * 1024 * 1024),
    )


def run_inner(*operands):
    shape = jax.ShapeDtypeStruct
    return call(
        inner_kernel,
        (
            shape((3 * ROWS, ROWS), F32),
            shape((CH, CELLS), F32),
            shape((ROWS, 2 * NX * LANES), BF16),
        ),
        [pltpu.VMEM((ROWS, NX * LANES), BF16)],
    )(*operands)


def run_outer(*operands):
    shape = jax.ShapeDtypeStruct
    return call(
        outer_kernel,
        (shape((32, 8, NX * LANES), F32), shape((CH, CELLS), BF16)),
        [pltpu.VMEM((16, CH, LANES), F32)],
    )(*operands)


def shifted_by(x, axis, by):
    count = lax.axis_size(axis)
    pairs = [(i, i + by) for i in range(count) if 0 <= i + by < count]
    return lax.ppermute(x, axis, pairs)


def local(activations, grad_out, kernel):
    py = ("y", "zhi")
    g = grad_out.reshape(CH, CELLS)

    def planes(cells):
        return jnp.concatenate([plane(g, x * NY + y) for x, y in cells], axis=1)

    low_rim = shifted_by(planes([(0, NY - 1), (NX - 1, NY - 1)]), py, 1)
    high_rim = shifted_by(planes([(0, 0), (NX - 1, 0)]), py, -1)
    low_mid = shifted_by(planes([(1, NY - 1), (2, NY - 1)]), py, 1)
    high_mid = shifted_by(planes([(1, 0), (2, 0)]), py, -1)
    below = shifted_by(g[:, 3 * NY * LANES :], "px", 1)
    above = shifted_by(g[:, : NY * LANES], "px", -1)

    a = activations.reshape(CH, CELLS)
    weights = kernel.reshape(CH, 3, 3, ROWS).transpose(3, 2, 1, 0).reshape(ROWS, 3 * ROWS)
    inner = run_inner(g, a, below, above, weights)
    low_rim, high_rim, *inner = lax.optimization_barrier((low_rim, high_rim, *inner))
    corner_below = shifted_by(jnp.concatenate([plane(low_rim, 1), plane(high_rim, 1)], axis=1), "px", 1)
    corner_above = shifted_by(jnp.concatenate([plane(low_rim, 0), plane(high_rim, 0)], axis=1), "px", -1)
    message, grad_input = run_outer(
        *inner, weights, low_rim, low_mid, high_rim, high_mid, corner_below, corner_above
    )

    parts = lax.all_to_all(message, ("core", "px", "y"), 0, 0)
    mine = jnp.sum(parts, axis=0).reshape(8, 1, 4, LANES)
    parts = lax.all_to_all(
        jnp.broadcast_to(mine, (8, 4, 4, LANES)).reshape(32, 4, LANES), ("zlo", "zhi"), 0, 0
    )
    mine = jnp.sum(parts, axis=0)
    parts = lax.all_to_all(jnp.broadcast_to(mine, (16, 4, LANES)), ("px", "y"), 0, 0)
    whole = parts.reshape(4, 16 * LANES)[:, : 9 * ROWS]
    total = 16 * 16 * 64 * 128
    return grad_input.reshape(1, CH, NX, NY, LANES), whole * (1.0 / math.sqrt(total))


def solution(mesh):
    axes = ("zlo", "core", "px", "y", "zhi")
    fine = Mesh(mesh.devices.reshape(8, 2, 4, 4, 4), axes)
    dp, py = ("zlo", "core"), ("y", "zhi")
    cells = P(dp, None, "px", py, None)
    return jax.shard_map(
        local, mesh=fine, in_specs=(cells, cells, P()), out_specs=(cells, P(dp, None)), check_vma=False
    )
```

time: 980 us -> 132 us (0.13)
  blocking collectives: 610 us -> 61.9 us
  waiting for transfers between devices: 249 us -> 13.7 us
  local copies, waits for them, and re-layouts: 72.3 us -> 4.19 us
  starting transfers between devices: 21.7 us -> 47.9 us
  between operations: 15.2 us -> 0.89 us
    psum x1 -> x0, blocking collectives: 610 us -> none  [local(): plane = lax.psum(local_terms, ('px', 'py'))]
    unnamed x2 -> x0, waiting for transfers between devices: 208 us -> none
    all_to_all x0 -> x2, blocking collectives: none -> 61.9 us  [the longest x1 41.1 us: local(): lax.all_to_all(jnp.broadcast_to(mine, (8, 4, 4, LANES)).reshape(32, 4, LA...]
    reshape x28 -> x6, local copies, waits for them, and re-layouts: 39.9 us -> 2.72 us  [the longest x1 1.13 us: local(): g = grad_out.reshape(CH, CELLS)]
    ppermute x4 -> x8, waiting for transfers between devices: 40.8 us -> 7.04 us  [shifted_by(): return lax.ppermute(x, axis, pairs)]
    ppermute x4 -> x8, starting transfers between devices: 21.7 us -> 44.4 us  [shifted_by(): return lax.ppermute(x, axis, pairs)]
    unnamed x72 -> x4, local copies, waits for them, and re-layouts: 18.5 us -> 0.75 us
  transfers between devices with their start and end apart: 5 -> 9, of which waited for: 5 -> 2; matrix products, arithmetic and copies ran while one was open for 1% -> 1% of each run, Pallas kernels for 0% -> 1%
where the time goes in v1:
time: 132 us; the launch traced here: 131 us
  blocking collectives  61.9 us (47%)
  starting transfers between devices  47.9 us (36%)
  waiting for transfers between devices  13.7 us (10%)
  local copies, waits for them, and re-layouts  4.19 us (3%)
  Pallas kernels  1.92 us (1%)
    ppermute x8, starting transfers between devices, shifted_by(): return lax.ppermute(x, axis, pairs)  44.4 us
    all_to_all x1, blocking collectives, local(): lax.all_to_all(jnp.broadcast_to(mine, (8, 4, 4, LANES)).reshape(32, 4, LA...  41.1 us
    all_to_all x1, blocking collectives, local(): parts = lax.all_to_all(message, ('core', 'px', 'y'), 0, 0)  20.8 us
    ppermute x8, waiting for transfers between devices, shifted_by(): return lax.ppermute(x, axis, pairs)  7.04 us
    all_to_all x1, waiting for transfers between devices, local(): lax.all_to_all(jnp.broadcast_to(mine, (16, 4, LANES)), ('px', 'y'), 0, 0)  6.69 us
    all_to_all x1, starting transfers between devices, local(): lax.all_to_all(jnp.broadcast_to(mine, (16, 4, LANES)), ('px', 'y'), 0, 0)  3.48 us
  transfers between devices with their start and end apart: 9, of which 2 were waited for; matrix products, arithmetic and copies ran while one was open for 1% of the time, Pallas kernels for 1%

profile of v1, /device:TPU:32, one launch (start us, length us, event | category | flops | bytes accessed | tf_op | source)
XLA Modules:
  0.0 131.2 jit_solution(894628338094228570)
XLA Ops:
  0.6 1.1 reshape.27.g_ref
  1.8 0.0 copy-start
  1.8 15.9 %collective-permute-start = (bf16[64,256]{1,0:T(8,128)(2,1)S(1)}, bf16[64,256]{1,0:T(8,128)(2,1)S(1)}, u32[]{:S(2)}, u32[]{:S(2)}) collective-permute-start(bf16[64,256]{1,0:T(8,128)(2,1)S(1)} %pad_maximum_fusion), channel_id=1, source_target_pairs={{0,1},{1,2},{2,3},{3,4},{4,5},{5,6},{6,7},{7,8},{8,9},{9,10},{10,1... | collective-permute-start | bytes 98312 | tf_op jit(solution)/shard_map/ppermute | solution.py:177
  17.7 1.3 collective-permute-start.1
  19.0 15.5 %collective-permute-start.4 = (bf16[64,256]{1,0:T(8,128)(2,1)S(1)}, bf16[64,256]{1,0:T(8,128)(2,1)S(1)}, u32[]{:S(2)}, u32[]{:S(2)}) collective-permute-start(bf16[64,256]{1,0:T(8,128)(2,1)S(1)} %pad_maximum_fusion.2), channel_id=1, source_target_pairs={{0,1},{1,2},{2,3},{3,4},{4,5},{5,6},{6,7},{7,8},{8,9},{9,10},{10,1... | collective-permute-start | bytes 98312 | tf_op jit(solution)/shard_map/ppermute | solution.py:177
  34.5 1.3 collective-permute-start.3
  35.8 4.5 %collective-permute-start.2 = (bf16[64,512]{1,0:T(8,128)(2,1)S(1)}, bf16[64,512]{1,0:T(8,128)(2,1)S(1)}, u32[]{:S(2)}, u32[]{:S(2)}) collective-permute-start(bf16[64,512]{1,0:T(8,128)(2,1)S(1)} %get-tuple-element.31), channel_id=1, source_target_pairs={{0,16},{16,32},{32,48},{1,17},{17,33},{33,49},{2,18},{18,34},{34,5... | collective-permute-start | bytes 196616 | tf_op jit(solution)/shard_map/ppermute | solution.py:177
  40.4 0.0 copy-done
  40.4 0.0 copy-start.1
  40.4 0.2 reshape.28.a_ref
  40.6 0.7 copy-done.1
  41.3 0.3 reshape.29
  41.7 0.2 copy.15.w_ref
  41.9 0.0 collective-permute-done.3.above_ref
  41.9 1.3 collective-permute-start.5
  43.2 0.0 collective-permute-done.2.below_ref
  43.2 1.4 %shard_map.50 = (f32[576,192]{1,0:T(8,128)S(1)}, f32[64,2048]{1,0:T(8,128)S(1)}, bf16[192,1024]{1,0:T(8,128)(2,1)S(1)}) custom-call(bf16[64,2048]{1,0:T(8,128)(2,1)S(1)} %reshape.27.g_ref, bf16[64,2048]{1,0:T(8,128)(2,1)S(1)} %reshape.28.a_ref, bf16[64,512]{1,0:T(8,128)(2,1)S(1)} %collective-permute-done.2.below_ref, ...), custom_call_target="tpu_custom_call" | custom-call | tf_op jit(solution)/shard_map/pallas_call | solution.py:154
  44.6 0.0 collective-permute-done.low_rim_ref
  44.6 0.0 collective-permute-done.1.high_rim_ref
  44.7 3.4 %collective-permute-start.6 = (bf16[64,256]{1,0:T(8,128)(2,1)S(1)}, bf16[64,256]{1,0:T(8,128)(2,1)S(1)}, u32[]{:S(2)}, u32[]{:S(2)}) collective-permute-start(bf16[64,256]{1,0:T(8,128)(2,1)S(1)} %pad_maximum_fusion.4), channel_id=1, source_target_pairs={{0,16},{16,32},{32,48},{1,17},{17,33},{33,49},{2,18},{18,34},{34,5... | collective-permute-start | bytes 98312 | tf_op jit(solution)/shard_map/ppermute | solution.py:177
  48.1 1.3 collective-permute-start.7
  49.4 0.0 collective-permute-done.4.low_mid_ref
  49.4 7.0 %collective-permute-done.5.high_mid_ref = bf16[64,256]{1,0:T(8,128)(2,1)S(1)} collective-permute-done((bf16[64,256]{1,0:T(8,128)(2,1)S(1)}, bf16[64,256]{1,0:T(8,128)(2,1)S(1)}, u32[]{:S(2)}, u32[]{:S(2)}) %collective-permute-start.5) | collective-permute-done | bytes 32800 | tf_op jit(solution)/shard_map/ppermute | solution.py:177
  56.4 0.0 collective-permute-done.6.below_ref
  56.4 0.0 collective-permute-done.7.above_ref
  56.4 0.5 shard_map.51
  56.9 20.8 %all_to_all.15 = f32[32,8,512]{2,1,0:T(8,128)S(1)} all-to-all(f32[32,8,512]{2,1,0:T(8,128)S(1)} %get-tuple-element.21), channel_id=1, replica_groups=mesh['zlo'=8,'core'=2,'px'=4,'y'=4,'zhi'=4] {'core','px','y'}, dimensions={0} | all-to-all | bytes 1048576 | tf_op jit(solution)/shard_map/all_to_all | solution.py:204
  77.8 41.1 %all_to_all.16 = f32[32,4,128]{2,1,0:T(4,128)S(1)} all-to-all(f32[32,4,128]{2,1,0:T(4,128)S(1)} %bitcast.5), channel_id=1, replica_groups=mesh['zlo'=8,'core'=2,'px'=4,'y'=4,'zhi'=4] {'zlo','zhi'}, dimensions={0} | all-to-all | bytes 131072 | tf_op jit(solution)/shard_map/all_to_all | solution.py:206
  118.9 0.6 broadcast_in_dim.12
  119.5 3.5 %all-to-all-start.2 = ((f32[16,4,128]{2,1,0:T(4,128)}), f32[16,4,128]{2,1,0:T(4,128)S(1)}, u32[]{:S(2)}, u32[]{:S(2)}) async-start(f32[16,4,128]{2,1,0:T(4,128)} %broadcast_in_dim.12), calls=%async_computation.2 | async-start | bytes 65536 | tf_op jit(solution)/shard_map/all_to_all | solution.py:210
  123.0 0.9 reshape.31
  123.9 6.7 %all-to-all-done.2 = f32[16,4,128]{2,1,0:T(4,128)S(1)} async-done(((f32[16,4,128]{2,1,0:T(4,128)}), f32[16,4,128]{2,1,0:T(4,128)S(1)}, u32[]{:S(2)}, u32[]{:S(2)}) %all-to-all-start.2) | async-done | bytes 32800 | tf_op jit(solution)/shard_map/all_to_all | solution.py:210
  130.6 0.6 slice_multiply_fusion
  (15 shorter events, 0.3 us)
Async XLA Ops:
  1.8 38.6 %copy-start = (bf16[1,64,4,4,128]{4,3,2,1,0:T(4,128)(2,1)S(1)}, bf16[1,64,4,4,128]{4,3,2,1,0:T(4,128)(2,1)}, u32[]{:S(2)}) copy-start(bf16[1,64,4,4,128]{4,3,2,1,0:T(4,128)(2,1)} %param.3) | copy-start | bytes 786436
  1.8 42.8 %collective-permute-start = (bf16[64,256]{1,0:T(8,128)(2,1)S(1)}, bf16[64,256]{1,0:T(8,128)(2,1)S(1)}, u32[]{:S(2)}, u32[]{:S(2)}) collective-permute-start(bf16[64,256]{1,0:T(8,128)(2,1)S(1)} %pad_maximum_fusion), channel_id=1, source_target_pairs={{0,1},{1,2},{2,3},{3,4},{4,5},{5,6},{6,7},{7,8},{8,9},{9,10},{10,1... | collective-permute-start | bytes 98312 | tf_op jit(solution)/shard_map/ppermute | solution.py:177
  17.7 26.9 %collective-permute-start.1 = (bf16[64,256]{1,0:T(8,128)(2,1)S(1)}, bf16[64,256]{1,0:T(8,128)(2,1)S(1)}, u32[]{:S(2)}, u32[]{:S(2)}) collective-permute-start(bf16[64,256]{1,0:T(8,128)(2,1)S(1)} %pad_maximum_fusion.1), channel_id=1, source_target_pairs={{1,0},{2,1},{3,2},{4,3},{5,4},{6,5},{7,6},{8,7},{9,8},{10,9},{11,1... | collective-permute-start | bytes 98312 | tf_op jit(solution)/shard_map/ppermute | solution.py:177
  19.0 30.4 %collective-permute-start.4 = (bf16[64,256]{1,0:T(8,128)(2,1)S(1)}, bf16[64,256]{1,0:T(8,128)(2,1)S(1)}, u32[]{:S(2)}, u32[]{:S(2)}) collective-permute-start(bf16[64,256]{1,0:T(8,128)(2,1)S(1)} %pad_maximum_fusion.2), channel_id=1, source_target_pairs={{0,1},{1,2},{2,3},{3,4},{4,5},{5,6},{6,7},{7,8},{8,9},{9,10},{10,1... | collective-permute-start | bytes 98312 | tf_op jit(solution)/shard_map/ppermute | solution.py:177
  34.5 7.4 %collective-permute-start.3 = (bf16[64,512]{1,0:T(8,128)(2,1)S(1)}, bf16[64,512]{1,0:T(8,128)(2,1)S(1)}, u32[]{:S(2)}, u32[]{:S(2)}) collective-permute-start(bf16[64,512]{1,0:T(8,128)(2,1)S(1)} %get-tuple-element.30), channel_id=1, source_target_pairs={{16,0},{32,16},{48,32},{17,1},{33,17},{49,33},{18,2},{34,18},{50,3... | collective-permute-start | bytes 196616 | tf_op jit(solution)/shard_map/ppermute | solution.py:177
  35.8 7.4 %collective-permute-start.2 = (bf16[64,512]{1,0:T(8,128)(2,1)S(1)}, bf16[64,512]{1,0:T(8,128)(2,1)S(1)}, u32[]{:S(2)}, u32[]{:S(2)}) collective-permute-start(bf16[64,512]{1,0:T(8,128)(2,1)S(1)} %get-tuple-element.31), channel_id=1, source_target_pairs={{0,16},{16,32},{32,48},{1,17},{17,33},{33,49},{2,18},{18,34},{34,5... | collective-permute-start | bytes 196616 | tf_op jit(solution)/shard_map/ppermute | solution.py:177
  40.4 0.9 copy-start.1
  41.9 14.5 %collective-permute-start.5 = (bf16[64,256]{1,0:T(8,128)(2,1)S(1)}, bf16[64,256]{1,0:T(8,128)(2,1)S(1)}, u32[]{:S(2)}, u32[]{:S(2)}) collective-permute-start(bf16[64,256]{1,0:T(8,128)(2,1)S(1)} %pad_maximum_fusion.3), channel_id=1, source_target_pairs={{1,0},{2,1},{3,2},{4,3},{5,4},{6,5},{7,6},{8,7},{9,8},{10,9},{11,1... | collective-permute-start | bytes 98312 | tf_op jit(solution)/shard_map/ppermute | solution.py:177
  44.7 11.8 %collective-permute-start.6 = (bf16[64,256]{1,0:T(8,128)(2,1)S(1)}, bf16[64,256]{1,0:T(8,128)(2,1)S(1)}, u32[]{:S(2)}, u32[]{:S(2)}) collective-permute-start(bf16[64,256]{1,0:T(8,128)(2,1)S(1)} %pad_maximum_fusion.4), channel_id=1, source_target_pairs={{0,16},{16,32},{32,48},{1,17},{17,33},{33,49},{2,18},{18,34},{34,5... | collective-permute-start | bytes 98312 | tf_op jit(solution)/shard_map/ppermute | solution.py:177
  48.1 8.3 %collective-permute-start.7 = (bf16[64,256]{1,0:T(8,128)(2,1)S(1)}, bf16[64,256]{1,0:T(8,128)(2,1)S(1)}, u32[]{:S(2)}, u32[]{:S(2)}) collective-permute-start(bf16[64,256]{1,0:T(8,128)(2,1)S(1)} %pad_maximum_fusion.5), channel_id=1, source_target_pairs={{16,0},{32,16},{48,32},{17,1},{33,17},{49,33},{18,2},{34,18},{50,3... | collective-permute-start | bytes 98312 | tf_op jit(solution)/shard_map/ppermute | solution.py:177
  119.5 11.0 %all-to-all-start.2 = ((f32[16,4,128]{2,1,0:T(4,128)}), f32[16,4,128]{2,1,0:T(4,128)S(1)}, u32[]{:S(2)}, u32[]{:S(2)}) async-start(f32[16,4,128]{2,1,0:T(4,128)} %broadcast_in_dim.12), calls=%async_computation.2 | async-start | bytes 65536 | tf_op jit(solution)/shard_map/all_to_all | solution.py:210

commit v2 on v1

v2 whole, which is shorter than its diff:
```python
import math

import jax
import jax.numpy as jnp
from jax import lax
from jax.experimental import pallas as pl
from jax.experimental.pallas import tpu as pltpu
from jax.sharding import Mesh, PartitionSpec as P

LANES = 128
CH = 64
NX = 4
NY = 4
CELLS = NX * NY * LANES
F32 = jnp.float32
BF16 = jnp.bfloat16
ROWS = 3 * CH
HALF = NX * LANES
WIDE = (NX + 2) * LANES


def plane(ref, index):
    return ref[:, index * LANES : (index + 1) * LANES]


def shift_z(x, by):
    lane = lax.broadcasted_iota(jnp.int32, x.shape, 1)
    if by == 1:
        return jnp.where(lane == 0, 0.0, pltpu.roll(x, 1, 1))
    return jnp.where(lane == LANES - 1, 0.0, pltpu.roll(x, LANES - 1, 1))


def collect_z(t):
    return shift_z(t[0:CH], -1) + t[CH : 2 * CH] + shift_z(t[2 * CH : ROWS], 1)


def over_x(get, y):
    return [
        jnp.concatenate([get(x - (a - 1), y) for x in range(NX)], axis=1) for a in range(3)
    ]


def dot_nt(x, y):
    return lax.dot_general(x, y, (((1,), (1,)), ((), ())), preferred_element_type=F32)


def all_shifts(cells):
    cells = cells.astype(F32)
    return jnp.concatenate([shift_z(cells, 1), cells, shift_z(cells, -1)], axis=0).astype(BF16)


def inner_kernel(g_ref, a_ref, gk_ref, row_ref, column_ref, a3_ref):
    def get(x, y):
        if x < 0 or x >= NX:
            return jnp.zeros((CH, LANES), BF16)
        return plane(g_ref, x * NY + y)

    for y in range(NY):
        for x in range(NX):
            a3_ref[:, x * LANES : (x + 1) * LANES] = all_shifts(plane(a_ref, x * NY + y))
        if y in (0, NY - 1):
            at = y // (NY - 1) * HALF
            row_ref[:, at : at + HALF] = a3_ref[...]
        for side in range(2):
            at = side * HALF + y * LANES
            column_ref[:, at : at + LANES] = plane(a3_ref, side * (NX - 1))
        taps = [b for b in range(3) if 0 <= y - (b - 1) < NY]
        rows = []
        for b in taps:
            rows += over_x(get, y - (b - 1))
        first, last = (taps[0] * ROWS, (taps[-1] + 1) * ROWS)
        terms = dot_nt(jnp.concatenate(rows, axis=0), a3_ref[...])
        if y == 0:
            gk_ref[first:last, :] = terms
            gk_ref[last:, :] = jnp.zeros((3 * ROWS - last, ROWS), F32)
        else:
            gk_ref[first:last, :] += terms


def message_kernel(
    gk_ref, row_ref, column_ref, below_ref, above_ref, low_ref, high_ref, msg_ref, wide_ref, rim_ref
):
    for side in range(2):
        at = side * WIDE
        rim_ref[:, at : at + LANES] = all_shifts(plane(below_ref, NY + side))
        rim_ref[:, at + LANES : at + LANES + HALF] = row_ref[:, side * HALF : (side + 1) * HALF]
        rim_ref[:, at + LANES + HALF : at + WIDE] = all_shifts(plane(above_ref, NY + side))

    def block(a, b):
        value = gk_ref[b * ROWS + a * CH : b * ROWS + (a + 1) * CH, :]
        if a != 1:
            face, side = (above_ref, 1) if a == 0 else (below_ref, 0)
            rows = [y for y in range(NY) if 0 <= y - (b - 1) < NY]
            of_g = (rows[0] - (b - 1)) * LANES
            of_a = side * HALF + rows[0] * LANES
            size = len(rows) * LANES
            value = value + dot_nt(face[:, of_g : of_g + size], column_ref[:, of_a : of_a + size])
        if b != 1:
            face, side = (high_ref, 1) if b == 0 else (low_ref, 0)
            at = side * WIDE + a * LANES
            value = value + dot_nt(face[...], rim_ref[:, at : at + HALF])
        return value

    pad = jnp.zeros((CH, 2 * LANES - ROWS), F32)
    lane = lax.broadcasted_iota(jnp.int32, (CH, LANES), 1)
    for m in range(5):
        even = jnp.concatenate([block(*divmod(2 * m, 3)), pad], axis=1)
        wide_ref[3 * m] = even[:, 0:LANES]
        if m == 4:
            wide_ref[3 * m + 1] = even[:, LANES:]
            wide_ref[3 * m + 2] = jnp.zeros((CH, LANES), F32)
            wide_ref[3 * m + 3] = jnp.zeros((CH, LANES), F32)
            break
        odd = jnp.concatenate([block(*divmod(2 * m + 1, 3)), pad], axis=1)
        odd = pltpu.roll(odd, CH, 1)
        wide_ref[3 * m + 1] = jnp.where(lane < CH, even[:, LANES:], odd[:, 0:LANES])
        wide_ref[3 * m + 2] = odd[:, LANES:]
    for s in range(8):
        for column in range(16):
            at = column % 4 * LANES
            msg_ref[s * 4 + column // 4, :, at : at + LANES] = wide_ref[
                column, pl.ds(s, 8, stride=8), :
            ]


def input_kernel(
    g_ref, w_ref, below_ref, above_ref, low_ref, high_ref, corner_below_ref, corner_above_ref, out_ref
):
    def get(x, y):
        if 0 <= y < NY:
            if x < 0:
                return plane(below_ref, y)
            if x >= NX:
                return plane(above_ref, y)
            return plane(g_ref, x * NY + y)
        side = 0 if y < 0 else 1
        if x < 0:
            return plane(corner_below_ref, side)
        if x >= NX:
            return plane(corner_above_ref, side)
        return plane((low_ref, high_ref)[side], x)

    for y in range(NY):
        rows = []
        for b in range(3):
            rows += over_x(get, y - (b - 1))
        t = jnp.dot(w_ref[...], jnp.concatenate(rows, axis=0), preferred_element_type=F32)
        for x in range(NX):
            lanes = (x * NY + y) * LANES
            out_ref[:, lanes : lanes + LANES] = collect_z(
                t[:, x * LANES : (x + 1) * LANES]
            ).astype(BF16)


def call(body, out_shape, scratch=(), cost=None):
    return pl.pallas_call(
        body,
        out_shape=out_shape,
        scratch_shapes=scratch,
        cost_estimate=cost,
        compiler_params=pltpu.CompilerParams(vmem_limit_bytes=48 * 1024 * 1024),
    )


def run_inner(*operands):
    shape = jax.ShapeDtypeStruct
    return call(
        inner_kernel,
        (shape((3 * ROWS, ROWS), F32), shape((ROWS, 2 * HALF), BF16), shape((ROWS, 2 * HALF), BF16)),
        [pltpu.VMEM((ROWS, HALF), BF16)],
        pl.CostEstimate(flops=20 * 10**9, transcendentals=0, bytes_accessed=2**20),
    )(*operands)


def run_message(*operands):
    return call(
        message_kernel,
        jax.ShapeDtypeStruct((32, 8, HALF), F32),
        [pltpu.VMEM((16, CH, LANES), F32), pltpu.VMEM((ROWS, 2 * WIDE), BF16)],
    )(*operands)


def run_input(*operands):
    return call(input_kernel, jax.ShapeDtypeStruct((CH, CELLS), BF16))(*operands)


def shifted_by(x, axis, by):
    count = lax.axis_size(axis)
    pairs = [(i, i + by) for i in range(count) if 0 <= i + by < count]
    return lax.ppermute(x, axis, pairs)


def local(activations, grad_out, kernel):
    py = ("y", "zhi")
    g = grad_out.reshape(CH, CELLS)

    def planes(cells):
        return jnp.concatenate([plane(g, x * NY + y) for x, y in cells], axis=1)

    low = shifted_by(planes([(x, NY - 1) for x in range(NX)]), py, 1)
    high = shifted_by(planes([(x, 0) for x in range(NX)]), py, -1)

    a = activations.reshape(CH, CELLS)

    weights = kernel.reshape(CH, 3, 3, ROWS).transpose(3, 2, 1, 0).reshape(ROWS, 3 * ROWS)

    def x_face(x):
        rows = g[:, x * NY * LANES : (x + 1) * NY * LANES]
        return jnp.concatenate([rows, plane(a, x * NY), plane(a, x * NY + NY - 1)], axis=1)

    below = shifted_by(x_face(NX - 1), "px", 1)
    above = shifted_by(x_face(0), "px", -1)
    inner = run_inner(g, a)
    weights, *inner = lax.optimization_barrier((weights, *inner))
    message = run_message(*inner, below, above, low, high)

    parts = lax.all_to_all(message, ("core", "px", "y"), 0, 0)
    mine = jnp.sum(parts, axis=0).reshape(8, 1, 4, LANES)
    mine, low, high = lax.optimization_barrier((mine, low, high))
    parts = lax.all_to_all(
        jnp.broadcast_to(mine, (8, 4, 4, LANES)).reshape(32, 4, LANES), ("zlo", "zhi"), 0, 0
    )
    last = (NX - 1) * LANES
    corner_below = shifted_by(jnp.concatenate([low[:, last:], high[:, last:]], axis=1), "px", 1)
    corner_above = shifted_by(jnp.concatenate([plane(low, 0), plane(high, 0)], axis=1), "px", -1)
    grad_input = run_input(g, weights, below, above, low, high, corner_below, corner_above)
    parts, grad_input = lax.optimization_barrier((parts, grad_input))
    mine = jnp.sum(parts, axis=0)
    parts = lax.all_to_all(jnp.broadcast_to(mine, (16, 4, LANES)), ("px", "y"), 0, 0)
    whole = parts.reshape(4, 16 * LANES)[:, : 9 * ROWS]
    total = 16 * 16 * 64 * 128
    return grad_input.reshape(1, CH, NX, NY, LANES), whole * (1.0 / math.sqrt(total))


def solution(mesh):
    axes = ("zlo", "core", "px", "y", "zhi")
    fine = Mesh(mesh.devices.reshape(8, 2, 4, 4, 4), axes)
    dp, py = ("zlo", "core"), ("y", "zhi")
    cells = P(dp, None, "px", py, None)
    return jax.shard_map(
        local, mesh=fine, in_specs=(cells, cells, P()), out_specs=(cells, P(dp, None)), check_vma=False
    )
```

time: 132 us -> 117 us (0.89)
  blocking collectives: 61.9 us -> 19.1 us
  waiting for transfers between devices: 13.7 us -> 42.6 us
    all_to_all x1 -> x0, blocking collectives: 41.1 us -> none  [local(): lax.all_to_all(jnp.broadcast_to(mine, (8, 4, 4, LANES)).reshape(32, 4, LA...]
    ppermute x8 -> x6, starting transfers between devices: 44.4 us -> 25.9 us  [shifted_by(): return lax.ppermute(x, axis, pairs)]
    all_to_all x0 -> x1, starting transfers between devices: none -> 17.5 us  [local(): lax.all_to_all(jnp.broadcast_to(mine, (8, 4, 4, LANES)).reshape(32, 4, LA...]
    ppermute x8 -> x6, waiting for transfers between devices: 7.04 us -> 22.3 us  [shifted_by(): return lax.ppermute(x, axis, pairs)]
    all_to_all x0 -> x1, waiting for transfers between devices: none -> 13.6 us  [local(): lax.all_to_all(jnp.broadcast_to(mine, (8, 4, 4, LANES)).reshape(32, 4, LA...]
    all_to_all x1, blocking collectives: 20.8 us -> 19.1 us  [local(): parts = lax.all_to_all(message, ('core', 'px', 'y'), 0, 0)]
  transfers between devices with their start and end apart: 9 -> 8, of which waited for: 2 -> 5; matrix products, arithmetic and copies ran while one was open for 1% -> 1% of each run, Pallas kernels for 1% -> 1%
where the time goes in v2:
time: 117 us
  starting transfers between devices  46.9 us (40%)
  waiting for transfers between devices  42.6 us (36%)
  blocking collectives  19.1 us (16%)
  local copies, waits for them, and re-layouts  4.09 us (3%)
  Pallas kernels  2.61 us (2%)
    ppermute x6, starting transfers between devices, shifted_by(): return lax.ppermute(x, axis, pairs)  25.9 us
    ppermute x6, waiting for transfers between devices, shifted_by(): return lax.ppermute(x, axis, pairs)  22.3 us
    all_to_all x1, blocking collectives, local(): parts = lax.all_to_all(message, ('core', 'px', 'y'), 0, 0)  19.1 us
    all_to_all x1, starting transfers between devices, local(): lax.all_to_all(jnp.broadcast_to(mine, (8, 4, 4, LANES)).reshape(32, 4, LA...  17.5 us
    all_to_all x1, waiting for transfers between devices, local(): lax.all_to_all(jnp.broadcast_to(mine, (8, 4, 4, LANES)).reshape(32, 4, LA...  13.6 us
    all_to_all x1, waiting for transfers between devices, local(): lax.all_to_all(jnp.broadcast_to(mine, (16, 4, LANES)), ('px', 'y'), 0, 0)  6.69 us
    all_to_all x1, starting transfers between devices, local(): lax.all_to_all(jnp.broadcast_to(mine, (16, 4, LANES)), ('px', 'y'), 0, 0)  3.48 us
  transfers between devices with their start and end apart: 8, of which 5 were waited for; matrix products, arithmetic and copies ran while one was open for 1% of the time, Pallas kernels for 1%

profile of v2, /device:TPU:32, one launch (start us, length us, event | category | flops | bytes accessed | tf_op | source)
XLA Modules:
  0.0 116.9 jit_solution(12587529348497921651)
XLA Ops:
  0.6 1.1 reshape.30.g_ref
  1.8 0.0 copy-start
  1.8 15.9 %collective-permute-start.2 = (bf16[64,512]{1,0:T(8,128)(2,1)S(1)}, bf16[64,512]{1,0:T(8,128)(2,1)S(1)}, u32[]{:S(2)}, u32[]{:S(2)}) collective-permute-start(bf16[64,512]{1,0:T(8,128)(2,1)S(1)} %pad_maximum_fusion.2), channel_id=1, source_target_pairs={{0,1},{1,2},{2,3},{3,4},{4,5},{5,6},{6,7},{7,8},{8,9},{9,10},{10,1... | collective-permute-start | bytes 196616 | tf_op jit(solution)/shard_map/ppermute | solution.py:190
  17.7 1.3 %collective-permute-start.3 = (bf16[64,512]{1,0:T(8,128)(2,1)S(1)}, bf16[64,512]{1,0:T(8,128)(2,1)S(1)}, u32[]{:S(2)}, u32[]{:S(2)}) collective-permute-start(bf16[64,512]{1,0:T(8,128)(2,1)S(1)} %pad_maximum_fusion.3), channel_id=1, source_target_pairs={{1,0},{2,1},{3,2},{4,3},{5,4},{6,5},{7,6},{8,7},{9,8},{10,9},{11,1... | collective-permute-start | bytes 196616 | tf_op jit(solution)/shard_map/ppermute | solution.py:190
  19.0 0.0 copy-done
  19.0 0.2 reshape.31.a_ref
  19.3 3.4 %collective-permute-start = (bf16[64,768]{1,0:T(8,128)(2,1)S(1)}, bf16[64,768]{1,0:T(8,128)(2,1)S(1)}, u32[]{:S(2)}, u32[]{:S(2)}) collective-permute-start(bf16[64,768]{1,0:T(8,128)(2,1)S(1)} %pad_maximum_fusion), channel_id=1, source_target_pairs={{0,16},{16,32},{32,48},{1,17},{17,33},{33,49},{2,18},{18,34},{34,5... | collective-permute-start | bytes 294920 | tf_op jit(solution)/shard_map/ppermute | solution.py:190
  22.7 0.0 copy-start.1
  22.7 1.4 %collective-permute-start.1 = (bf16[64,768]{1,0:T(8,128)(2,1)S(1)}, bf16[64,768]{1,0:T(8,128)(2,1)S(1)}, u32[]{:S(2)}, u32[]{:S(2)}) collective-permute-start(bf16[64,768]{1,0:T(8,128)(2,1)S(1)} %pad_maximum_fusion.1), channel_id=1, source_target_pairs={{16,0},{32,16},{48,32},{17,1},{33,17},{49,33},{18,2},{34,18},{50,3... | collective-permute-start | bytes 294920 | tf_op jit(solution)/shard_map/ppermute | solution.py:190
  24.1 0.9 shard_map.50
  25.0 0.0 copy-done.1
  25.0 0.3 reshape.28
  25.4 0.0 collective-permute-done.2.low_ref
  25.4 17.9 %collective-permute-done.3.high_ref = bf16[64,512]{1,0:T(8,128)(2,1)S(1)} collective-permute-done((bf16[64,512]{1,0:T(8,128)(2,1)S(1)}, bf16[64,512]{1,0:T(8,128)(2,1)S(1)}, u32[]{:S(2)}, u32[]{:S(2)}) %collective-permute-start.3) | collective-permute-done | bytes 65568 | tf_op jit(solution)/shard_map/ppermute | solution.py:190
  43.4 0.0 collective-permute-done.below_ref
  43.4 0.0 collective-permute-done.1.above_ref
  43.4 0.9 shard_map.51
  44.2 19.1 %all_to_all.15 = f32[32,8,512]{2,1,0:T(8,128)S(1)} all-to-all(f32[32,8,512]{2,1,0:T(8,128)S(1)} %shard_map.51), channel_id=1, replica_groups=mesh['zlo'=8,'core'=2,'px'=4,'y'=4,'zhi'=4] {'core','px','y'}, dimensions={0} | all-to-all | bytes 1048576 | tf_op jit(solution)/shard_map/all_to_all | solution.py:217
  63.4 0.6 broadcast_in_dim.11
  64.0 17.5 %all-to-all-start.1 = ((f32[32,4,128]{2,1,0:T(4,128)}), f32[32,4,128]{2,1,0:T(4,128)S(1)}, u32[]{:S(2)}, u32[]{:S(2)}) async-start(f32[32,4,128]{2,1,0:T(4,128)} %bitcast.4), calls=%async_computation.1 | async-start | bytes 131072 | tf_op jit(solution)/shard_map/all_to_all | solution.py:220
  81.6 2.7 %collective-permute-start.4 = (bf16[64,256]{1,0:T(8,128)(2,1)S(1)}, bf16[64,256]{1,0:T(8,128)(2,1)S(1)}, u32[]{:S(2)}, u32[]{:S(2)}) collective-permute-start(bf16[64,256]{1,0:T(8,128)(2,1)S(1)} %pad_maximum_fusion.4), channel_id=1, source_target_pairs={{0,16},{16,32},{32,48},{1,17},{17,33},{33,49},{2,18},{18,34},{34,5... | collective-permute-start | bytes 98312 | tf_op jit(solution)/shard_map/ppermute | solution.py:190
  84.3 1.3 %collective-permute-start.5 = (bf16[64,256]{1,0:T(8,128)(2,1)S(1)}, bf16[64,256]{1,0:T(8,128)(2,1)S(1)}, u32[]{:S(2)}, u32[]{:S(2)}) collective-permute-start(bf16[64,256]{1,0:T(8,128)(2,1)S(1)} %pad_maximum_fusion.5), channel_id=1, source_target_pairs={{16,0},{32,16},{48,32},{17,1},{33,17},{49,33},{18,2},{34,18},{50,3... | collective-permute-start | bytes 98312 | tf_op jit(solution)/shard_map/ppermute | solution.py:190
  85.6 0.2 copy.9.w_ref
  85.7 0.1 collective-permute-done.4.corner_below_ref
  85.8 4.2 %collective-permute-done.5.corner_above_ref = bf16[64,256]{1,0:T(8,128)(2,1)S(1)} collective-permute-done((bf16[64,256]{1,0:T(8,128)(2,1)S(1)}, bf16[64,256]{1,0:T(8,128)(2,1)S(1)}, u32[]{:S(2)}, u32[]{:S(2)}) %collective-permute-start.5) | collective-permute-done | bytes 32800 | tf_op jit(solution)/shard_map/ppermute | solution.py:190
  90.1 0.9 shard_map.52
  90.9 13.6 %all-to-all-done.1 = f32[32,4,128]{2,1,0:T(4,128)S(1)} async-done(((f32[32,4,128]{2,1,0:T(4,128)}), f32[32,4,128]{2,1,0:T(4,128)S(1)}, u32[]{:S(2)}, u32[]{:S(2)}) %all-to-all-start.1) | async-done | bytes 65568 | tf_op jit(solution)/shard_map/all_to_all | solution.py:220
  104.6 0.6 broadcast_in_dim.12
  105.2 3.5 %all-to-all-start.2 = ((f32[16,4,128]{2,1,0:T(4,128)}), f32[16,4,128]{2,1,0:T(4,128)S(1)}, u32[]{:S(2)}, u32[]{:S(2)}) async-start(f32[16,4,128]{2,1,0:T(4,128)} %broadcast_in_dim.12), calls=%async_computation.2 | async-start | bytes 65536 | tf_op jit(solution)/shard_map/all_to_all | solution.py:229
  108.7 0.9 reshape.34
  109.6 6.7 %all-to-all-done.2 = f32[16,4,128]{2,1,0:T(4,128)S(1)} async-done(((f32[16,4,128]{2,1,0:T(4,128)}), f32[16,4,128]{2,1,0:T(4,128)S(1)}, u32[]{:S(2)}, u32[]{:S(2)}) %all-to-all-start.2) | async-done | bytes 32800 | tf_op jit(solution)/shard_map/all_to_all | solution.py:229
  116.3 0.6 slice_multiply_fusion
  (15 shorter events, 0.3 us)
Async XLA Ops:
  1.8 17.2 %copy-start = (bf16[1,64,4,4,128]{4,3,2,1,0:T(4,128)(2,1)S(1)}, bf16[1,64,4,4,128]{4,3,2,1,0:T(4,128)(2,1)}, u32[]{:S(2)}) copy-start(bf16[1,64,4,4,128]{4,3,2,1,0:T(4,128)(2,1)} %param.3) | copy-start | bytes 786436
  1.8 23.6 %collective-permute-start.2 = (bf16[64,512]{1,0:T(8,128)(2,1)S(1)}, bf16[64,512]{1,0:T(8,128)(2,1)S(1)}, u32[]{:S(2)}, u32[]{:S(2)}) collective-permute-start(bf16[64,512]{1,0:T(8,128)(2,1)S(1)} %pad_maximum_fusion.2), channel_id=1, source_target_pairs={{0,1},{1,2},{2,3},{3,4},{4,5},{5,6},{6,7},{7,8},{8,9},{9,10},{10,1... | collective-permute-start | bytes 196616 | tf_op jit(solution)/shard_map/ppermute | solution.py:190
  17.7 25.7 %collective-permute-start.3 = (bf16[64,512]{1,0:T(8,128)(2,1)S(1)}, bf16[64,512]{1,0:T(8,128)(2,1)S(1)}, u32[]{:S(2)}, u32[]{:S(2)}) collective-permute-start(bf16[64,512]{1,0:T(8,128)(2,1)S(1)} %pad_maximum_fusion.3), channel_id=1, source_target_pairs={{1,0},{2,1},{3,2},{4,3},{5,4},{6,5},{7,6},{8,7},{9,8},{10,9},{11,1... | collective-permute-start | bytes 196616 | tf_op jit(solution)/shard_map/ppermute | solution.py:190
  19.3 24.1 %collective-permute-start = (bf16[64,768]{1,0:T(8,128)(2,1)S(1)}, bf16[64,768]{1,0:T(8,128)(2,1)S(1)}, u32[]{:S(2)}, u32[]{:S(2)}) collective-permute-start(bf16[64,768]{1,0:T(8,128)(2,1)S(1)} %pad_maximum_fusion), channel_id=1, source_target_pairs={{0,16},{16,32},{32,48},{1,17},{17,33},{33,49},{2,18},{18,34},{34,5... | collective-permute-start | bytes 294920 | tf_op jit(solution)/shard_map/ppermute | solution.py:190
  22.7 2.3 %copy-start.1 = (bf16[64,1728]{1,0:T(8,128)(2,1)S(1)}, bf16[64,1728]{1,0:T(8,128)(2,1)}, u32[]{:S(2)}) copy-start(bf16[64,1728]{1,0:T(8,128)(2,1)} %param.5) | copy-start | bytes 663556
  22.7 20.7 %collective-permute-start.1 = (bf16[64,768]{1,0:T(8,128)(2,1)S(1)}, bf16[64,768]{1,0:T(8,128)(2,1)S(1)}, u32[]{:S(2)}, u32[]{:S(2)}) collective-permute-start(bf16[64,768]{1,0:T(8,128)(2,1)S(1)} %pad_maximum_fusion.1), channel_id=1, source_target_pairs={{16,0},{32,16},{48,32},{17,1},{33,17},{49,33},{18,2},{34,18},{50,3... | collective-permute-start | bytes 294920 | tf_op jit(solution)/shard_map/ppermute | solution.py:190
  64.0 40.5 %all-to-all-start.1 = ((f32[32,4,128]{2,1,0:T(4,128)}), f32[32,4,128]{2,1,0:T(4,128)S(1)}, u32[]{:S(2)}, u32[]{:S(2)}) async-start(f32[32,4,128]{2,1,0:T(4,128)} %bitcast.4), calls=%async_computation.1 | async-start | bytes 131072 | tf_op jit(solution)/shard_map/all_to_all | solution.py:220
  81.6 4.3 %collective-permute-start.4 = (bf16[64,256]{1,0:T(8,128)(2,1)S(1)}, bf16[64,256]{1,0:T(8,128)(2,1)S(1)}, u32[]{:S(2)}, u32[]{:S(2)}) collective-permute-start(bf16[64,256]{1,0:T(8,128)(2,1)S(1)} %pad_maximum_fusion.4), channel_id=1, source_target_pairs={{0,16},{16,32},{32,48},{1,17},{17,33},{33,49},{2,18},{18,34},{34,5... | collective-permute-start | bytes 98312 | tf_op jit(solution)/shard_map/ppermute | solution.py:190
  84.3 5.8 %collective-permute-start.5 = (bf16[64,256]{1,0:T(8,128)(2,1)S(1)}, bf16[64,256]{1,0:T(8,128)(2,1)S(1)}, u32[]{:S(2)}, u32[]{:S(2)}) collective-permute-start(bf16[64,256]{1,0:T(8,128)(2,1)S(1)} %pad_maximum_fusion.5), channel_id=1, source_target_pairs={{16,0},{32,16},{48,32},{17,1},{33,17},{49,33},{18,2},{34,18},{50,3... | collective-permute-start | bytes 98312 | tf_op jit(solution)/shard_map/ppermute | solution.py:190
  105.2 11.0 %all-to-all-start.2 = ((f32[16,4,128]{2,1,0:T(4,128)}), f32[16,4,128]{2,1,0:T(4,128)S(1)}, u32[]{:S(2)}, u32[]{:S(2)}) async-start(f32[16,4,128]{2,1,0:T(4,128)} %broadcast_in_dim.12), calls=%async_computation.2 | async-start | bytes 65536 | tf_op jit(solution)/shard_map/all_to_all | solution.py:229

commit v3 on v2

--- a/solution.py
+++ b/solution.py
@@ -215,21 +215,22 @@
     message = run_message(*inner, below, above, low, high)
 
     parts = lax.all_to_all(message, ("core", "px", "y"), 0, 0)
-    mine = jnp.sum(parts, axis=0).reshape(8, 1, 4, LANES)
+    mine = jnp.sum(parts, axis=0).reshape(8, 4, LANES)
     mine, low, high = lax.optimization_barrier((mine, low, high))
-    parts = lax.all_to_all(
-        jnp.broadcast_to(mine, (8, 4, 4, LANES)).reshape(32, 4, LANES), ("zlo", "zhi"), 0, 0
-    )
+    parts = lax.all_to_all(mine, "zlo", 0, 0)
     last = (NX - 1) * LANES
     corner_below = shifted_by(jnp.concatenate([low[:, last:], high[:, last:]], axis=1), "px", 1)
     corner_above = shifted_by(jnp.concatenate([plane(low, 0), plane(high, 0)], axis=1), "px", -1)
+    parts, corner_below, corner_above = lax.optimization_barrier((parts, corner_below, corner_above))
+    mine = jnp.sum(parts, axis=0)
+    parts = lax.all_to_all(jnp.broadcast_to(mine, (4, 4, LANES)), "zhi", 0, 0)
     grad_input = run_input(g, weights, below, above, low, high, corner_below, corner_above)
     parts, grad_input = lax.optimization_barrier((parts, grad_input))
-    mine = jnp.sum(parts, axis=0)
+    total = 16 * 16 * 64 * 128
+    mine = jnp.sum(parts, axis=0) * (1.0 / math.sqrt(total))
     parts = lax.all_to_all(jnp.broadcast_to(mine, (16, 4, LANES)), ("px", "y"), 0, 0)
     whole = parts.reshape(4, 16 * LANES)[:, : 9 * ROWS]
-    total = 16 * 16 * 64 * 128
-    return grad_input.reshape(1, CH, NX, NY, LANES), whole * (1.0 / math.sqrt(total))
+    return grad_input.reshape(1, CH, NX, NY, LANES), whole
 
 
 def solution(mesh):

time: 117 us -> 130 us (1.11)
  waiting for transfers between devices: 42.6 us -> 50.7 us
  starting transfers between devices: 46.9 us -> 50 us
    all_to_all x1 -> x2, waiting for transfers between devices: 13.6 us -> 21.6 us  [the longest x1 21.1 us: local(): parts = lax.all_to_all(jnp.broadcast_to(mine, (4, 4, LANES)), 'zhi', 0, 0)]
    all_to_all x1 -> x2, starting transfers between devices: 17.5 us -> 20.6 us  [the longest x1 15.5 us: local(): parts = lax.all_to_all(jnp.broadcast_to(mine, (4, 4, LANES)), 'zhi', 0, 0)]
  transfers between devices with their start and end apart: 8 -> 9, of which waited for: 5 -> 6; matrix products, arithmetic and copies ran while one was open for 1% -> 1% of each run, Pallas kernels for 1% -> 1%
where the time goes in v3:
time: 130 us; the launch traced here: 129 us
  waiting for transfers between devices  50.7 us (39%)
  starting transfers between devices  50 us (38%)
  blocking collectives  19.1 us (15%)
  local copies, waits for them, and re-layouts  5.29 us (4%)
  Pallas kernels  2.62 us (2%)
    ppermute x6, starting transfers between devices, shifted_by(): return lax.ppermute(x, axis, pairs)  25.9 us
    ppermute x6, waiting for transfers between devices, shifted_by(): return lax.ppermute(x, axis, pairs)  22.4 us
    all_to_all x1, waiting for transfers between devices, local(): parts = lax.all_to_all(jnp.broadcast_to(mine, (4, 4, LANES)), 'zhi', 0, 0)  21.1 us
    all_to_all x1, blocking collectives, local(): parts = lax.all_to_all(message, ('core', 'px', 'y'), 0, 0)  19.1 us
    all_to_all x1, starting transfers between devices, local(): parts = lax.all_to_all(jnp.broadcast_to(mine, (4, 4, LANES)), 'zhi', 0, 0)  15.5 us
    all_to_all x1, waiting for transfers between devices, local(): lax.all_to_all(jnp.broadcast_to(mine, (16, 4, LANES)), ('px', 'y'), 0, 0)  6.69 us
    all_to_all x1, starting transfers between devices, local(): parts = lax.all_to_all(mine, 'zlo', 0, 0)  5.05 us
    all_to_all x1, starting transfers between devices, local(): lax.all_to_all(jnp.broadcast_to(mine, (16, 4, LANES)), ('px', 'y'), 0, 0)  3.48 us
  transfers between devices with their start and end apart: 9, of which 6 were waited for; matrix products, arithmetic and copies ran while one was open for 1% of the time, Pallas kernels for 1%

profile of v3, /device:TPU:32, one launch (start us, length us, event | category | flops | bytes accessed | tf_op | source)
XLA Modules:
  0.0 128.7 jit_solution(2424811964017596046)
XLA Ops:
  0.6 1.1 reshape.27.g_ref
  1.8 0.0 copy-start
  1.8 15.9 %collective-permute-start.2 = (bf16[64,512]{1,0:T(8,128)(2,1)S(1)}, bf16[64,512]{1,0:T(8,128)(2,1)S(1)}, u32[]{:S(2)}, u32[]{:S(2)}) collective-permute-start(bf16[64,512]{1,0:T(8,128)(2,1)S(1)} %pad_maximum_fusion.2), channel_id=1, source_target_pairs={{0,1},{1,2},{2,3},{3,4},{4,5},{5,6},{6,7},{7,8},{8,9},{9,10},{10,1... | collective-permute-start | bytes 196616 | tf_op jit(solution)/shard_map/ppermute | solution.py:190
  17.7 1.3 %collective-permute-start.3 = (bf16[64,512]{1,0:T(8,128)(2,1)S(1)}, bf16[64,512]{1,0:T(8,128)(2,1)S(1)}, u32[]{:S(2)}, u32[]{:S(2)}) collective-permute-start(bf16[64,512]{1,0:T(8,128)(2,1)S(1)} %pad_maximum_fusion.3), channel_id=1, source_target_pairs={{1,0},{2,1},{3,2},{4,3},{5,4},{6,5},{7,6},{8,7},{9,8},{10,9},{11,1... | collective-permute-start | bytes 196616 | tf_op jit(solution)/shard_map/ppermute | solution.py:190
  19.0 0.0 copy-done
  19.0 0.2 reshape.28.a_ref
  19.3 3.4 %collective-permute-start = (bf16[64,768]{1,0:T(8,128)(2,1)S(1)}, bf16[64,768]{1,0:T(8,128)(2,1)S(1)}, u32[]{:S(2)}, u32[]{:S(2)}) collective-permute-start(bf16[64,768]{1,0:T(8,128)(2,1)S(1)} %pad_maximum_fusion), channel_id=1, source_target_pairs={{0,16},{16,32},{32,48},{1,17},{17,33},{33,49},{2,18},{18,34},{34,5... | collective-permute-start | bytes 294920 | tf_op jit(solution)/shard_map/ppermute | solution.py:190
  22.7 0.0 copy-start.1
  22.7 1.4 %collective-permute-start.1 = (bf16[64,768]{1,0:T(8,128)(2,1)S(1)}, bf16[64,768]{1,0:T(8,128)(2,1)S(1)}, u32[]{:S(2)}, u32[]{:S(2)}) collective-permute-start(bf16[64,768]{1,0:T(8,128)(2,1)S(1)} %pad_maximum_fusion.1), channel_id=1, source_target_pairs={{16,0},{32,16},{48,32},{17,1},{33,17},{49,33},{18,2},{34,18},{50,3... | collective-permute-start | bytes 294920 | tf_op jit(solution)/shard_map/ppermute | solution.py:190
  24.1 0.9 shard_map.50
  25.0 0.0 copy-done.1
  25.0 0.3 reshape.25
  25.4 0.0 collective-permute-done.2.low_ref
  25.4 17.9 %collective-permute-done.3.high_ref = bf16[64,512]{1,0:T(8,128)(2,1)S(1)} collective-permute-done((bf16[64,512]{1,0:T(8,128)(2,1)S(1)}, bf16[64,512]{1,0:T(8,128)(2,1)S(1)}, u32[]{:S(2)}, u32[]{:S(2)}) %collective-permute-start.3) | collective-permute-done | bytes 65568 | tf_op jit(solution)/shard_map/ppermute | solution.py:190
  43.4 0.0 collective-permute-done.below_ref
  43.4 0.0 collective-permute-done.1.above_ref
  43.4 0.9 shard_map.51
  44.2 19.1 %all_to_all.20 = f32[32,8,512]{2,1,0:T(8,128)S(1)} all-to-all(f32[32,8,512]{2,1,0:T(8,128)S(1)} %shard_map.51), channel_id=1, replica_groups=mesh['zlo'=8,'core'=2,'px'=4,'y'=4,'zhi'=4] {'core','px','y'}, dimensions={0} | all-to-all | bytes 1048576 | tf_op jit(solution)/shard_map/all_to_all | solution.py:217
  63.4 0.6 reshape.29
  64.0 5.1 %all-to-all-start.1 = ((f32[8,4,128]{2,1,0:T(4,128)}), f32[8,4,128]{2,1,0:T(4,128)S(1)}, u32[]{:S(2)}, u32[]{:S(2)}) async-start(f32[8,4,128]{2,1,0:T(4,128)} %reshape.29), calls=%async_computation.1 | async-start | bytes 32768 | tf_op jit(solution)/shard_map/all_to_all | solution.py:220
  69.1 2.7 %collective-permute-start.4 = (bf16[64,256]{1,0:T(8,128)(2,1)S(1)}, bf16[64,256]{1,0:T(8,128)(2,1)S(1)}, u32[]{:S(2)}, u32[]{:S(2)}) collective-permute-start(bf16[64,256]{1,0:T(8,128)(2,1)S(1)} %pad_maximum_fusion.4), channel_id=1, source_target_pairs={{0,16},{16,32},{32,48},{1,17},{17,33},{33,49},{2,18},{18,34},{34,5... | collective-permute-start | bytes 98312 | tf_op jit(solution)/shard_map/ppermute | solution.py:190
  71.8 1.3 %collective-permute-start.5 = (bf16[64,256]{1,0:T(8,128)(2,1)S(1)}, bf16[64,256]{1,0:T(8,128)(2,1)S(1)}, u32[]{:S(2)}, u32[]{:S(2)}) collective-permute-start(bf16[64,256]{1,0:T(8,128)(2,1)S(1)} %pad_maximum_fusion.5), channel_id=1, source_target_pairs={{16,0},{32,16},{48,32},{17,1},{33,17},{49,33},{18,2},{34,18},{50,3... | collective-permute-start | bytes 98312 | tf_op jit(solution)/shard_map/ppermute | solution.py:190
  73.1 0.3 collective-permute-done.4.corner_below_ref
  73.3 4.2 %collective-permute-done.5.corner_above_ref = bf16[64,256]{1,0:T(8,128)(2,1)S(1)} collective-permute-done((bf16[64,256]{1,0:T(8,128)(2,1)S(1)}, bf16[64,256]{1,0:T(8,128)(2,1)S(1)}, u32[]{:S(2)}, u32[]{:S(2)}) %collective-permute-start.5) | collective-permute-done | bytes 32800 | tf_op jit(solution)/shard_map/ppermute | solution.py:190
  77.6 0.5 all-to-all-done.1
  78.1 0.6 broadcast_in_dim.6
  78.7 15.5 %all-to-all-start.2 = ((f32[4,4,128]{2,1,0:T(4,128)}), f32[4,4,128]{2,1,0:T(4,128)S(1)}, u32[]{:S(2)}, u32[]{:S(2)}) async-start(f32[4,4,128]{2,1,0:T(4,128)} %broadcast_in_dim.6), calls=%async_computation.2 | async-start | bytes 16384 | tf_op jit(solution)/shard_map/all_to_all | solution.py:226
  94.2 0.2 copy.9.w_ref
  94.4 0.9 shard_map.52
  95.3 21.1 %all-to-all-done.2 = f32[4,4,128]{2,1,0:T(4,128)S(1)} async-done(((f32[4,4,128]{2,1,0:T(4,128)}), f32[4,4,128]{2,1,0:T(4,128)S(1)}, u32[]{:S(2)}, u32[]{:S(2)}) %all-to-all-start.2) | async-done | bytes 8224 | tf_op jit(solution)/shard_map/all_to_all | solution.py:226
  116.4 0.6 broadcast_in_dim.7
  117.0 3.5 %all-to-all-start.3 = ((f32[16,4,128]{2,1,0:T(4,128)}), f32[16,4,128]{2,1,0:T(4,128)S(1)}, u32[]{:S(2)}, u32[]{:S(2)}) async-start(f32[16,4,128]{2,1,0:T(4,128)} %broadcast_in_dim.7), calls=%async_computation.3 | async-start | bytes 65536 | tf_op jit(solution)/shard_map/all_to_all | solution.py:231
  120.5 0.9 reshape.30
  121.4 6.7 %all-to-all-done.3 = f32[16,4,128]{2,1,0:T(4,128)S(1)} async-done(((f32[16,4,128]{2,1,0:T(4,128)}), f32[16,4,128]{2,1,0:T(4,128)S(1)}, u32[]{:S(2)}, u32[]{:S(2)}) %all-to-all-start.3) | async-done | bytes 32800 | tf_op jit(solution)/shard_map/all_to_all | solution.py:231
  128.1 0.6 slice.90
  (16 shorter events, 0.3 us)
Async XLA Ops:
  1.8 17.2 %copy-start = (bf16[1,64,4,4,128]{4,3,2,1,0:T(4,128)(2,1)S(1)}, bf16[1,64,4,4,128]{4,3,2,1,0:T(4,128)(2,1)}, u32[]{:S(2)}) copy-start(bf16[1,64,4,4,128]{4,3,2,1,0:T(4,128)(2,1)} %param.3) | copy-start | bytes 786436
  1.8 23.6 %collective-permute-start.2 = (bf16[64,512]{1,0:T(8,128)(2,1)S(1)}, bf16[64,512]{1,0:T(8,128)(2,1)S(1)}, u32[]{:S(2)}, u32[]{:S(2)}) collective-permute-start(bf16[64,512]{1,0:T(8,128)(2,1)S(1)} %pad_maximum_fusion.2), channel_id=1, source_target_pairs={{0,1},{1,2},{2,3},{3,4},{4,5},{5,6},{6,7},{7,8},{8,9},{9,10},{10,1... | collective-permute-start | bytes 196616 | tf_op jit(solution)/shard_map/ppermute | solution.py:190
  17.7 25.7 %collective-permute-start.3 = (bf16[64,512]{1,0:T(8,128)(2,1)S(1)}, bf16[64,512]{1,0:T(8,128)(2,1)S(1)}, u32[]{:S(2)}, u32[]{:S(2)}) collective-permute-start(bf16[64,512]{1,0:T(8,128)(2,1)S(1)} %pad_maximum_fusion.3), channel_id=1, source_target_pairs={{1,0},{2,1},{3,2},{4,3},{5,4},{6,5},{7,6},{8,7},{9,8},{10,9},{11,1... | collective-permute-start | bytes 196616 | tf_op jit(solution)/shard_map/ppermute | solution.py:190
  19.3 24.1 %collective-permute-start = (bf16[64,768]{1,0:T(8,128)(2,1)S(1)}, bf16[64,768]{1,0:T(8,128)(2,1)S(1)}, u32[]{:S(2)}, u32[]{:S(2)}) collective-permute-start(bf16[64,768]{1,0:T(8,128)(2,1)S(1)} %pad_maximum_fusion), channel_id=1, source_target_pairs={{0,16},{16,32},{32,48},{1,17},{17,33},{33,49},{2,18},{18,34},{34,5... | collective-permute-start | bytes 294920 | tf_op jit(solution)/shard_map/ppermute | solution.py:190
  22.7 2.3 %copy-start.1 = (bf16[64,1728]{1,0:T(8,128)(2,1)S(1)}, bf16[64,1728]{1,0:T(8,128)(2,1)}, u32[]{:S(2)}) copy-start(bf16[64,1728]{1,0:T(8,128)(2,1)} %param.5) | copy-start | bytes 663556
  22.7 20.7 %collective-permute-start.1 = (bf16[64,768]{1,0:T(8,128)(2,1)S(1)}, bf16[64,768]{1,0:T(8,128)(2,1)S(1)}, u32[]{:S(2)}, u32[]{:S(2)}) collective-permute-start(bf16[64,768]{1,0:T(8,128)(2,1)S(1)} %pad_maximum_fusion.1), channel_id=1, source_target_pairs={{16,0},{32,16},{48,32},{17,1},{33,17},{49,33},{18,2},{34,18},{50,3... | collective-permute-start | bytes 294920 | tf_op jit(solution)/shard_map/ppermute | solution.py:190
  64.0 14.1 %all-to-all-start.1 = ((f32[8,4,128]{2,1,0:T(4,128)}), f32[8,4,128]{2,1,0:T(4,128)S(1)}, u32[]{:S(2)}, u32[]{:S(2)}) async-start(f32[8,4,128]{2,1,0:T(4,128)} %reshape.29), calls=%async_computation.1 | async-start | bytes 32768 | tf_op jit(solution)/shard_map/all_to_all | solution.py:220
  69.1 4.3 %collective-permute-start.4 = (bf16[64,256]{1,0:T(8,128)(2,1)S(1)}, bf16[64,256]{1,0:T(8,128)(2,1)S(1)}, u32[]{:S(2)}, u32[]{:S(2)}) collective-permute-start(bf16[64,256]{1,0:T(8,128)(2,1)S(1)} %pad_maximum_fusion.4), channel_id=1, source_target_pairs={{0,16},{16,32},{32,48},{1,17},{17,33},{33,49},{2,18},{18,34},{34,5... | collective-permute-start | bytes 98312 | tf_op jit(solution)/shard_map/ppermute | solution.py:190
  71.8 5.8 %collective-permute-start.5 = (bf16[64,256]{1,0:T(8,128)(2,1)S(1)}, bf16[64,256]{1,0:T(8,128)(2,1)S(1)}, u32[]{:S(2)}, u32[]{:S(2)}) collective-permute-start(bf16[64,256]{1,0:T(8,128)(2,1)S(1)} %pad_maximum_fusion.5), channel_id=1, source_target_pairs={{16,0},{32,16},{48,32},{17,1},{33,17},{49,33},{18,2},{34,18},{50,3... | collective-permute-start | bytes 98312 | tf_op jit(solution)/shard_map/ppermute | solution.py:190
  78.7 37.7 %all-to-all-start.2 = ((f32[4,4,128]{2,1,0:T(4,128)}), f32[4,4,128]{2,1,0:T(4,128)S(1)}, u32[]{:S(2)}, u32[]{:S(2)}) async-start(f32[4,4,128]{2,1,0:T(4,128)} %broadcast_in_dim.6), calls=%async_computation.2 | async-start | bytes 16384 | tf_op jit(solution)/shard_map/all_to_all | solution.py:226
  117.0 11.0 %all-to-all-start.3 = ((f32[16,4,128]{2,1,0:T(4,128)}), f32[16,4,128]{2,1,0:T(4,128)S(1)}, u32[]{:S(2)}, u32[]{:S(2)}) async-start(f32[16,4,128]{2,1,0:T(4,128)} %broadcast_in_dim.7), calls=%async_computation.3 | async-start | bytes 65536 | tf_op jit(solution)/shard_map/all_to_all | solution.py:231

commit v4 on v2

--- a/solution.py
+++ b/solution.py
@@ -78,13 +78,28 @@
 
 
 def message_kernel(
-    gk_ref, row_ref, column_ref, below_ref, above_ref, low_ref, high_ref, msg_ref, wide_ref, rim_ref
+    core_ref, g_ref, gk_ref, row_ref, column_ref, below_ref, above_ref, far_ref, msg_ref, wide_ref, rim_ref, far3_ref
 ):
-    for side in range(2):
-        at = side * WIDE
-        rim_ref[:, at : at + LANES] = all_shifts(plane(below_ref, NY + side))
-        rim_ref[:, at + LANES : at + LANES + HALF] = row_ref[:, side * HALF : (side + 1) * HALF]
-        rim_ref[:, at + LANES + HALF : at + WIDE] = all_shifts(plane(above_ref, NY + side))
+    upward = core_ref[0] == 0
+
+    def near(low, high):
+        return jnp.where(upward, low, high)
+
+    rim_ref[:, 0:LANES] = all_shifts(near(plane(below_ref, NY), plane(below_ref, NY + 1)))
+    rim_ref[:, LANES : LANES + HALF] = near(row_ref[:, 0:HALF], row_ref[:, HALF : 2 * HALF])
+    rim_ref[:, LANES + HALF : WIDE] = all_shifts(near(plane(above_ref, NY), plane(above_ref, NY + 1)))
+    for x in range(NX):
+        far3_ref[:, x * LANES : (x + 1) * LANES] = all_shifts(plane(far_ref, NX + x))
+    own = [near(plane(below_ref, 0), plane(below_ref, NY - 1))]
+    own += [near(plane(g_ref, x * NY), plane(g_ref, x * NY + NY - 1)) for x in range(NX)]
+    own += [near(plane(above_ref, 0), plane(above_ref, NY - 1))]
+
+    def across(a):
+        of_far = dot_nt(far_ref[:, 0:HALF], rim_ref[:, a * LANES : a * LANES + HALF])
+        of_own = dot_nt(jnp.concatenate(own[2 - a : 2 - a + NX], axis=1), far3_ref[...])
+        return jnp.where(upward, of_own, of_far), jnp.where(upward, of_far, of_own)
+
+    pairs = [across(a) for a in range(3)]
 
     def block(a, b):
         value = gk_ref[b * ROWS + a * CH : b * ROWS + (a + 1) * CH, :]
@@ -96,9 +111,7 @@
             size = len(rows) * LANES
             value = value + dot_nt(face[:, of_g : of_g + size], column_ref[:, of_a : of_a + size])
         if b != 1:
-            face, side = (high_ref, 1) if b == 0 else (low_ref, 0)
-            at = side * WIDE + a * LANES
-            value = value + dot_nt(face[...], rim_ref[:, at : at + HALF])
+            value = value + pairs[a][b // 2]
         return value
 
     pad = jnp.zeros((CH, 2 * LANES - ROWS), F32)
@@ -152,13 +165,14 @@
             ).astype(BF16)
 
 
-def call(body, out_shape, scratch=(), cost=None):
+def call(body, out_shape, scratch=(), cost=None, **specs):
     return pl.pallas_call(
         body,
         out_shape=out_shape,
         scratch_shapes=scratch,
         cost_estimate=cost,
         compiler_params=pltpu.CompilerParams(vmem_limit_bytes=48 * 1024 * 1024),
+        **specs,
     )
 
 
@@ -172,12 +186,19 @@
     )(*operands)
 
 
-def run_message(*operands):
+def run_message(core, *operands):
+    vmem = pl.BlockSpec(memory_space=pltpu.VMEM)
     return call(
         message_kernel,
         jax.ShapeDtypeStruct((32, 8, HALF), F32),
-        [pltpu.VMEM((16, CH, LANES), F32), pltpu.VMEM((ROWS, 2 * WIDE), BF16)],
-    )(*operands)
+        [
+            pltpu.VMEM((16, CH, LANES), F32),
+            pltpu.VMEM((ROWS, WIDE), BF16),
+            pltpu.VMEM((ROWS, HALF), BF16),
+        ],
+        in_specs=[pl.BlockSpec(memory_space=pltpu.SMEM)] + [vmem] * len(operands),
+        out_specs=vmem,
+    )(core.reshape(1), *operands)
 
 
 def run_input(*operands):
@@ -190,33 +211,46 @@
     return lax.ppermute(x, axis, pairs)
 
 
+def along_y(x, by):
+    count = lax.axis_size("y") * lax.axis_size("zhi")
+    pairs = []
+    for core, step in enumerate((by, -by)):
+        pairs += [(core * count + i, core * count + i + step) for i in range(count) if 0 <= i + step < count]
+    return lax.ppermute(x, ("core", "y", "zhi"), pairs)
+
+
 def local(activations, grad_out, kernel):
-    py = ("y", "zhi")
+    core = lax.axis_index("core")
     g = grad_out.reshape(CH, CELLS)
-
-    def planes(cells):
-        return jnp.concatenate([plane(g, x * NY + y) for x, y in cells], axis=1)
-
-    low = shifted_by(planes([(x, NY - 1) for x in range(NX)]), py, 1)
-    high = shifted_by(planes([(x, 0) for x in range(NX)]), py, -1)
-
     a = activations.reshape(CH, CELLS)
 
+    def rows(cells, y):
+        return jnp.concatenate([plane(cells, x * NY + y) for x in range(NX)], axis=1)
+
+    g_low, g_high = rows(g, 0), rows(g, NY - 1)
+    ahead = jnp.where(core == 0, g_high, g_low)
+    ahead = jnp.concatenate([ahead, jnp.where(core == 0, rows(a, NY - 1), rows(a, 0))], axis=1)
+    far = along_y(ahead, 1)
+    back = along_y(jnp.where(core == 0, g_low, g_high), -1)
+
+
     weights = kernel.reshape(CH, 3, 3, ROWS).transpose(3, 2, 1, 0).reshape(ROWS, 3 * ROWS)
 
     def x_face(x):
-        rows = g[:, x * NY * LANES : (x + 1) * NY * LANES]
-        return jnp.concatenate([rows, plane(a, x * NY), plane(a, x * NY + NY - 1)], axis=1)
+        cells = g[:, x * NY * LANES : (x + 1) * NY * LANES]
+        return jnp.concatenate([cells, plane(a, x * NY), plane(a, x * NY + NY - 1), cells[:, LANES:]], axis=1)
 
     below = shifted_by(x_face(NX - 1), "px", 1)
     above = shifted_by(x_face(0), "px", -1)
     inner = run_inner(g, a)
     weights, *inner = lax.optimization_barrier((weights, *inner))
-    message = run_message(*inner, below, above, low, high)
+    message = run_message(core, g, *inner, below, above, far)
 
     parts = lax.all_to_all(message, ("core", "px", "y"), 0, 0)
     mine = jnp.sum(parts, axis=0).reshape(8, 1, 4, LANES)
-    mine, low, high = lax.optimization_barrier((mine, low, high))
+    mine, far = lax.optimization_barrier((mine, far))
+    low = jnp.where(core == 0, far[:, :HALF], back)
+    high = jnp.where(core == 0, back, far[:, :HALF])
     parts = lax.all_to_all(
         jnp.broadcast_to(mine, (8, 4, 4, LANES)).reshape(32, 4, LANES), ("zlo", "zhi"), 0, 0
     )

time: 117 us -> 114 us (0.974)
  blocking collectives: 19.1 us -> 0 us
  starting transfers between devices: 46.9 us -> 63.5 us
  waiting for transfers between devices: 42.6 us -> 39.7 us
    all_to_all x1 -> x0, blocking collectives: 19.1 us -> none  [local(): parts = lax.all_to_all(message, ('core', 'px', 'y'), 0, 0)]
    ppermute x6 -> x4, starting transfers between devices: 25.9 us -> 8.79 us  [shifted_by(): return lax.ppermute(x, axis, pairs)]
    ppermute x0 -> x2, starting transfers between devices: none -> 17 us  [along_y(): return lax.ppermute(x, ('core', 'y', 'zhi'), pairs)]
    ppermute x6 -> x4, waiting for transfers between devices: 22.3 us -> 7.29 us  [shifted_by(): return lax.ppermute(x, axis, pairs)]
    all_to_all x0 -> x1, starting transfers between devices: none -> 12.8 us  [local(): parts = lax.all_to_all(message, ('core', 'px', 'y'), 0, 0)]
    all_to_all x0 -> x1, waiting for transfers between devices: none -> 10.7 us  [local(): parts = lax.all_to_all(message, ('core', 'px', 'y'), 0, 0)]
    all_to_all x1, starting transfers between devices: 17.5 us -> 21.3 us  [local(): lax.all_to_all(jnp.broadcast_to(mine, (8, 4, 4, LANES)).reshape(32, 4, LA...]
    ppermute x0 -> x2, waiting for transfers between devices: none -> 1.49 us  [along_y(): return lax.ppermute(x, ('core', 'y', 'zhi'), pairs)]
  transfers between devices with their start and end apart: 8 -> 9, of which waited for: 5 -> 7; matrix products, arithmetic and copies ran while one was open for 1% -> 2% of each run, Pallas kernels for 1% -> 2%
where the time goes in v4:
time: 114 us; the launch traced here: 113 us
  starting transfers between devices  63.5 us (56%)
  waiting for transfers between devices  39.7 us (35%)
  local copies, waits for them, and re-layouts  4.16 us (4%)
  Pallas kernels  3.59 us (3%)
  other arithmetic  1.46 us (1%)
    all_to_all x1, starting transfers between devices, local(): lax.all_to_all(jnp.broadcast_to(mine, (8, 4, 4, LANES)).reshape(32, 4, LA...  21.3 us
    ppermute x2, starting transfers between devices, along_y(): return lax.ppermute(x, ('core', 'y', 'zhi'), pairs)  17 us
    all_to_all x1, waiting for transfers between devices, local(): lax.all_to_all(jnp.broadcast_to(mine, (8, 4, 4, LANES)).reshape(32, 4, LA...  13.6 us
    all_to_all x1, starting transfers between devices, local(): parts = lax.all_to_all(message, ('core', 'px', 'y'), 0, 0)  12.8 us
    all_to_all x1, waiting for transfers between devices, local(): parts = lax.all_to_all(message, ('core', 'px', 'y'), 0, 0)  10.7 us
    ppermute x4, starting transfers between devices, shifted_by(): return lax.ppermute(x, axis, pairs)  8.79 us
    ppermute x4, waiting for transfers between devices, shifted_by(): return lax.ppermute(x, axis, pairs)  7.29 us
    all_to_all x1, waiting for transfers between devices, local(): lax.all_to_all(jnp.broadcast_to(mine, (16, 4, LANES)), ('px', 'y'), 0, 0)  6.69 us
  transfers between devices with their start and end apart: 9, of which 7 were waited for; matrix products, arithmetic and copies ran while one was open for 2% of the time, Pallas kernels for 2%

profile of v4, /device:TPU:32, one launch (start us, length us, event | category | flops | bytes accessed | tf_op | source)
XLA Modules:
  0.0 113.3 jit_solution(5858949322998969814)
XLA Ops:
  0.6 0.0 copy-start
  0.6 1.2 %reshape.32.g_ref = bf16[64,2048]{1,0:T(8,128)(2,1)S(1)} reshape(bf16[1,64,4,4,128]{4,3,2,1,0:T(4,128)(2,1)} %param.4) | data formatting | bytes 524288 | tf_op jit(solution)/shard_map/reshape | solution.py:224
  1.9 0.0 copy-done
  1.9 0.2 reshape.35.a_ref
  2.1 0.7 broadcast_select_fusion.2
  2.8 15.7 %collective-permute-start.2 = (bf16[64,1024]{1,0:T(8,128)(2,1)S(1)}, bf16[64,1024]{1,0:T(8,128)(2,1)S(1)}, u32[]{:S(2)}, u32[]{:S(2)}) collective-permute-start(bf16[64,1024]{1,0:T(8,128)(2,1)S(1)} %pad_maximum_fusion.2), channel_id=1, source_target_pairs={{0,1},{1,2},{2,3},{3,4},{4,5},{5,6},{6,7},{7,8},{8,9},{9,10},{10,1... | collective-permute-start | bytes 393224 | tf_op jit(solution)/shard_map/ppermute | solution.py:219
  18.6 3.4 %collective-permute-start = (bf16[64,1152]{1,0:T(8,128)(2,1)S(1)}, bf16[64,1152]{1,0:T(8,128)(2,1)S(1)}, u32[]{:S(2)}, u32[]{:S(2)}) collective-permute-start(bf16[64,1152]{1,0:T(8,128)(2,1)S(1)} %pad_maximum_fusion), channel_id=1, source_target_pairs={{0,16},{16,32},{32,48},{1,17},{17,33},{33,49},{2,18},{18,34},{34,5... | collective-permute-start | bytes 442376 | tf_op jit(solution)/shard_map/ppermute | solution.py:211
  22.0 0.0 copy-start.1
  22.0 1.4 %collective-permute-start.1 = (bf16[64,1152]{1,0:T(8,128)(2,1)S(1)}, bf16[64,1152]{1,0:T(8,128)(2,1)S(1)}, u32[]{:S(2)}, u32[]{:S(2)}) collective-permute-start(bf16[64,1152]{1,0:T(8,128)(2,1)S(1)} %pad_maximum_fusion.1), channel_id=1, source_target_pairs={{16,0},{32,16},{48,32},{17,1},{33,17},{49,33},{18,2},{34,18},{50,3... | collective-permute-start | bytes 442376 | tf_op jit(solution)/shard_map/ppermute | solution.py:211
  23.5 0.9 shard_map.50
  24.4 0.0 copy-done.1
  24.4 0.3 reshape.33
  24.8 1.5 %collective-permute-done.2.far_ref = bf16[64,1024]{1,0:T(8,128)(2,1)S(1)} collective-permute-done((bf16[64,1024]{1,0:T(8,128)(2,1)S(1)}, bf16[64,1024]{1,0:T(8,128)(2,1)S(1)}, u32[]{:S(2)}, u32[]{:S(2)}) %collective-permute-start.2) | collective-permute-done | bytes 131104 | tf_op jit(solution)/shard_map/ppermute | solution.py:219
  26.2 0.0 collective-permute-done.below_ref
  26.2 3.0 %collective-permute-done.1.above_ref = bf16[64,1152]{1,0:T(8,128)(2,1)S(1)} collective-permute-done((bf16[64,1152]{1,0:T(8,128)(2,1)S(1)}, bf16[64,1152]{1,0:T(8,128)(2,1)S(1)}, u32[]{:S(2)}, u32[]{:S(2)}) %collective-permute-start.1) | collective-permute-done | bytes 147488 | tf_op jit(solution)/shard_map/ppermute | solution.py:211
  29.2 1.8 %shard_map.51 = f32[32,8,512]{2,1,0:T(8,128)} custom-call(s32[1]{0:T(128)} %bitcast.core_ref, bf16[64,2048]{1,0:T(8,128)(2,1)S(1)} %reshape.32.g_ref, f32[576,192]{1,0:T(8,128)S(1)} %get-tuple-element.16.gk_ref, bf16[192,1024]{1,0:T(8,128)(2,1)S(1)} %get-tuple-element.17.row_ref, bf16[192,1024]{1,0:T(8,128)(2,1)S(1)} %get-tuple-element.18.column_ref, ...), custom_call_target="tpu_custom_call" | custom-call | tf_op jit(solution)/shard_map/pallas_call | solution.py:191
  31.0 0.0 copy-start.2
  31.0 12.8 %all-to-all-start = ((f32[32,8,512]{2,1,0:T(8,128)}), f32[32,8,512]{2,1,0:T(8,128)S(1)}, u32[]{:S(2)}, u32[]{:S(2)}) async-start(f32[32,8,512]{2,1,0:T(8,128)} %shard_map.51), calls=%async_computation | async-start | bytes 1048576 | tf_op jit(solution)/shard_map/all_to_all | solution.py:249
  43.9 0.0 copy-done.2
  43.9 1.3 %collective-permute-start.3 = (bf16[64,512]{1,0:T(8,128)(2,1)S(1)}, bf16[64,512]{1,0:T(8,128)(2,1)S(1)}, u32[]{:S(2)}, u32[]{:S(2)}) collective-permute-start(bf16[64,512]{1,0:T(8,128)(2,1)S(1)} %copy-done.2), channel_id=1, source_target_pairs={{1,0},{2,1},{3,2},{4,3},{5,4},{6,5},{7,6},{8,7},{9,8},{10,9},{11,1... | collective-permute-start | bytes 196616 | tf_op jit(solution)/shard_map/ppermute | solution.py:219
  45.2 10.7 %all-to-all-done = f32[32,8,512]{2,1,0:T(8,128)S(1)} async-done(((f32[32,8,512]{2,1,0:T(8,128)}), f32[32,8,512]{2,1,0:T(8,128)S(1)}, u32[]{:S(2)}, u32[]{:S(2)}) %all-to-all-start) | async-done | bytes 524320 | tf_op jit(solution)/shard_map/all_to_all | solution.py:249
  55.9 0.6 broadcast_in_dim.11
  56.6 21.3 %all-to-all-start.1 = ((f32[32,4,128]{2,1,0:T(4,128)}), f32[32,4,128]{2,1,0:T(4,128)S(1)}, u32[]{:S(2)}, u32[]{:S(2)}) async-start(f32[32,4,128]{2,1,0:T(4,128)} %bitcast.5), calls=%async_computation.1 | async-start | bytes 131072 | tf_op jit(solution)/shard_map/all_to_all | solution.py:254
  77.9 0.0 collective-permute-done.3
  78.0 2.7 %collective-permute-start.4 = (bf16[64,256]{1,0:T(8,128)(2,1)S(1)}, bf16[64,256]{1,0:T(8,128)(2,1)S(1)}, u32[]{:S(2)}, u32[]{:S(2)}) collective-permute-start(bf16[64,256]{1,0:T(8,128)(2,1)S(1)} %pad_maximum_fusion.5), channel_id=1, source_target_pairs={{0,16},{16,32},{32,48},{1,17},{17,33},{33,49},{2,18},{18,34},{34,5... | collective-permute-start | bytes 98312 | tf_op jit(solution)/shard_map/ppermute | solution.py:211
  80.7 1.3 %collective-permute-start.5 = (bf16[64,256]{1,0:T(8,128)(2,1)S(1)}, bf16[64,256]{1,0:T(8,128)(2,1)S(1)}, u32[]{:S(2)}, u32[]{:S(2)}) collective-permute-start(bf16[64,256]{1,0:T(8,128)(2,1)S(1)} %pad_maximum_fusion.6), channel_id=1, source_target_pairs={{16,0},{32,16},{48,32},{17,1},{33,17},{49,33},{18,2},{34,18},{50,3... | collective-permute-start | bytes 98312 | tf_op jit(solution)/shard_map/ppermute | solution.py:211
  82.0 0.2 copy.9.w_ref
  82.1 0.1 collective-permute-done.4.corner_below_ref
  82.2 4.2 %collective-permute-done.5.corner_above_ref = bf16[64,256]{1,0:T(8,128)(2,1)S(1)} collective-permute-done((bf16[64,256]{1,0:T(8,128)(2,1)S(1)}, bf16[64,256]{1,0:T(8,128)(2,1)S(1)}, u32[]{:S(2)}, u32[]{:S(2)}) %collective-permute-start.5) | collective-permute-done | bytes 32800 | tf_op jit(solution)/shard_map/ppermute | solution.py:211
  86.5 0.9 shard_map.52
  87.4 13.6 %all-to-all-done.1 = f32[32,4,128]{2,1,0:T(4,128)S(1)} async-done(((f32[32,4,128]{2,1,0:T(4,128)}), f32[32,4,128]{2,1,0:T(4,128)S(1)}, u32[]{:S(2)}, u32[]{:S(2)}) %all-to-all-start.1) | async-done | bytes 65568 | tf_op jit(solution)/shard_map/all_to_all | solution.py:254
  101.0 0.6 broadcast_in_dim.12
  101.6 3.5 %all-to-all-start.2 = ((f32[16,4,128]{2,1,0:T(4,128)}), f32[16,4,128]{2,1,0:T(4,128)S(1)}, u32[]{:S(2)}, u32[]{:S(2)}) async-start(f32[16,4,128]{2,1,0:T(4,128)} %broadcast_in_dim.12), calls=%async_computation.2 | async-start | bytes 65536 | tf_op jit(solution)/shard_map/all_to_all | solution.py:263
  105.1 0.9 reshape.38
  106.0 6.7 %all-to-all-done.2 = f32[16,4,128]{2,1,0:T(4,128)S(1)} async-done(((f32[16,4,128]{2,1,0:T(4,128)}), f32[16,4,128]{2,1,0:T(4,128)S(1)}, u32[]{:S(2)}, u32[]{:S(2)}) %all-to-all-start.2) | async-done | bytes 32800 | tf_op jit(solution)/shard_map/all_to_all | solution.py:263
  112.7 0.6 slice_multiply_fusion
  (17 shorter events, 0.3 us)
Async XLA Ops:
  0.6 1.2 %copy-start = (bf16[1,64,4,4,128]{4,3,2,1,0:T(4,128)(2,1)S(1)}, bf16[1,64,4,4,128]{4,3,2,1,0:T(4,128)(2,1)}, u32[]{:S(2)}) copy-start(bf16[1,64,4,4,128]{4,3,2,1,0:T(4,128)(2,1)} %param.3) | copy-start | bytes 786436
  2.8 23.4 %collective-permute-start.2 = (bf16[64,1024]{1,0:T(8,128)(2,1)S(1)}, bf16[64,1024]{1,0:T(8,128)(2,1)S(1)}, u32[]{:S(2)}, u32[]{:S(2)}) collective-permute-start(bf16[64,1024]{1,0:T(8,128)(2,1)S(1)} %pad_maximum_fusion.2), channel_id=1, source_target_pairs={{0,1},{1,2},{2,3},{3,4},{4,5},{5,6},{6,7},{7,8},{8,9},{9,10},{10,1... | collective-permute-start | bytes 393224 | tf_op jit(solution)/shard_map/ppermute | solution.py:219
  18.6 7.7 %collective-permute-start = (bf16[64,1152]{1,0:T(8,128)(2,1)S(1)}, bf16[64,1152]{1,0:T(8,128)(2,1)S(1)}, u32[]{:S(2)}, u32[]{:S(2)}) collective-permute-start(bf16[64,1152]{1,0:T(8,128)(2,1)S(1)} %pad_maximum_fusion), channel_id=1, source_target_pairs={{0,16},{16,32},{32,48},{1,17},{17,33},{33,49},{2,18},{18,34},{34,5... | collective-permute-start | bytes 442376 | tf_op jit(solution)/shard_map/ppermute | solution.py:211
  22.0 2.3 %copy-start.1 = (bf16[64,1728]{1,0:T(8,128)(2,1)S(1)}, bf16[64,1728]{1,0:T(8,128)(2,1)}, u32[]{:S(2)}) copy-start(bf16[64,1728]{1,0:T(8,128)(2,1)} %param.5) | copy-start | bytes 663556
  22.0 7.2 %collective-permute-start.1 = (bf16[64,1152]{1,0:T(8,128)(2,1)S(1)}, bf16[64,1152]{1,0:T(8,128)(2,1)S(1)}, u32[]{:S(2)}, u32[]{:S(2)}) collective-permute-start(bf16[64,1152]{1,0:T(8,128)(2,1)S(1)} %pad_maximum_fusion.1), channel_id=1, source_target_pairs={{16,0},{32,16},{48,32},{17,1},{33,17},{49,33},{18,2},{34,18},{50,3... | collective-permute-start | bytes 442376 | tf_op jit(solution)/shard_map/ppermute | solution.py:211
  31.0 12.9 %copy-start.2 = (bf16[64,512]{1,0:T(8,128)(2,1)S(1)}, bf16[64,512]{1,0:T(8,128)(2,1)}, u32[]{:S(2)}) copy-start(bf16[64,512]{1,0:T(8,128)(2,1)} %get-tuple-element.46) | copy-start | bytes 196612
  31.0 24.8 %all-to-all-start = ((f32[32,8,512]{2,1,0:T(8,128)}), f32[32,8,512]{2,1,0:T(8,128)S(1)}, u32[]{:S(2)}, u32[]{:S(2)}) async-start(f32[32,8,512]{2,1,0:T(8,128)} %shard_map.51), calls=%async_computation | async-start | bytes 1048576 | tf_op jit(solution)/shard_map/all_to_all | solution.py:249
  43.9 34.0 %collective-permute-start.3 = (bf16[64,512]{1,0:T(8,128)(2,1)S(1)}, bf16[64,512]{1,0:T(8,128)(2,1)S(1)}, u32[]{:S(2)}, u32[]{:S(2)}) collective-permute-start(bf16[64,512]{1,0:T(8,128)(2,1)S(1)} %copy-done.2), channel_id=1, source_target_pairs={{1,0},{2,1},{3,2},{4,3},{5,4},{6,5},{7,6},{8,7},{9,8},{10,9},{11,1... | collective-permute-start | bytes 196616 | tf_op jit(solution)/shard_map/ppermute | solution.py:219
  56.6 44.4 %all-to-all-start.1 = ((f32[32,4,128]{2,1,0:T(4,128)}), f32[32,4,128]{2,1,0:T(4,128)S(1)}, u32[]{:S(2)}, u32[]{:S(2)}) async-start(f32[32,4,128]{2,1,0:T(4,128)} %bitcast.5), calls=%async_computation.1 | async-start | bytes 131072 | tf_op jit(solution)/shard_map/all_to_all | solution.py:254
  78.0 4.3 %collective-permute-start.4 = (bf16[64,256]{1,0:T(8,128)(2,1)S(1)}, bf16[64,256]{1,0:T(8,128)(2,1)S(1)}, u32[]{:S(2)}, u32[]{:S(2)}) collective-permute-start(bf16[64,256]{1,0:T(8,128)(2,1)S(1)} %pad_maximum_fusion.5), channel_id=1, source_target_pairs={{0,16},{16,32},{32,48},{1,17},{17,33},{33,49},{2,18},{18,34},{34,5... | collective-permute-start | bytes 98312 | tf_op jit(solution)/shard_map/ppermute | solution.py:211
  80.7 5.8 %collective-permute-start.5 = (bf16[64,256]{1,0:T(8,128)(2,1)S(1)}, bf16[64,256]{1,0:T(8,128)(2,1)S(1)}, u32[]{:S(2)}, u32[]{:S(2)}) collective-permute-start(bf16[64,256]{1,0:T(8,128)(2,1)S(1)} %pad_maximum_fusion.6), channel_id=1, source_target_pairs={{16,0},{32,16},{48,32},{17,1},{33,17},{49,33},{18,2},{34,18},{50,3... | collective-permute-start | bytes 98312 | tf_op jit(solution)/shard_map/ppermute | solution.py:211
  101.6 11.1 %all-to-all-start.2 = ((f32[16,4,128]{2,1,0:T(4,128)}), f32[16,4,128]{2,1,0:T(4,128)S(1)}, u32[]{:S(2)}, u32[]{:S(2)}) async-start(f32[16,4,128]{2,1,0:T(4,128)} %broadcast_in_dim.12), calls=%async_computation.2 | async-start | bytes 65536 | tf_op jit(solution)/shard_map/all_to_all | solution.py:263

commit v5 on v4

--- a/solution.py
+++ b/solution.py
@@ -2,11 +2,13 @@
 
 import jax
 import jax.numpy as jnp
+import numpy as np
 from jax import lax
 from jax.experimental import pallas as pl
 from jax.experimental.pallas import tpu as pltpu
 from jax.sharding import Mesh, PartitionSpec as P
 
+AXES = ("zlo", "core", "px", "y", "zhi")
 LANES = 128
 CH = 64
 NX = 4
@@ -211,6 +213,13 @@
     return lax.ppermute(x, axis, pairs)
 
 
+def lines_along_z(first):
+    sizes = [lax.axis_size(axis) for axis in AXES]
+    place = np.arange(math.prod(sizes)).reshape(sizes)
+    lines = place.transpose(1, 2, 3, 4, 0).reshape(-1, sizes[4] * sizes[0])
+    return np.roll(lines, -first, axis=1).tolist()
+
+
 def along_y(x, by):
     count = lax.axis_size("y") * lax.axis_size("zhi")
     pairs = []
@@ -247,12 +256,13 @@
     message = run_message(core, g, *inner, below, above, far)
 
     parts = lax.all_to_all(message, ("core", "px", "y"), 0, 0)
-    mine = jnp.sum(parts, axis=0).reshape(8, 1, 4, LANES)
+    mine = jnp.sum(parts, axis=0)
     mine, far = lax.optimization_barrier((mine, far))
     low = jnp.where(core == 0, far[:, :HALF], back)
     high = jnp.where(core == 0, back, far[:, :HALF])
     parts = lax.all_to_all(
-        jnp.broadcast_to(mine, (8, 4, 4, LANES)).reshape(32, 4, LANES), ("zlo", "zhi"), 0, 0
+        jnp.broadcast_to(mine.reshape(1, 8, 4, LANES), (4, 8, 4, LANES)).reshape(32, 4, LANES),
+        AXES, 0, 0, axis_index_groups=lines_along_z(16),
     )
     last = (NX - 1) * LANES
     corner_below = shifted_by(jnp.concatenate([low[:, last:], high[:, last:]], axis=1), "px", 1)
@@ -267,8 +277,7 @@
 
 
 def solution(mesh):
-    axes = ("zlo", "core", "px", "y", "zhi")
-    fine = Mesh(mesh.devices.reshape(8, 2, 4, 4, 4), axes)
+    fine = Mesh(mesh.devices.reshape(8, 2, 4, 4, 4), AXES)
     dp, py = ("zlo", "core"), ("y", "zhi")
     cells = P(dp, None, "px", py, None)
     return jax.shard_map(

time: 114 us -> 108 us (0.947)
  the two profiles are of different devices: /device:TPU:32 before, /device:TPU:2 now
where the time goes in v5:
time: 108 us; the launch traced here: 107 us
  starting transfers between devices  76.7 us (71%)
  waiting for transfers between devices  20.6 us (19%)
  local copies, waits for them, and re-layouts  4.16 us (4%)
  Pallas kernels  3.59 us (3%)
  other arithmetic  1.46 us (1%)
    all_to_all x1, starting transfers between devices, local(): lax.all_to_all(jnp.broadcast_to(mine.reshape(1, 8, 4, LANES), (4, 8, 4, L...  25.2 us
    ppermute x2, starting transfers between devices, along_y(): return lax.ppermute(x, ('core', 'y', 'zhi'), pairs)  17 us
    all_to_all x1, starting transfers between devices, local(): parts = lax.all_to_all(message, ('core', 'px', 'y'), 0, 0)  15.4 us
    ppermute x4, starting transfers between devices, shifted_by(): return lax.ppermute(x, axis, pairs)  11.8 us
    all_to_all x1, waiting for transfers between devices, local(): parts = lax.all_to_all(message, ('core', 'px', 'y'), 0, 0)  9.64 us
    all_to_all x1, starting transfers between devices, local(): lax.all_to_all(jnp.broadcast_to(mine, (16, 4, LANES)), ('px', 'y'), 0, 0)  7.17 us
    ppermute x4, waiting for transfers between devices, shifted_by(): return lax.ppermute(x, axis, pairs)  5.63 us
    all_to_all x1, waiting for transfers between devices, local(): lax.all_to_all(jnp.broadcast_to(mine, (16, 4, LANES)), ('px', 'y'), 0, 0)  5.37 us
  transfers between devices with their start and end apart: 9, of which 4 were waited for; matrix products, arithmetic and copies ran while one was open for 2% of the time, Pallas kernels for 2%

profile of v5, /device:TPU:2, one launch (start us, length us, event | category | flops | bytes accessed | tf_op | source)
XLA Modules:
  0.0 107.4 jit_solution(12932295332491115961)
XLA Ops:
  0.6 0.0 copy-start
  0.6 1.2 %reshape.31.g_ref = bf16[64,2048]{1,0:T(8,128)(2,1)S(1)} reshape(bf16[1,64,4,4,128]{4,3,2,1,0:T(4,128)(2,1)} %param.4) | data formatting | bytes 524288 | tf_op jit(solution)/shard_map/reshape | solution.py:233
  1.9 0.0 copy-done
  1.9 0.2 reshape.34.a_ref
  2.1 0.7 broadcast_select_fusion.2
  2.8 15.7 %collective-permute-start.2 = (bf16[64,1024]{1,0:T(8,128)(2,1)S(1)}, bf16[64,1024]{1,0:T(8,128)(2,1)S(1)}, u32[]{:S(2)}, u32[]{:S(2)}) collective-permute-start(bf16[64,1024]{1,0:T(8,128)(2,1)S(1)} %pad_maximum_fusion.2), channel_id=1, source_target_pairs={{0,1},{1,2},{2,3},{3,4},{4,5},{5,6},{6,7},{7,8},{8,9},{9,10},{10,1... | collective-permute-start | bytes 393224 | tf_op jit(solution)/shard_map/ppermute | solution.py:228
  18.6 3.4 %collective-permute-start = (bf16[64,1152]{1,0:T(8,128)(2,1)S(1)}, bf16[64,1152]{1,0:T(8,128)(2,1)S(1)}, u32[]{:S(2)}, u32[]{:S(2)}) collective-permute-start(bf16[64,1152]{1,0:T(8,128)(2,1)S(1)} %pad_maximum_fusion), channel_id=1, source_target_pairs={{0,16},{16,32},{32,48},{1,17},{17,33},{33,49},{2,18},{18,34},{34,5... | collective-permute-start | bytes 442376 | tf_op jit(solution)/shard_map/ppermute | solution.py:213
  22.0 0.0 copy-start.1
  22.0 2.6 %collective-permute-start.1 = (bf16[64,1152]{1,0:T(8,128)(2,1)S(1)}, bf16[64,1152]{1,0:T(8,128)(2,1)S(1)}, u32[]{:S(2)}, u32[]{:S(2)}) collective-permute-start(bf16[64,1152]{1,0:T(8,128)(2,1)S(1)} %pad_maximum_fusion.1), channel_id=1, source_target_pairs={{16,0},{32,16},{48,32},{17,1},{33,17},{49,33},{18,2},{34,18},{50,3... | collective-permute-start | bytes 442376 | tf_op jit(solution)/shard_map/ppermute | solution.py:213
  24.6 0.9 shard_map.50
  25.5 0.0 copy-done.1
  25.5 0.3 reshape.32
  25.9 0.0 collective-permute-done.2.far_ref
  25.9 0.0 collective-permute-done.below_ref
  25.9 3.3 %collective-permute-done.1.above_ref = bf16[64,1152]{1,0:T(8,128)(2,1)S(1)} collective-permute-done((bf16[64,1152]{1,0:T(8,128)(2,1)S(1)}, bf16[64,1152]{1,0:T(8,128)(2,1)S(1)}, u32[]{:S(2)}, u32[]{:S(2)}) %collective-permute-start.1) | collective-permute-done | bytes 147488 | tf_op jit(solution)/shard_map/ppermute | solution.py:213
  29.2 1.8 %shard_map.51 = f32[32,8,512]{2,1,0:T(8,128)} custom-call(s32[1]{0:T(128)} %bitcast.core_ref, bf16[64,2048]{1,0:T(8,128)(2,1)S(1)} %reshape.31.g_ref, f32[576,192]{1,0:T(8,128)S(1)} %get-tuple-element.16.gk_ref, bf16[192,1024]{1,0:T(8,128)(2,1)S(1)} %get-tuple-element.17.row_ref, bf16[192,1024]{1,0:T(8,128)(2,1)S(1)} %get-tuple-element.18.column_ref, ...), custom_call_target="tpu_custom_call" | custom-call | tf_op jit(solution)/shard_map/pallas_call | solution.py:193
  31.0 0.0 copy-start.2
  31.0 15.4 %all-to-all-start = ((f32[32,8,512]{2,1,0:T(8,128)}), f32[32,8,512]{2,1,0:T(8,128)S(1)}, u32[]{:S(2)}, u32[]{:S(2)}) async-start(f32[32,8,512]{2,1,0:T(8,128)} %shard_map.51), calls=%async_computation | async-start | bytes 1048576 | tf_op jit(solution)/shard_map/all_to_all | solution.py:258
  46.5 0.0 copy-done.2
  46.5 1.3 %collective-permute-start.3 = (bf16[64,512]{1,0:T(8,128)(2,1)S(1)}, bf16[64,512]{1,0:T(8,128)(2,1)S(1)}, u32[]{:S(2)}, u32[]{:S(2)}) collective-permute-start(bf16[64,512]{1,0:T(8,128)(2,1)S(1)} %copy-done.2), channel_id=1, source_target_pairs={{1,0},{2,1},{3,2},{4,3},{5,4},{6,5},{7,6},{8,7},{9,8},{10,9},{11,1... | collective-permute-start | bytes 196616 | tf_op jit(solution)/shard_map/ppermute | solution.py:228
  47.8 9.6 %all-to-all-done = f32[32,8,512]{2,1,0:T(8,128)S(1)} async-done(((f32[32,8,512]{2,1,0:T(8,128)}), f32[32,8,512]{2,1,0:T(8,128)S(1)}, u32[]{:S(2)}, u32[]{:S(2)}) %all-to-all-start) | async-done | bytes 524320 | tf_op jit(solution)/shard_map/all_to_all | solution.py:258
  57.5 0.6 broadcast_in_dim.11
  58.1 25.2 %all-to-all-start.1 = ((f32[32,4,128]{2,1,0:T(4,128)}), f32[32,4,128]{2,1,0:T(4,128)S(1)}, u32[]{:S(2)}, u32[]{:S(2)}) async-start(f32[32,4,128]{2,1,0:T(4,128)} %bitcast.4), calls=%async_computation.1 | async-start | bytes 131072 | tf_op jit(solution)/shard_map/all_to_all | solution.py:263
  83.3 0.0 collective-permute-done.3
  83.4 2.6 %collective-permute-start.4 = (bf16[64,256]{1,0:T(8,128)(2,1)S(1)}, bf16[64,256]{1,0:T(8,128)(2,1)S(1)}, u32[]{:S(2)}, u32[]{:S(2)}) collective-permute-start(bf16[64,256]{1,0:T(8,128)(2,1)S(1)} %pad_maximum_fusion.5), channel_id=1, source_target_pairs={{0,16},{16,32},{32,48},{1,17},{17,33},{33,49},{2,18},{18,34},{34,5... | collective-permute-start | bytes 98312 | tf_op jit(solution)/shard_map/ppermute | solution.py:213
  86.0 3.3 %collective-permute-start.5 = (bf16[64,256]{1,0:T(8,128)(2,1)S(1)}, bf16[64,256]{1,0:T(8,128)(2,1)S(1)}, u32[]{:S(2)}, u32[]{:S(2)}) collective-permute-start(bf16[64,256]{1,0:T(8,128)(2,1)S(1)} %pad_maximum_fusion.6), channel_id=1, source_target_pairs={{16,0},{32,16},{48,32},{17,1},{33,17},{49,33},{18,2},{34,18},{50,3... | collective-permute-start | bytes 98312 | tf_op jit(solution)/shard_map/ppermute | solution.py:213
  89.3 0.2 copy.9.w_ref
  89.5 0.0 collective-permute-done.4.corner_below_ref
  89.5 2.4 %collective-permute-done.5.corner_above_ref = bf16[64,256]{1,0:T(8,128)(2,1)S(1)} collective-permute-done((bf16[64,256]{1,0:T(8,128)(2,1)S(1)}, bf16[64,256]{1,0:T(8,128)(2,1)S(1)}, u32[]{:S(2)}, u32[]{:S(2)}) %collective-permute-start.5) | collective-permute-done | bytes 32800 | tf_op jit(solution)/shard_map/ppermute | solution.py:213
  91.8 0.9 shard_map.52
  92.7 0.0 all-to-all-done.1
  92.8 0.6 broadcast_in_dim.12
  93.4 7.2 %all-to-all-start.2 = ((f32[16,4,128]{2,1,0:T(4,128)}), f32[16,4,128]{2,1,0:T(4,128)S(1)}, u32[]{:S(2)}, u32[]{:S(2)}) async-start(f32[16,4,128]{2,1,0:T(4,128)} %broadcast_in_dim.12), calls=%async_computation.2 | async-start | bytes 65536 | tf_op jit(solution)/shard_map/all_to_all | solution.py:273
  100.5 0.9 reshape.36
  101.4 5.4 %all-to-all-done.2 = f32[16,4,128]{2,1,0:T(4,128)S(1)} async-done(((f32[16,4,128]{2,1,0:T(4,128)}), f32[16,4,128]{2,1,0:T(4,128)S(1)}, u32[]{:S(2)}, u32[]{:S(2)}) %all-to-all-start.2) | async-done | bytes 32800 | tf_op jit(solution)/shard_map/all_to_all | solution.py:273
  106.8 0.6 slice_multiply_fusion
  (17 shorter events, 0.3 us)
Async XLA Ops:
  0.6 1.2 %copy-start = (bf16[1,64,4,4,128]{4,3,2,1,0:T(4,128)(2,1)S(1)}, bf16[1,64,4,4,128]{4,3,2,1,0:T(4,128)(2,1)}, u32[]{:S(2)}) copy-start(bf16[1,64,4,4,128]{4,3,2,1,0:T(4,128)(2,1)} %param.3) | copy-start | bytes 786436
  2.8 23.1 %collective-permute-start.2 = (bf16[64,1024]{1,0:T(8,128)(2,1)S(1)}, bf16[64,1024]{1,0:T(8,128)(2,1)S(1)}, u32[]{:S(2)}, u32[]{:S(2)}) collective-permute-start(bf16[64,1024]{1,0:T(8,128)(2,1)S(1)} %pad_maximum_fusion.2), channel_id=1, source_target_pairs={{0,1},{1,2},{2,3},{3,4},{4,5},{5,6},{6,7},{7,8},{8,9},{9,10},{10,1... | collective-permute-start | bytes 393224 | tf_op jit(solution)/shard_map/ppermute | solution.py:228
  18.6 7.3 %collective-permute-start = (bf16[64,1152]{1,0:T(8,128)(2,1)S(1)}, bf16[64,1152]{1,0:T(8,128)(2,1)S(1)}, u32[]{:S(2)}, u32[]{:S(2)}) collective-permute-start(bf16[64,1152]{1,0:T(8,128)(2,1)S(1)} %pad_maximum_fusion), channel_id=1, source_target_pairs={{0,16},{16,32},{32,48},{1,17},{17,33},{33,49},{2,18},{18,34},{34,5... | collective-permute-start | bytes 442376 | tf_op jit(solution)/shard_map/ppermute | solution.py:213
  22.0 3.5 %copy-start.1 = (bf16[64,1728]{1,0:T(8,128)(2,1)S(1)}, bf16[64,1728]{1,0:T(8,128)(2,1)}, u32[]{:S(2)}) copy-start(bf16[64,1728]{1,0:T(8,128)(2,1)} %param.5) | copy-start | bytes 663556
  22.0 7.2 %collective-permute-start.1 = (bf16[64,1152]{1,0:T(8,128)(2,1)S(1)}, bf16[64,1152]{1,0:T(8,128)(2,1)S(1)}, u32[]{:S(2)}, u32[]{:S(2)}) collective-permute-start(bf16[64,1152]{1,0:T(8,128)(2,1)S(1)} %pad_maximum_fusion.1), channel_id=1, source_target_pairs={{16,0},{32,16},{48,32},{17,1},{33,17},{49,33},{18,2},{34,18},{50,3... | collective-permute-start | bytes 442376 | tf_op jit(solution)/shard_map/ppermute | solution.py:213
  31.0 15.4 %copy-start.2 = (bf16[64,512]{1,0:T(8,128)(2,1)S(1)}, bf16[64,512]{1,0:T(8,128)(2,1)}, u32[]{:S(2)}) copy-start(bf16[64,512]{1,0:T(8,128)(2,1)} %get-tuple-element.46) | copy-start | bytes 196612
  31.0 26.4 %all-to-all-start = ((f32[32,8,512]{2,1,0:T(8,128)}), f32[32,8,512]{2,1,0:T(8,128)S(1)}, u32[]{:S(2)}, u32[]{:S(2)}) async-start(f32[32,8,512]{2,1,0:T(8,128)} %shard_map.51), calls=%async_computation | async-start | bytes 1048576 | tf_op jit(solution)/shard_map/all_to_all | solution.py:258
  46.5 36.9 %collective-permute-start.3 = (bf16[64,512]{1,0:T(8,128)(2,1)S(1)}, bf16[64,512]{1,0:T(8,128)(2,1)S(1)}, u32[]{:S(2)}, u32[]{:S(2)}) collective-permute-start(bf16[64,512]{1,0:T(8,128)(2,1)S(1)} %copy-done.2), channel_id=1, source_target_pairs={{1,0},{2,1},{3,2},{4,3},{5,4},{6,5},{7,6},{8,7},{9,8},{10,9},{11,1... | collective-permute-start | bytes 196616 | tf_op jit(solution)/shard_map/ppermute | solution.py:228
  58.1 34.6 %all-to-all-start.1 = ((f32[32,4,128]{2,1,0:T(4,128)}), f32[32,4,128]{2,1,0:T(4,128)S(1)}, u32[]{:S(2)}, u32[]{:S(2)}) async-start(f32[32,4,128]{2,1,0:T(4,128)} %bitcast.4), calls=%async_computation.1 | async-start | bytes 131072 | tf_op jit(solution)/shard_map/all_to_all | solution.py:263
  83.4 6.1 %collective-permute-start.4 = (bf16[64,256]{1,0:T(8,128)(2,1)S(1)}, bf16[64,256]{1,0:T(8,128)(2,1)S(1)}, u32[]{:S(2)}, u32[]{:S(2)}) collective-permute-start(bf16[64,256]{1,0:T(8,128)(2,1)S(1)} %pad_maximum_fusion.5), channel_id=1, source_target_pairs={{0,16},{16,32},{32,48},{1,17},{17,33},{33,49},{2,18},{18,34},{34,5... | collective-permute-start | bytes 98312 | tf_op jit(solution)/shard_map/ppermute | solution.py:213
  86.0 5.8 %collective-permute-start.5 = (bf16[64,256]{1,0:T(8,128)(2,1)S(1)}, bf16[64,256]{1,0:T(8,128)(2,1)S(1)}, u32[]{:S(2)}, u32[]{:S(2)}) collective-permute-start(bf16[64,256]{1,0:T(8,128)(2,1)S(1)} %pad_maximum_fusion.6), channel_id=1, source_target_pairs={{16,0},{32,16},{48,32},{17,1},{33,17},{49,33},{18,2},{34,18},{50,3... | collective-permute-start | bytes 98312 | tf_op jit(solution)/shard_map/ppermute | solution.py:213
  93.4 13.4 %all-to-all-start.2 = ((f32[16,4,128]{2,1,0:T(4,128)}), f32[16,4,128]{2,1,0:T(4,128)S(1)}, u32[]{:S(2)}, u32[]{:S(2)}) async-start(f32[16,4,128]{2,1,0:T(4,128)} %broadcast_in_dim.12), calls=%async_computation.2 | async-start | bytes 65536 | tf_op jit(solution)/shard_map/all_to_all | solution.py:273

commit v6 on v5

--- a/solution.py
+++ b/solution.py
@@ -262,7 +262,7 @@
     high = jnp.where(core == 0, back, far[:, :HALF])
     parts = lax.all_to_all(
         jnp.broadcast_to(mine.reshape(1, 8, 4, LANES), (4, 8, 4, LANES)).reshape(32, 4, LANES),
-        AXES, 0, 0, axis_index_groups=lines_along_z(16),
+        AXES, 0, 0, axis_index_groups=lines_along_z(8),
     )
     last = (NX - 1) * LANES
     corner_below = shifted_by(jnp.concatenate([low[:, last:], high[:, last:]], axis=1), "px", 1)

time: 108 us -> 110 us (1.019)
  the two profiles are of different devices: /device:TPU:2 before, /device:TPU:32 now
where the time goes in v6:
time: 110 us
  starting transfers between devices  66.9 us (61%)
  waiting for transfers between devices  32.9 us (30%)
  local copies, waits for them, and re-layouts  4.16 us (4%)
  Pallas kernels  3.59 us (3%)
  other arithmetic  1.46 us (1%)
    all_to_all x1, starting transfers between devices, local(): lax.all_to_all(jnp.broadcast_to(mine.reshape(1, 8, 4, LANES), (4, 8, 4, L...  24.5 us
    ppermute x2, starting transfers between devices, along_y(): return lax.ppermute(x, ('core', 'y', 'zhi'), pairs)  17 us
    all_to_all x1, starting transfers between devices, local(): parts = lax.all_to_all(message, ('core', 'px', 'y'), 0, 0)  12.8 us
    all_to_all x1, waiting for transfers between devices, local(): parts = lax.all_to_all(message, ('core', 'px', 'y'), 0, 0)  10.7 us
    ppermute x4, starting transfers between devices, shifted_by(): return lax.ppermute(x, axis, pairs)  8.79 us
    ppermute x4, waiting for transfers between devices, shifted_by(): return lax.ppermute(x, axis, pairs)  7.29 us
    all_to_all x1, waiting for transfers between devices, local(): lax.all_to_all(jnp.broadcast_to(mine, (16, 4, LANES)), ('px', 'y'), 0, 0)  6.75 us
    all_to_all x1, waiting for transfers between devices, local(): lax.all_to_all(jnp.broadcast_to(mine.reshape(1, 8, 4, LANES), (4, 8, 4, L...  6.74 us
  transfers between devices with their start and end apart: 9, of which 7 were waited for; matrix products, arithmetic and copies ran while one was open for 2% of the time, Pallas kernels for 2%

profile of v6, /device:TPU:32, one launch (start us, length us, event | category | flops | bytes accessed | tf_op | source)
XLA Modules:
  0.0 110.0 jit_solution(3186033244648980698)
XLA Ops:
  0.6 0.0 copy-start
  0.6 1.2 %reshape.31.g_ref = bf16[64,2048]{1,0:T(8,128)(2,1)S(1)} reshape(bf16[1,64,4,4,128]{4,3,2,1,0:T(4,128)(2,1)} %param.4) | data formatting | bytes 524288 | tf_op jit(solution)/shard_map/reshape | solution.py:233
  1.9 0.0 copy-done
  1.9 0.2 reshape.34.a_ref
  2.1 0.7 broadcast_select_fusion.2
  2.8 15.7 %collective-permute-start.2 = (bf16[64,1024]{1,0:T(8,128)(2,1)S(1)}, bf16[64,1024]{1,0:T(8,128)(2,1)S(1)}, u32[]{:S(2)}, u32[]{:S(2)}) collective-permute-start(bf16[64,1024]{1,0:T(8,128)(2,1)S(1)} %pad_maximum_fusion.2), channel_id=1, source_target_pairs={{0,1},{1,2},{2,3},{3,4},{4,5},{5,6},{6,7},{7,8},{8,9},{9,10},{10,1... | collective-permute-start | bytes 393224 | tf_op jit(solution)/shard_map/ppermute | solution.py:228
  18.6 3.4 %collective-permute-start = (bf16[64,1152]{1,0:T(8,128)(2,1)S(1)}, bf16[64,1152]{1,0:T(8,128)(2,1)S(1)}, u32[]{:S(2)}, u32[]{:S(2)}) collective-permute-start(bf16[64,1152]{1,0:T(8,128)(2,1)S(1)} %pad_maximum_fusion), channel_id=1, source_target_pairs={{0,16},{16,32},{32,48},{1,17},{17,33},{33,49},{2,18},{18,34},{34,5... | collective-permute-start | bytes 442376 | tf_op jit(solution)/shard_map/ppermute | solution.py:213
  22.0 0.0 copy-start.1
  22.0 1.4 %collective-permute-start.1 = (bf16[64,1152]{1,0:T(8,128)(2,1)S(1)}, bf16[64,1152]{1,0:T(8,128)(2,1)S(1)}, u32[]{:S(2)}, u32[]{:S(2)}) collective-permute-start(bf16[64,1152]{1,0:T(8,128)(2,1)S(1)} %pad_maximum_fusion.1), channel_id=1, source_target_pairs={{16,0},{32,16},{48,32},{17,1},{33,17},{49,33},{18,2},{34,18},{50,3... | collective-permute-start | bytes 442376 | tf_op jit(solution)/shard_map/ppermute | solution.py:213
  23.5 0.9 shard_map.50
  24.4 0.0 copy-done.1
  24.4 0.3 reshape.32
  24.8 1.5 %collective-permute-done.2.far_ref = bf16[64,1024]{1,0:T(8,128)(2,1)S(1)} collective-permute-done((bf16[64,1024]{1,0:T(8,128)(2,1)S(1)}, bf16[64,1024]{1,0:T(8,128)(2,1)S(1)}, u32[]{:S(2)}, u32[]{:S(2)}) %collective-permute-start.2) | collective-permute-done | bytes 131104 | tf_op jit(solution)/shard_map/ppermute | solution.py:228
  26.2 0.0 collective-permute-done.below_ref
  26.2 3.0 %collective-permute-done.1.above_ref = bf16[64,1152]{1,0:T(8,128)(2,1)S(1)} collective-permute-done((bf16[64,1152]{1,0:T(8,128)(2,1)S(1)}, bf16[64,1152]{1,0:T(8,128)(2,1)S(1)}, u32[]{:S(2)}, u32[]{:S(2)}) %collective-permute-start.1) | collective-permute-done | bytes 147488 | tf_op jit(solution)/shard_map/ppermute | solution.py:213
  29.2 1.8 %shard_map.51 = f32[32,8,512]{2,1,0:T(8,128)} custom-call(s32[1]{0:T(128)} %bitcast.core_ref, bf16[64,2048]{1,0:T(8,128)(2,1)S(1)} %reshape.31.g_ref, f32[576,192]{1,0:T(8,128)S(1)} %get-tuple-element.16.gk_ref, bf16[192,1024]{1,0:T(8,128)(2,1)S(1)} %get-tuple-element.17.row_ref, bf16[192,1024]{1,0:T(8,128)(2,1)S(1)} %get-tuple-element.18.column_ref, ...), custom_call_target="tpu_custom_call" | custom-call | tf_op jit(solution)/shard_map/pallas_call | solution.py:193
  31.0 0.0 copy-start.2
  31.0 12.8 %all-to-all-start = ((f32[32,8,512]{2,1,0:T(8,128)}), f32[32,8,512]{2,1,0:T(8,128)S(1)}, u32[]{:S(2)}, u32[]{:S(2)}) async-start(f32[32,8,512]{2,1,0:T(8,128)} %shard_map.51), calls=%async_computation | async-start | bytes 1048576 | tf_op jit(solution)/shard_map/all_to_all | solution.py:258
  43.9 0.0 copy-done.2
  43.9 1.3 %collective-permute-start.3 = (bf16[64,512]{1,0:T(8,128)(2,1)S(1)}, bf16[64,512]{1,0:T(8,128)(2,1)S(1)}, u32[]{:S(2)}, u32[]{:S(2)}) collective-permute-start(bf16[64,512]{1,0:T(8,128)(2,1)S(1)} %copy-done.2), channel_id=1, source_target_pairs={{1,0},{2,1},{3,2},{4,3},{5,4},{6,5},{7,6},{8,7},{9,8},{10,9},{11,1... | collective-permute-start | bytes 196616 | tf_op jit(solution)/shard_map/ppermute | solution.py:228
  45.2 10.7 %all-to-all-done = f32[32,8,512]{2,1,0:T(8,128)S(1)} async-done(((f32[32,8,512]{2,1,0:T(8,128)}), f32[32,8,512]{2,1,0:T(8,128)S(1)}, u32[]{:S(2)}, u32[]{:S(2)}) %all-to-all-start) | async-done | bytes 524320 | tf_op jit(solution)/shard_map/all_to_all | solution.py:258
  55.9 0.6 broadcast_in_dim.11
  56.6 24.5 %all-to-all-start.1 = ((f32[32,4,128]{2,1,0:T(4,128)}), f32[32,4,128]{2,1,0:T(4,128)S(1)}, u32[]{:S(2)}, u32[]{:S(2)}) async-start(f32[32,4,128]{2,1,0:T(4,128)} %bitcast.4), calls=%async_computation.1 | async-start | bytes 131072 | tf_op jit(solution)/shard_map/all_to_all | solution.py:263
  81.0 0.0 collective-permute-done.3
  81.1 2.7 %collective-permute-start.4 = (bf16[64,256]{1,0:T(8,128)(2,1)S(1)}, bf16[64,256]{1,0:T(8,128)(2,1)S(1)}, u32[]{:S(2)}, u32[]{:S(2)}) collective-permute-start(bf16[64,256]{1,0:T(8,128)(2,1)S(1)} %pad_maximum_fusion.5), channel_id=1, source_target_pairs={{0,16},{16,32},{32,48},{1,17},{17,33},{33,49},{2,18},{18,34},{34,5... | collective-permute-start | bytes 98312 | tf_op jit(solution)/shard_map/ppermute | solution.py:213
  83.8 1.3 %collective-permute-start.5 = (bf16[64,256]{1,0:T(8,128)(2,1)S(1)}, bf16[64,256]{1,0:T(8,128)(2,1)S(1)}, u32[]{:S(2)}, u32[]{:S(2)}) collective-permute-start(bf16[64,256]{1,0:T(8,128)(2,1)S(1)} %pad_maximum_fusion.6), channel_id=1, source_target_pairs={{16,0},{32,16},{48,32},{17,1},{33,17},{49,33},{18,2},{34,18},{50,3... | collective-permute-start | bytes 98312 | tf_op jit(solution)/shard_map/ppermute | solution.py:213
  85.1 0.2 copy.9.w_ref
  85.3 0.1 collective-permute-done.4.corner_below_ref
  85.4 4.2 %collective-permute-done.5.corner_above_ref = bf16[64,256]{1,0:T(8,128)(2,1)S(1)} collective-permute-done((bf16[64,256]{1,0:T(8,128)(2,1)S(1)}, bf16[64,256]{1,0:T(8,128)(2,1)S(1)}, u32[]{:S(2)}, u32[]{:S(2)}) %collective-permute-start.5) | collective-permute-done | bytes 32800 | tf_op jit(solution)/shard_map/ppermute | solution.py:213
  89.6 0.9 shard_map.52
  90.5 6.7 %all-to-all-done.1 = f32[32,4,128]{2,1,0:T(4,128)S(1)} async-done(((f32[32,4,128]{2,1,0:T(4,128)}), f32[32,4,128]{2,1,0:T(4,128)S(1)}, u32[]{:S(2)}, u32[]{:S(2)}) %all-to-all-start.1) | async-done | bytes 65568 | tf_op jit(solution)/shard_map/all_to_all | solution.py:263
  97.3 0.6 broadcast_in_dim.12
  97.9 3.8 %all-to-all-start.2 = ((f32[16,4,128]{2,1,0:T(4,128)}), f32[16,4,128]{2,1,0:T(4,128)S(1)}, u32[]{:S(2)}, u32[]{:S(2)}) async-start(f32[16,4,128]{2,1,0:T(4,128)} %broadcast_in_dim.12), calls=%async_computation.2 | async-start | bytes 65536 | tf_op jit(solution)/shard_map/all_to_all | solution.py:273
  101.7 0.9 reshape.36
  102.6 6.7 %all-to-all-done.2 = f32[16,4,128]{2,1,0:T(4,128)S(1)} async-done(((f32[16,4,128]{2,1,0:T(4,128)}), f32[16,4,128]{2,1,0:T(4,128)S(1)}, u32[]{:S(2)}, u32[]{:S(2)}) %all-to-all-start.2) | async-done | bytes 32800 | tf_op jit(solution)/shard_map/all_to_all | solution.py:273
  109.4 0.6 slice_multiply_fusion
  (17 shorter events, 0.3 us)
Async XLA Ops:
  0.6 1.2 %copy-start = (bf16[1,64,4,4,128]{4,3,2,1,0:T(4,128)(2,1)S(1)}, bf16[1,64,4,4,128]{4,3,2,1,0:T(4,128)(2,1)}, u32[]{:S(2)}) copy-start(bf16[1,64,4,4,128]{4,3,2,1,0:T(4,128)(2,1)} %param.3) | copy-start | bytes 786436
  2.8 23.4 %collective-permute-start.2 = (bf16[64,1024]{1,0:T(8,128)(2,1)S(1)}, bf16[64,1024]{1,0:T(8,128)(2,1)S(1)}, u32[]{:S(2)}, u32[]{:S(2)}) collective-permute-start(bf16[64,1024]{1,0:T(8,128)(2,1)S(1)} %pad_maximum_fusion.2), channel_id=1, source_target_pairs={{0,1},{1,2},{2,3},{3,4},{4,5},{5,6},{6,7},{7,8},{8,9},{9,10},{10,1... | collective-permute-start | bytes 393224 | tf_op jit(solution)/shard_map/ppermute | solution.py:228
  18.6 7.7 %collective-permute-start = (bf16[64,1152]{1,0:T(8,128)(2,1)S(1)}, bf16[64,1152]{1,0:T(8,128)(2,1)S(1)}, u32[]{:S(2)}, u32[]{:S(2)}) collective-permute-start(bf16[64,1152]{1,0:T(8,128)(2,1)S(1)} %pad_maximum_fusion), channel_id=1, source_target_pairs={{0,16},{16,32},{32,48},{1,17},{17,33},{33,49},{2,18},{18,34},{34,5... | collective-permute-start | bytes 442376 | tf_op jit(solution)/shard_map/ppermute | solution.py:213
  22.0 2.3 %copy-start.1 = (bf16[64,1728]{1,0:T(8,128)(2,1)S(1)}, bf16[64,1728]{1,0:T(8,128)(2,1)}, u32[]{:S(2)}) copy-start(bf16[64,1728]{1,0:T(8,128)(2,1)} %param.5) | copy-start | bytes 663556
  22.0 7.2 %collective-permute-start.1 = (bf16[64,1152]{1,0:T(8,128)(2,1)S(1)}, bf16[64,1152]{1,0:T(8,128)(2,1)S(1)}, u32[]{:S(2)}, u32[]{:S(2)}) collective-permute-start(bf16[64,1152]{1,0:T(8,128)(2,1)S(1)} %pad_maximum_fusion.1), channel_id=1, source_target_pairs={{16,0},{32,16},{48,32},{17,1},{33,17},{49,33},{18,2},{34,18},{50,3... | collective-permute-start | bytes 442376 | tf_op jit(solution)/shard_map/ppermute | solution.py:213
  31.0 12.9 %copy-start.2 = (bf16[64,512]{1,0:T(8,128)(2,1)S(1)}, bf16[64,512]{1,0:T(8,128)(2,1)}, u32[]{:S(2)}) copy-start(bf16[64,512]{1,0:T(8,128)(2,1)} %get-tuple-element.46) | copy-start | bytes 196612
  31.0 24.8 %all-to-all-start = ((f32[32,8,512]{2,1,0:T(8,128)}), f32[32,8,512]{2,1,0:T(8,128)S(1)}, u32[]{:S(2)}, u32[]{:S(2)}) async-start(f32[32,8,512]{2,1,0:T(8,128)} %shard_map.51), calls=%async_computation | async-start | bytes 1048576 | tf_op jit(solution)/shard_map/all_to_all | solution.py:258
  43.9 37.1 %collective-permute-start.3 = (bf16[64,512]{1,0:T(8,128)(2,1)S(1)}, bf16[64,512]{1,0:T(8,128)(2,1)S(1)}, u32[]{:S(2)}, u32[]{:S(2)}) collective-permute-start(bf16[64,512]{1,0:T(8,128)(2,1)S(1)} %copy-done.2), channel_id=1, source_target_pairs={{1,0},{2,1},{3,2},{4,3},{5,4},{6,5},{7,6},{8,7},{9,8},{10,9},{11,1... | collective-permute-start | bytes 196616 | tf_op jit(solution)/shard_map/ppermute | solution.py:228
  56.6 40.7 %all-to-all-start.1 = ((f32[32,4,128]{2,1,0:T(4,128)}), f32[32,4,128]{2,1,0:T(4,128)S(1)}, u32[]{:S(2)}, u32[]{:S(2)}) async-start(f32[32,4,128]{2,1,0:T(4,128)} %bitcast.4), calls=%async_computation.1 | async-start | bytes 131072 | tf_op jit(solution)/shard_map/all_to_all | solution.py:263
  81.1 4.3 %collective-permute-start.4 = (bf16[64,256]{1,0:T(8,128)(2,1)S(1)}, bf16[64,256]{1,0:T(8,128)(2,1)S(1)}, u32[]{:S(2)}, u32[]{:S(2)}) collective-permute-start(bf16[64,256]{1,0:T(8,128)(2,1)S(1)} %pad_maximum_fusion.5), channel_id=1, source_target_pairs={{0,16},{16,32},{32,48},{1,17},{17,33},{33,49},{2,18},{18,34},{34,5... | collective-permute-start | bytes 98312 | tf_op jit(solution)/shard_map/ppermute | solution.py:213
  83.8 5.8 %collective-permute-start.5 = (bf16[64,256]{1,0:T(8,128)(2,1)S(1)}, bf16[64,256]{1,0:T(8,128)(2,1)S(1)}, u32[]{:S(2)}, u32[]{:S(2)}) collective-permute-start(bf16[64,256]{1,0:T(8,128)(2,1)S(1)} %pad_maximum_fusion.6), channel_id=1, source_target_pairs={{16,0},{32,16},{48,32},{17,1},{33,17},{49,33},{18,2},{34,18},{50,3... | collective-permute-start | bytes 98312 | tf_op jit(solution)/shard_map/ppermute | solution.py:213
  97.9 11.5 %all-to-all-start.2 = ((f32[16,4,128]{2,1,0:T(4,128)}), f32[16,4,128]{2,1,0:T(4,128)S(1)}, u32[]{:S(2)}, u32[]{:S(2)}) async-start(f32[16,4,128]{2,1,0:T(4,128)} %broadcast_in_dim.12), calls=%async_computation.2 | async-start | bytes 65536 | tf_op jit(solution)/shard_map/all_to_all | solution.py:273

commit v7 on v6

--- a/solution.py
+++ b/solution.py
@@ -262,7 +262,7 @@
     high = jnp.where(core == 0, back, far[:, :HALF])
     parts = lax.all_to_all(
         jnp.broadcast_to(mine.reshape(1, 8, 4, LANES), (4, 8, 4, LANES)).reshape(32, 4, LANES),
-        AXES, 0, 0, axis_index_groups=lines_along_z(8),
+        AXES, 0, 0, axis_index_groups=lines_along_z(24),
     )
     last = (NX - 1) * LANES
     corner_below = shifted_by(jnp.concatenate([low[:, last:], high[:, last:]], axis=1), "px", 1)

time: 110 us -> 108 us (0.982)
  the two profiles are of different devices: /device:TPU:32 before, /device:TPU:1 now
where the time goes in v7:
time: 108 us; the launch traced here: 107 us
  starting transfers between devices  69.4 us (64%)
  waiting for transfers between devices  27.9 us (26%)
  local copies, waits for them, and re-layouts  4.16 us (4%)
  Pallas kernels  3.58 us (3%)
  other arithmetic  1.46 us (1%)
    all_to_all x1, starting transfers between devices, local(): parts = lax.all_to_all(message, ('core', 'px', 'y'), 0, 0)  24.2 us
    all_to_all x1, starting transfers between devices, local(): lax.all_to_all(jnp.broadcast_to(mine.reshape(1, 8, 4, LANES), (4, 8, 4, L...  19.6 us
    ppermute x2, waiting for transfers between devices, along_y(): return lax.ppermute(x, ('core', 'y', 'zhi'), pairs)  10.6 us
    ppermute x4, starting transfers between devices, shifted_by(): return lax.ppermute(x, axis, pairs)  9.95 us
    ppermute x2, starting transfers between devices, along_y(): return lax.ppermute(x, ('core', 'y', 'zhi'), pairs)  9.74 us
    all_to_all x1, starting transfers between devices, local(): lax.all_to_all(jnp.broadcast_to(mine, (16, 4, LANES)), ('px', 'y'), 0, 0)  5.95 us
    all_to_all x1, waiting for transfers between devices, local(): lax.all_to_all(jnp.broadcast_to(mine, (16, 4, LANES)), ('px', 'y'), 0, 0)  5.6 us
    all_to_all x1, waiting for transfers between devices, local(): lax.all_to_all(jnp.broadcast_to(mine.reshape(1, 8, 4, LANES), (4, 8, 4, L...  5.5 us
  transfers between devices with their start and end apart: 9, of which 5 were waited for; matrix products, arithmetic and copies ran while one was open for 2% of the time, Pallas kernels for 2%

profile of v7, /device:TPU:1, one launch (start us, length us, event | category | flops | bytes accessed | tf_op | source)
XLA Modules:
  0.0 107.4 jit_solution(8091641036164502258)
XLA Ops:
  0.6 0.0 copy-start
  0.6 1.2 %reshape.31.g_ref = bf16[64,2048]{1,0:T(8,128)(2,1)S(1)} reshape(bf16[1,64,4,4,128]{4,3,2,1,0:T(4,128)(2,1)} %param.4) | data formatting | bytes 524288 | tf_op jit(solution)/shard_map/reshape | solution.py:233
  1.9 0.0 copy-done
  1.9 0.2 reshape.34.a_ref
  2.1 0.7 broadcast_select_fusion.2
  2.8 1.3 %collective-permute-start.2 = (bf16[64,1024]{1,0:T(8,128)(2,1)S(1)}, bf16[64,1024]{1,0:T(8,128)(2,1)S(1)}, u32[]{:S(2)}, u32[]{:S(2)}) collective-permute-start(bf16[64,1024]{1,0:T(8,128)(2,1)S(1)} %pad_maximum_fusion.2), channel_id=1, source_target_pairs={{0,1},{1,2},{2,3},{3,4},{4,5},{5,6},{6,7},{7,8},{8,9},{9,10},{10,1... | collective-permute-start | bytes 393224 | tf_op jit(solution)/shard_map/ppermute | solution.py:228
  4.2 4.0 %collective-permute-start = (bf16[64,1152]{1,0:T(8,128)(2,1)S(1)}, bf16[64,1152]{1,0:T(8,128)(2,1)S(1)}, u32[]{:S(2)}, u32[]{:S(2)}) collective-permute-start(bf16[64,1152]{1,0:T(8,128)(2,1)S(1)} %pad_maximum_fusion), channel_id=1, source_target_pairs={{0,16},{16,32},{32,48},{1,17},{17,33},{33,49},{2,18},{18,34},{34,5... | collective-permute-start | bytes 442376 | tf_op jit(solution)/shard_map/ppermute | solution.py:213
  8.1 0.0 copy-start.1
  8.1 1.4 %collective-permute-start.1 = (bf16[64,1152]{1,0:T(8,128)(2,1)S(1)}, bf16[64,1152]{1,0:T(8,128)(2,1)S(1)}, u32[]{:S(2)}, u32[]{:S(2)}) collective-permute-start(bf16[64,1152]{1,0:T(8,128)(2,1)S(1)} %pad_maximum_fusion.1), channel_id=1, source_target_pairs={{16,0},{32,16},{48,32},{17,1},{33,17},{49,33},{18,2},{34,18},{50,3... | collective-permute-start | bytes 442376 | tf_op jit(solution)/shard_map/ppermute | solution.py:213
  9.6 0.9 shard_map.50
  10.5 0.0 copy-done.1
  10.5 0.3 reshape.32
  10.9 10.6 %collective-permute-done.2.far_ref = bf16[64,1024]{1,0:T(8,128)(2,1)S(1)} collective-permute-done((bf16[64,1024]{1,0:T(8,128)(2,1)S(1)}, bf16[64,1024]{1,0:T(8,128)(2,1)S(1)}, u32[]{:S(2)}, u32[]{:S(2)}) %collective-permute-start.2) | collective-permute-done | bytes 131104 | tf_op jit(solution)/shard_map/ppermute | solution.py:228
  21.4 0.0 collective-permute-done.below_ref
  21.4 0.0 collective-permute-done.1.above_ref
  21.4 1.8 %shard_map.51 = f32[32,8,512]{2,1,0:T(8,128)} custom-call(s32[1]{0:T(128)} %bitcast.core_ref, bf16[64,2048]{1,0:T(8,128)(2,1)S(1)} %reshape.31.g_ref, f32[576,192]{1,0:T(8,128)S(1)} %get-tuple-element.16.gk_ref, bf16[192,1024]{1,0:T(8,128)(2,1)S(1)} %get-tuple-element.17.row_ref, bf16[192,1024]{1,0:T(8,128)(2,1)S(1)} %get-tuple-element.18.column_ref, ...), custom_call_target="tpu_custom_call" | custom-call | tf_op jit(solution)/shard_map/pallas_call | solution.py:193
  23.3 0.0 copy-start.2
  23.3 24.2 %all-to-all-start = ((f32[32,8,512]{2,1,0:T(8,128)}), f32[32,8,512]{2,1,0:T(8,128)S(1)}, u32[]{:S(2)}, u32[]{:S(2)}) async-start(f32[32,8,512]{2,1,0:T(8,128)} %shard_map.51), calls=%async_computation | async-start | bytes 1048576 | tf_op jit(solution)/shard_map/all_to_all | solution.py:258
  47.4 0.0 copy-done.2
  47.4 8.4 %collective-permute-start.3 = (bf16[64,512]{1,0:T(8,128)(2,1)S(1)}, bf16[64,512]{1,0:T(8,128)(2,1)S(1)}, u32[]{:S(2)}, u32[]{:S(2)}) collective-permute-start(bf16[64,512]{1,0:T(8,128)(2,1)S(1)} %copy-done.2), channel_id=1, source_target_pairs={{1,0},{2,1},{3,2},{4,3},{5,4},{6,5},{7,6},{8,7},{9,8},{10,9},{11,1... | collective-permute-start | bytes 196616 | tf_op jit(solution)/shard_map/ppermute | solution.py:228
  55.9 2.7 %all-to-all-done = f32[32,8,512]{2,1,0:T(8,128)S(1)} async-done(((f32[32,8,512]{2,1,0:T(8,128)}), f32[32,8,512]{2,1,0:T(8,128)S(1)}, u32[]{:S(2)}, u32[]{:S(2)}) %all-to-all-start) | async-done | bytes 524320 | tf_op jit(solution)/shard_map/all_to_all | solution.py:258
  58.7 0.6 broadcast_in_dim.11
  59.3 19.6 %all-to-all-start.1 = ((f32[32,4,128]{2,1,0:T(4,128)}), f32[32,4,128]{2,1,0:T(4,128)S(1)}, u32[]{:S(2)}, u32[]{:S(2)}) async-start(f32[32,4,128]{2,1,0:T(4,128)} %bitcast.4), calls=%async_computation.1 | async-start | bytes 131072 | tf_op jit(solution)/shard_map/all_to_all | solution.py:263
  78.9 0.0 collective-permute-done.3
  79.0 3.3 %collective-permute-start.4 = (bf16[64,256]{1,0:T(8,128)(2,1)S(1)}, bf16[64,256]{1,0:T(8,128)(2,1)S(1)}, u32[]{:S(2)}, u32[]{:S(2)}) collective-permute-start(bf16[64,256]{1,0:T(8,128)(2,1)S(1)} %pad_maximum_fusion.5), channel_id=1, source_target_pairs={{0,16},{16,32},{32,48},{1,17},{17,33},{33,49},{2,18},{18,34},{34,5... | collective-permute-start | bytes 98312 | tf_op jit(solution)/shard_map/ppermute | solution.py:213
  82.3 1.3 %collective-permute-start.5 = (bf16[64,256]{1,0:T(8,128)(2,1)S(1)}, bf16[64,256]{1,0:T(8,128)(2,1)S(1)}, u32[]{:S(2)}, u32[]{:S(2)}) collective-permute-start(bf16[64,256]{1,0:T(8,128)(2,1)S(1)} %pad_maximum_fusion.6), channel_id=1, source_target_pairs={{16,0},{32,16},{48,32},{17,1},{33,17},{49,33},{18,2},{34,18},{50,3... | collective-permute-start | bytes 98312 | tf_op jit(solution)/shard_map/ppermute | solution.py:213
  83.6 0.2 copy.9.w_ref
  83.8 0.0 collective-permute-done.4.corner_below_ref
  83.8 3.5 %collective-permute-done.5.corner_above_ref = bf16[64,256]{1,0:T(8,128)(2,1)S(1)} collective-permute-done((bf16[64,256]{1,0:T(8,128)(2,1)S(1)}, bf16[64,256]{1,0:T(8,128)(2,1)S(1)}, u32[]{:S(2)}, u32[]{:S(2)}) %collective-permute-start.5) | collective-permute-done | bytes 32800 | tf_op jit(solution)/shard_map/ppermute | solution.py:213
  87.3 0.9 shard_map.52
  88.1 5.5 %all-to-all-done.1 = f32[32,4,128]{2,1,0:T(4,128)S(1)} async-done(((f32[32,4,128]{2,1,0:T(4,128)}), f32[32,4,128]{2,1,0:T(4,128)S(1)}, u32[]{:S(2)}, u32[]{:S(2)}) %all-to-all-start.1) | async-done | bytes 65568 | tf_op jit(solution)/shard_map/all_to_all | solution.py:263
  93.7 0.6 broadcast_in_dim.12
  94.3 6.0 %all-to-all-start.2 = ((f32[16,4,128]{2,1,0:T(4,128)}), f32[16,4,128]{2,1,0:T(4,128)S(1)}, u32[]{:S(2)}, u32[]{:S(2)}) async-start(f32[16,4,128]{2,1,0:T(4,128)} %broadcast_in_dim.12), calls=%async_computation.2 | async-start | bytes 65536 | tf_op jit(solution)/shard_map/all_to_all | solution.py:273
  100.3 0.9 reshape.36
  101.1 5.6 %all-to-all-done.2 = f32[16,4,128]{2,1,0:T(4,128)S(1)} async-done(((f32[16,4,128]{2,1,0:T(4,128)}), f32[16,4,128]{2,1,0:T(4,128)S(1)}, u32[]{:S(2)}, u32[]{:S(2)}) %all-to-all-start.2) | async-done | bytes 32800 | tf_op jit(solution)/shard_map/all_to_all | solution.py:273
  106.8 0.6 slice_multiply_fusion
  (17 shorter events, 0.3 us)
Async XLA Ops:
  0.6 1.2 %copy-start = (bf16[1,64,4,4,128]{4,3,2,1,0:T(4,128)(2,1)S(1)}, bf16[1,64,4,4,128]{4,3,2,1,0:T(4,128)(2,1)}, u32[]{:S(2)}) copy-start(bf16[1,64,4,4,128]{4,3,2,1,0:T(4,128)(2,1)} %param.3) | copy-start | bytes 786436
  2.8 18.6 %collective-permute-start.2 = (bf16[64,1024]{1,0:T(8,128)(2,1)S(1)}, bf16[64,1024]{1,0:T(8,128)(2,1)S(1)}, u32[]{:S(2)}, u32[]{:S(2)}) collective-permute-start(bf16[64,1024]{1,0:T(8,128)(2,1)S(1)} %pad_maximum_fusion.2), channel_id=1, source_target_pairs={{0,1},{1,2},{2,3},{3,4},{4,5},{5,6},{6,7},{7,8},{8,9},{9,10},{10,1... | collective-permute-start | bytes 393224 | tf_op jit(solution)/shard_map/ppermute | solution.py:228
  4.2 17.3 %collective-permute-start = (bf16[64,1152]{1,0:T(8,128)(2,1)S(1)}, bf16[64,1152]{1,0:T(8,128)(2,1)S(1)}, u32[]{:S(2)}, u32[]{:S(2)}) collective-permute-start(bf16[64,1152]{1,0:T(8,128)(2,1)S(1)} %pad_maximum_fusion), channel_id=1, source_target_pairs={{0,16},{16,32},{32,48},{1,17},{17,33},{33,49},{2,18},{18,34},{34,5... | collective-permute-start | bytes 442376 | tf_op jit(solution)/shard_map/ppermute | solution.py:213
  8.1 2.3 %copy-start.1 = (bf16[64,1728]{1,0:T(8,128)(2,1)S(1)}, bf16[64,1728]{1,0:T(8,128)(2,1)}, u32[]{:S(2)}) copy-start(bf16[64,1728]{1,0:T(8,128)(2,1)} %param.5) | copy-start | bytes 663556
  8.1 13.3 %collective-permute-start.1 = (bf16[64,1152]{1,0:T(8,128)(2,1)S(1)}, bf16[64,1152]{1,0:T(8,128)(2,1)S(1)}, u32[]{:S(2)}, u32[]{:S(2)}) collective-permute-start(bf16[64,1152]{1,0:T(8,128)(2,1)S(1)} %pad_maximum_fusion.1), channel_id=1, source_target_pairs={{16,0},{32,16},{48,32},{17,1},{33,17},{49,33},{18,2},{34,18},{50,3... | collective-permute-start | bytes 442376 | tf_op jit(solution)/shard_map/ppermute | solution.py:213
  23.3 24.2 %copy-start.2 = (bf16[64,512]{1,0:T(8,128)(2,1)S(1)}, bf16[64,512]{1,0:T(8,128)(2,1)}, u32[]{:S(2)}) copy-start(bf16[64,512]{1,0:T(8,128)(2,1)} %get-tuple-element.46) | copy-start | bytes 196612
  23.3 35.3 %all-to-all-start = ((f32[32,8,512]{2,1,0:T(8,128)}), f32[32,8,512]{2,1,0:T(8,128)S(1)}, u32[]{:S(2)}, u32[]{:S(2)}) async-start(f32[32,8,512]{2,1,0:T(8,128)} %shard_map.51), calls=%async_computation | async-start | bytes 1048576 | tf_op jit(solution)/shard_map/all_to_all | solution.py:258
  47.4 31.5 %collective-permute-start.3 = (bf16[64,512]{1,0:T(8,128)(2,1)S(1)}, bf16[64,512]{1,0:T(8,128)(2,1)S(1)}, u32[]{:S(2)}, u32[]{:S(2)}) collective-permute-start(bf16[64,512]{1,0:T(8,128)(2,1)S(1)} %copy-done.2), channel_id=1, source_target_pairs={{1,0},{2,1},{3,2},{4,3},{5,4},{6,5},{7,6},{8,7},{9,8},{10,9},{11,1... | collective-permute-start | bytes 196616 | tf_op jit(solution)/shard_map/ppermute | solution.py:228
  59.3 34.3 %all-to-all-start.1 = ((f32[32,4,128]{2,1,0:T(4,128)}), f32[32,4,128]{2,1,0:T(4,128)S(1)}, u32[]{:S(2)}, u32[]{:S(2)}) async-start(f32[32,4,128]{2,1,0:T(4,128)} %bitcast.4), calls=%async_computation.1 | async-start | bytes 131072 | tf_op jit(solution)/shard_map/all_to_all | solution.py:263
  79.0 4.8 %collective-permute-start.4 = (bf16[64,256]{1,0:T(8,128)(2,1)S(1)}, bf16[64,256]{1,0:T(8,128)(2,1)S(1)}, u32[]{:S(2)}, u32[]{:S(2)}) collective-permute-start(bf16[64,256]{1,0:T(8,128)(2,1)S(1)} %pad_maximum_fusion.5), channel_id=1, source_target_pairs={{0,16},{16,32},{32,48},{1,17},{17,33},{33,49},{2,18},{18,34},{34,5... | collective-permute-start | bytes 98312 | tf_op jit(solution)/shard_map/ppermute | solution.py:213
  82.3 5.0 %collective-permute-start.5 = (bf16[64,256]{1,0:T(8,128)(2,1)S(1)}, bf16[64,256]{1,0:T(8,128)(2,1)S(1)}, u32[]{:S(2)}, u32[]{:S(2)}) collective-permute-start(bf16[64,256]{1,0:T(8,128)(2,1)S(1)} %pad_maximum_fusion.6), channel_id=1, source_target_pairs={{16,0},{32,16},{48,32},{17,1},{33,17},{49,33},{18,2},{34,18},{50,3... | collective-permute-start | bytes 98312 | tf_op jit(solution)/shard_map/ppermute | solution.py:213
  94.3 12.4 %all-to-all-start.2 = ((f32[16,4,128]{2,1,0:T(4,128)}), f32[16,4,128]{2,1,0:T(4,128)S(1)}, u32[]{:S(2)}, u32[]{:S(2)}) async-start(f32[16,4,128]{2,1,0:T(4,128)} %broadcast_in_dim.12), calls=%async_computation.2 | async-start | bytes 65536 | tf_op jit(solution)/shard_map/all_to_all | solution.py:273

commit v8 on v5

--- a/solution.py
+++ b/solution.py
@@ -267,9 +267,9 @@
     last = (NX - 1) * LANES
     corner_below = shifted_by(jnp.concatenate([low[:, last:], high[:, last:]], axis=1), "px", 1)
     corner_above = shifted_by(jnp.concatenate([plane(low, 0), plane(high, 0)], axis=1), "px", -1)
+    mine = jnp.sum(parts, axis=0)
+    mine, g = lax.optimization_barrier((mine, g))
     grad_input = run_input(g, weights, below, above, low, high, corner_below, corner_above)
-    parts, grad_input = lax.optimization_barrier((parts, grad_input))
-    mine = jnp.sum(parts, axis=0)
     parts = lax.all_to_all(jnp.broadcast_to(mine, (16, 4, LANES)), ("px", "y"), 0, 0)
     whole = parts.reshape(4, 16 * LANES)[:, : 9 * ROWS]
     total = 16 * 16 * 64 * 128

time: 108 us -> 104 us (0.963)
  waiting for transfers between devices: 20.6 us -> 17.2 us
    ppermute x4, waiting for transfers between devices: 5.63 us -> 3.28 us  [shifted_by(): return lax.ppermute(x, axis, pairs)]
    all_to_all x1, waiting for transfers between devices: 5.37 us -> 4.28 us  [local(): lax.all_to_all(jnp.broadcast_to(mine, (16, 4, LANES)), ('px', 'y'), 0, 0)]
  transfers between devices with their start and end apart: 9 -> 9, of which waited for: 4 -> 3; matrix products, arithmetic and copies ran while one was open for 2% -> 3% of each run, Pallas kernels for 2% -> 2%
where the time goes in v8:
time: 104 us
  starting transfers between devices  76.2 us (73%)
  waiting for transfers between devices  17.2 us (17%)
  local copies, waits for them, and re-layouts  4.16 us (4%)
  Pallas kernels  3.6 us (3%)
  other arithmetic  1.46 us (1%)
    all_to_all x1, starting transfers between devices, local(): lax.all_to_all(jnp.broadcast_to(mine.reshape(1, 8, 4, LANES), (4, 8, 4, L...  25.2 us
    ppermute x2, starting transfers between devices, along_y(): return lax.ppermute(x, ('core', 'y', 'zhi'), pairs)  17 us
    all_to_all x1, starting transfers between devices, local(): parts = lax.all_to_all(message, ('core', 'px', 'y'), 0, 0)  15.4 us
    ppermute x4, starting transfers between devices, shifted_by(): return lax.ppermute(x, axis, pairs)  11.8 us
    all_to_all x1, waiting for transfers between devices, local(): parts = lax.all_to_all(message, ('core', 'px', 'y'), 0, 0)  9.64 us
    all_to_all x1, starting transfers between devices, local(): lax.all_to_all(jnp.broadcast_to(mine, (16, 4, LANES)), ('px', 'y'), 0, 0)  6.67 us
    all_to_all x1, waiting for transfers between devices, local(): lax.all_to_all(jnp.broadcast_to(mine, (16, 4, LANES)), ('px', 'y'), 0, 0)  4.28 us
    ppermute x4, waiting for transfers between devices, shifted_by(): return lax.ppermute(x, axis, pairs)  3.28 us
  transfers between devices with their start and end apart: 9, of which 3 were waited for; matrix products, arithmetic and copies ran while one was open for 3% of the time, Pallas kernels for 2%

profile of v8, /device:TPU:2, one launch (start us, length us, event | category | flops | bytes accessed | tf_op | source)
XLA Modules:
  0.0 103.5 jit_solution(65185291121568196)
XLA Ops:
  0.6 0.0 copy-start
  0.6 1.2 %reshape.31.g_ref = bf16[64,2048]{1,0:T(8,128)(2,1)S(1)} reshape(bf16[1,64,4,4,128]{4,3,2,1,0:T(4,128)(2,1)} %param.4) | data formatting | bytes 524288 | tf_op jit(solution)/shard_map/reshape | solution.py:233
  1.9 0.0 copy-done
  1.9 0.2 reshape.34.a_ref
  2.1 0.7 broadcast_select_fusion.2
  2.8 15.7 %collective-permute-start.2 = (bf16[64,1024]{1,0:T(8,128)(2,1)S(1)}, bf16[64,1024]{1,0:T(8,128)(2,1)S(1)}, u32[]{:S(2)}, u32[]{:S(2)}) collective-permute-start(bf16[64,1024]{1,0:T(8,128)(2,1)S(1)} %pad_maximum_fusion.2), channel_id=1, source_target_pairs={{0,1},{1,2},{2,3},{3,4},{4,5},{5,6},{6,7},{7,8},{8,9},{9,10},{10,1... | collective-permute-start | bytes 393224 | tf_op jit(solution)/shard_map/ppermute | solution.py:228
  18.6 3.4 %collective-permute-start = (bf16[64,1152]{1,0:T(8,128)(2,1)S(1)}, bf16[64,1152]{1,0:T(8,128)(2,1)S(1)}, u32[]{:S(2)}, u32[]{:S(2)}) collective-permute-start(bf16[64,1152]{1,0:T(8,128)(2,1)S(1)} %pad_maximum_fusion), channel_id=1, source_target_pairs={{0,16},{16,32},{32,48},{1,17},{17,33},{33,49},{2,18},{18,34},{34,5... | collective-permute-start | bytes 442376 | tf_op jit(solution)/shard_map/ppermute | solution.py:213
  22.0 0.0 copy-start.1
  22.0 2.6 %collective-permute-start.1 = (bf16[64,1152]{1,0:T(8,128)(2,1)S(1)}, bf16[64,1152]{1,0:T(8,128)(2,1)S(1)}, u32[]{:S(2)}, u32[]{:S(2)}) collective-permute-start(bf16[64,1152]{1,0:T(8,128)(2,1)S(1)} %pad_maximum_fusion.1), channel_id=1, source_target_pairs={{16,0},{32,16},{48,32},{17,1},{33,17},{49,33},{18,2},{34,18},{50,3... | collective-permute-start | bytes 442376 | tf_op jit(solution)/shard_map/ppermute | solution.py:213
  24.6 0.9 shard_map.50
  25.5 0.0 copy-done.1
  25.5 0.3 reshape.32
  25.9 0.0 collective-permute-done.2.far_ref
  25.9 0.0 collective-permute-done.below_ref
  25.9 3.3 %collective-permute-done.1.above_ref = bf16[64,1152]{1,0:T(8,128)(2,1)S(1)} collective-permute-done((bf16[64,1152]{1,0:T(8,128)(2,1)S(1)}, bf16[64,1152]{1,0:T(8,128)(2,1)S(1)}, u32[]{:S(2)}, u32[]{:S(2)}) %collective-permute-start.1) | collective-permute-done | bytes 147488 | tf_op jit(solution)/shard_map/ppermute | solution.py:213
  29.2 1.8 %shard_map.51 = f32[32,8,512]{2,1,0:T(8,128)} custom-call(s32[1]{0:T(128)} %bitcast.core_ref, bf16[64,2048]{1,0:T(8,128)(2,1)S(1)} %reshape.31.g_ref, f32[576,192]{1,0:T(8,128)S(1)} %get-tuple-element.16.gk_ref, bf16[192,1024]{1,0:T(8,128)(2,1)S(1)} %get-tuple-element.17.row_ref, bf16[192,1024]{1,0:T(8,128)(2,1)S(1)} %get-tuple-element.18.column_ref, ...), custom_call_target="tpu_custom_call" | custom-call | tf_op jit(solution)/shard_map/pallas_call | solution.py:193
  31.0 0.0 copy-start.2
  31.0 15.4 %all-to-all-start = ((f32[32,8,512]{2,1,0:T(8,128)}), f32[32,8,512]{2,1,0:T(8,128)S(1)}, u32[]{:S(2)}, u32[]{:S(2)}) async-start(f32[32,8,512]{2,1,0:T(8,128)} %shard_map.51), calls=%async_computation | async-start | bytes 1048576 | tf_op jit(solution)/shard_map/all_to_all | solution.py:258
  46.5 0.0 copy-done.2
  46.5 1.3 %collective-permute-start.3 = (bf16[64,512]{1,0:T(8,128)(2,1)S(1)}, bf16[64,512]{1,0:T(8,128)(2,1)S(1)}, u32[]{:S(2)}, u32[]{:S(2)}) collective-permute-start(bf16[64,512]{1,0:T(8,128)(2,1)S(1)} %copy-done.2), channel_id=1, source_target_pairs={{1,0},{2,1},{3,2},{4,3},{5,4},{6,5},{7,6},{8,7},{9,8},{10,9},{11,1... | collective-permute-start | bytes 196616 | tf_op jit(solution)/shard_map/ppermute | solution.py:228
  47.8 9.6 %all-to-all-done = f32[32,8,512]{2,1,0:T(8,128)S(1)} async-done(((f32[32,8,512]{2,1,0:T(8,128)}), f32[32,8,512]{2,1,0:T(8,128)S(1)}, u32[]{:S(2)}, u32[]{:S(2)}) %all-to-all-start) | async-done | bytes 524320 | tf_op jit(solution)/shard_map/all_to_all | solution.py:258
  57.5 0.6 broadcast_in_dim.11
  58.1 25.2 %all-to-all-start.1 = ((f32[32,4,128]{2,1,0:T(4,128)}), f32[32,4,128]{2,1,0:T(4,128)S(1)}, u32[]{:S(2)}, u32[]{:S(2)}) async-start(f32[32,4,128]{2,1,0:T(4,128)} %bitcast.3), calls=%async_computation.1 | async-start | bytes 131072 | tf_op jit(solution)/shard_map/all_to_all | solution.py:263
  83.3 0.0 collective-permute-done.3
  83.4 2.6 %collective-permute-start.4 = (bf16[64,256]{1,0:T(8,128)(2,1)S(1)}, bf16[64,256]{1,0:T(8,128)(2,1)S(1)}, u32[]{:S(2)}, u32[]{:S(2)}) collective-permute-start(bf16[64,256]{1,0:T(8,128)(2,1)S(1)} %pad_maximum_fusion.5), channel_id=1, source_target_pairs={{0,16},{16,32},{32,48},{1,17},{17,33},{33,49},{2,18},{18,34},{34,5... | collective-permute-start | bytes 98312 | tf_op jit(solution)/shard_map/ppermute | solution.py:213
  86.0 3.3 %collective-permute-start.5 = (bf16[64,256]{1,0:T(8,128)(2,1)S(1)}, bf16[64,256]{1,0:T(8,128)(2,1)S(1)}, u32[]{:S(2)}, u32[]{:S(2)}) collective-permute-start(bf16[64,256]{1,0:T(8,128)(2,1)S(1)} %pad_maximum_fusion.6), channel_id=1, source_target_pairs={{16,0},{32,16},{48,32},{17,1},{33,17},{49,33},{18,2},{34,18},{50,3... | collective-permute-start | bytes 98312 | tf_op jit(solution)/shard_map/ppermute | solution.py:213
  89.3 0.0 all-to-all-done.1
  89.3 0.6 broadcast_in_dim.12
  90.0 6.7 %all-to-all-start.2 = ((f32[16,4,128]{2,1,0:T(4,128)}), f32[16,4,128]{2,1,0:T(4,128)S(1)}, u32[]{:S(2)}, u32[]{:S(2)}) async-start(f32[16,4,128]{2,1,0:T(4,128)} %broadcast_in_dim.12), calls=%async_computation.2 | async-start | bytes 65536 | tf_op jit(solution)/shard_map/all_to_all | solution.py:273
  96.6 0.2 copy.14.w_ref
  96.8 0.0 collective-permute-done.4.corner_below_ref
  96.8 0.0 collective-permute-done.5.corner_above_ref
  96.8 0.9 shard_map.52
  97.7 0.9 reshape.36
  98.6 4.3 %all-to-all-done.2 = f32[16,4,128]{2,1,0:T(4,128)S(1)} async-done(((f32[16,4,128]{2,1,0:T(4,128)}), f32[16,4,128]{2,1,0:T(4,128)S(1)}, u32[]{:S(2)}, u32[]{:S(2)}) %all-to-all-start.2) | async-done | bytes 32800 | tf_op jit(solution)/shard_map/all_to_all | solution.py:273
  102.9 0.6 slice_multiply_fusion
  (17 shorter events, 0.3 us)
Async XLA Ops:
  0.6 1.2 %copy-start = (bf16[1,64,4,4,128]{4,3,2,1,0:T(4,128)(2,1)S(1)}, bf16[1,64,4,4,128]{4,3,2,1,0:T(4,128)(2,1)}, u32[]{:S(2)}) copy-start(bf16[1,64,4,4,128]{4,3,2,1,0:T(4,128)(2,1)} %param.3) | copy-start | bytes 786436
  2.8 23.1 %collective-permute-start.2 = (bf16[64,1024]{1,0:T(8,128)(2,1)S(1)}, bf16[64,1024]{1,0:T(8,128)(2,1)S(1)}, u32[]{:S(2)}, u32[]{:S(2)}) collective-permute-start(bf16[64,1024]{1,0:T(8,128)(2,1)S(1)} %pad_maximum_fusion.2), channel_id=1, source_target_pairs={{0,1},{1,2},{2,3},{3,4},{4,5},{5,6},{6,7},{7,8},{8,9},{9,10},{10,1... | collective-permute-start | bytes 393224 | tf_op jit(solution)/shard_map/ppermute | solution.py:228
  18.6 7.3 %collective-permute-start = (bf16[64,1152]{1,0:T(8,128)(2,1)S(1)}, bf16[64,1152]{1,0:T(8,128)(2,1)S(1)}, u32[]{:S(2)}, u32[]{:S(2)}) collective-permute-start(bf16[64,1152]{1,0:T(8,128)(2,1)S(1)} %pad_maximum_fusion), channel_id=1, source_target_pairs={{0,16},{16,32},{32,48},{1,17},{17,33},{33,49},{2,18},{18,34},{34,5... | collective-permute-start | bytes 442376 | tf_op jit(solution)/shard_map/ppermute | solution.py:213
  22.0 3.5 %copy-start.1 = (bf16[64,1728]{1,0:T(8,128)(2,1)S(1)}, bf16[64,1728]{1,0:T(8,128)(2,1)}, u32[]{:S(2)}) copy-start(bf16[64,1728]{1,0:T(8,128)(2,1)} %param.5) | copy-start | bytes 663556
  22.0 7.2 %collective-permute-start.1 = (bf16[64,1152]{1,0:T(8,128)(2,1)S(1)}, bf16[64,1152]{1,0:T(8,128)(2,1)S(1)}, u32[]{:S(2)}, u32[]{:S(2)}) collective-permute-start(bf16[64,1152]{1,0:T(8,128)(2,1)S(1)} %pad_maximum_fusion.1), channel_id=1, source_target_pairs={{16,0},{32,16},{48,32},{17,1},{33,17},{49,33},{18,2},{34,18},{50,3... | collective-permute-start | bytes 442376 | tf_op jit(solution)/shard_map/ppermute | solution.py:213
  31.0 15.4 %copy-start.2 = (bf16[64,512]{1,0:T(8,128)(2,1)S(1)}, bf16[64,512]{1,0:T(8,128)(2,1)}, u32[]{:S(2)}) copy-start(bf16[64,512]{1,0:T(8,128)(2,1)} %get-tuple-element.46) | copy-start | bytes 196612
  31.0 26.4 %all-to-all-start = ((f32[32,8,512]{2,1,0:T(8,128)}), f32[32,8,512]{2,1,0:T(8,128)S(1)}, u32[]{:S(2)}, u32[]{:S(2)}) async-start(f32[32,8,512]{2,1,0:T(8,128)} %shard_map.51), calls=%async_computation | async-start | bytes 1048576 | tf_op jit(solution)/shard_map/all_to_all | solution.py:258
  46.5 36.9 %collective-permute-start.3 = (bf16[64,512]{1,0:T(8,128)(2,1)S(1)}, bf16[64,512]{1,0:T(8,128)(2,1)S(1)}, u32[]{:S(2)}, u32[]{:S(2)}) collective-permute-start(bf16[64,512]{1,0:T(8,128)(2,1)S(1)} %copy-done.2), channel_id=1, source_target_pairs={{1,0},{2,1},{3,2},{4,3},{5,4},{6,5},{7,6},{8,7},{9,8},{10,9},{11,1... | collective-permute-start | bytes 196616 | tf_op jit(solution)/shard_map/ppermute | solution.py:228
  58.1 31.2 %all-to-all-start.1 = ((f32[32,4,128]{2,1,0:T(4,128)}), f32[32,4,128]{2,1,0:T(4,128)S(1)}, u32[]{:S(2)}, u32[]{:S(2)}) async-start(f32[32,4,128]{2,1,0:T(4,128)} %bitcast.3), calls=%async_computation.1 | async-start | bytes 131072 | tf_op jit(solution)/shard_map/all_to_all | solution.py:263
  83.4 13.4 %collective-permute-start.4 = (bf16[64,256]{1,0:T(8,128)(2,1)S(1)}, bf16[64,256]{1,0:T(8,128)(2,1)S(1)}, u32[]{:S(2)}, u32[]{:S(2)}) collective-permute-start(bf16[64,256]{1,0:T(8,128)(2,1)S(1)} %pad_maximum_fusion.5), channel_id=1, source_target_pairs={{0,16},{16,32},{32,48},{1,17},{17,33},{33,49},{2,18},{18,34},{34,5... | collective-permute-start | bytes 98312 | tf_op jit(solution)/shard_map/ppermute | solution.py:213
  86.0 10.8 %collective-permute-start.5 = (bf16[64,256]{1,0:T(8,128)(2,1)S(1)}, bf16[64,256]{1,0:T(8,128)(2,1)S(1)}, u32[]{:S(2)}, u32[]{:S(2)}) collective-permute-start(bf16[64,256]{1,0:T(8,128)(2,1)S(1)} %pad_maximum_fusion.6), channel_id=1, source_target_pairs={{16,0},{32,16},{48,32},{17,1},{33,17},{49,33},{18,2},{34,18},{50,3... | collective-permute-start | bytes 98312 | tf_op jit(solution)/shard_map/ppermute | solution.py:213
  90.0 12.9 %all-to-all-start.2 = ((f32[16,4,128]{2,1,0:T(4,128)}), f32[16,4,128]{2,1,0:T(4,128)S(1)}, u32[]{:S(2)}, u32[]{:S(2)}) async-start(f32[16,4,128]{2,1,0:T(4,128)} %broadcast_in_dim.12), calls=%async_computation.2 | async-start | bytes 65536 | tf_op jit(solution)/shard_map/all_to_all | solution.py:273

commit v9 on v8

--- a/solution.py
+++ b/solution.py
@@ -203,6 +203,32 @@
     )(core.reshape(1), *operands)
 
 
+def rows_kernel(core_ref, g_ref, a_ref, ahead_ref, behind_ref, last_ref, first_ref):
+    upward = core_ref[0] == 0
+    for x in range(NX):
+        low, high = (x * NY, x * NY + NY - 1)
+        lanes = slice(x * LANES, (x + 1) * LANES)
+        ahead_ref[:, lanes] = jnp.where(upward, plane(g_ref, high), plane(g_ref, low))
+        behind_ref[:, lanes] = jnp.where(upward, plane(g_ref, low), plane(g_ref, high))
+        lanes = slice(HALF + x * LANES, HALF + (x + 1) * LANES)
+        ahead_ref[:, lanes] = jnp.where(upward, plane(a_ref, high), plane(a_ref, low))
+    size = NY * LANES
+    for x, out_ref in ((NX - 1, last_ref), (0, first_ref)):
+        out_ref[:, 0:size] = g_ref[:, x * size : (x + 1) * size]
+        out_ref[:, size : size + LANES] = plane(a_ref, x * NY)
+        out_ref[:, size + LANES : size + 2 * LANES] = plane(a_ref, x * NY + NY - 1)
+
+
+def run_rows(core, *operands):
+    vmem = pl.BlockSpec(memory_space=pltpu.VMEM)
+    return call(
+        rows_kernel,
+        tuple(jax.ShapeDtypeStruct((CH, n * LANES), BF16) for n in (2 * NX, NX, 6, 6)),
+        in_specs=[pl.BlockSpec(memory_space=pltpu.SMEM), vmem, vmem],
+        out_specs=(vmem,) * 4,
+    )(core.reshape(1), *operands)
+
+
 def run_input(*operands):
     return call(input_kernel, jax.ShapeDtypeStruct((CH, CELLS), BF16))(*operands)
 
@@ -233,24 +259,15 @@
     g = grad_out.reshape(CH, CELLS)
     a = activations.reshape(CH, CELLS)
 
-    def rows(cells, y):
-        return jnp.concatenate([plane(cells, x * NY + y) for x in range(NX)], axis=1)
-
-    g_low, g_high = rows(g, 0), rows(g, NY - 1)
-    ahead = jnp.where(core == 0, g_high, g_low)
-    ahead = jnp.concatenate([ahead, jnp.where(core == 0, rows(a, NY - 1), rows(a, 0))], axis=1)
+    ahead, behind, last_face, first_face = run_rows(core, g, a)
     far = along_y(ahead, 1)
-    back = along_y(jnp.where(core == 0, g_low, g_high), -1)
+    back = along_y(behind, -1)
 
 
     weights = kernel.reshape(CH, 3, 3, ROWS).transpose(3, 2, 1, 0).reshape(ROWS, 3 * ROWS)
 
-    def x_face(x):
-        cells = g[:, x * NY * LANES : (x + 1) * NY * LANES]
-        return jnp.concatenate([cells, plane(a, x * NY), plane(a, x * NY + NY - 1), cells[:, LANES:]], axis=1)
-
-    below = shifted_by(x_face(NX - 1), "px", 1)
-    above = shifted_by(x_face(0), "px", -1)
+    below = shifted_by(last_face, "px", 1)
+    above = shifted_by(first_face, "px", -1)
     inner = run_inner(g, a)
     weights, *inner = lax.optimization_barrier((weights, *inner))
     message = run_message(core, g, *inner, below, above, far)

time: 104 us -> 103 us (level)
  no operation moved by 1% of the time
where the time goes in v9:
time: 103 us
  starting transfers between devices  76.6 us (74%)
  waiting for transfers between devices  16.7 us (16%)
  local copies, waits for them, and re-layouts  4.09 us (4%)
  Pallas kernels  3.66 us (4%)
    all_to_all x1, starting transfers between devices, local(): lax.all_to_all(jnp.broadcast_to(mine.reshape(1, 8, 4, LANES), (4, 8, 4, L...  25.2 us
    ppermute x2, starting transfers between devices, along_y(): return lax.ppermute(x, ('core', 'y', 'zhi'), pairs)  17 us
    all_to_all x1, starting transfers between devices, local(): parts = lax.all_to_all(message, ('core', 'px', 'y'), 0, 0)  15.9 us
    ppermute x4, starting transfers between devices, shifted_by(): return lax.ppermute(x, axis, pairs)  11.8 us
    all_to_all x1, waiting for transfers between devices, local(): parts = lax.all_to_all(message, ('core', 'px', 'y'), 0, 0)  9.64 us
    all_to_all x1, starting transfers between devices, local(): lax.all_to_all(jnp.broadcast_to(mine, (16, 4, LANES)), ('px', 'y'), 0, 0)  6.66 us
    all_to_all x1, waiting for transfers between devices, local(): lax.all_to_all(jnp.broadcast_to(mine, (16, 4, LANES)), ('px', 'y'), 0, 0)  4.28 us
    ppermute x4, waiting for transfers between devices, shifted_by(): return lax.ppermute(x, axis, pairs)  2.77 us
  transfers between devices with their start and end apart: 9, of which 3 were waited for; matrix products, arithmetic and copies ran while one was open for 3% of the time, Pallas kernels for 2%

profile of v9, /device:TPU:2, one launch (start us, length us, event | category | flops | bytes accessed | tf_op | source)
XLA Modules:
  0.0 102.7 jit_solution(2976076978133861617)
XLA Ops:
  0.6 0.0 copy-start
  0.6 1.2 %reshape.32.g_ref = bf16[64,2048]{1,0:T(8,128)(2,1)S(1)} reshape(bf16[1,64,4,4,128]{4,3,2,1,0:T(4,128)(2,1)} %param.4) | data formatting | bytes 524288 | tf_op jit(solution)/shard_map/reshape | solution.py:259
  1.8 0.0 copy-done
  1.8 0.2 reshape.35.a_ref
  2.0 0.1 shard_map.51
  2.1 15.7 %collective-permute-start.2 = (bf16[64,1024]{1,0:T(8,128)(2,1)S(1)}, bf16[64,1024]{1,0:T(8,128)(2,1)S(1)}, u32[]{:S(2)}, u32[]{:S(2)}) collective-permute-start(bf16[64,1024]{1,0:T(8,128)(2,1)S(1)} %get-tuple-element.25), channel_id=1, source_target_pairs={{0,1},{1,2},{2,3},{3,4},{4,5},{5,6},{6,7},{7,8},{8,9},{9,10},{10,1... | collective-permute-start | bytes 393224 | tf_op jit(solution)/shard_map/ppermute | solution.py:254
  17.8 3.4 %collective-permute-start = (bf16[64,768]{1,0:T(8,128)(2,1)S(1)}, bf16[64,768]{1,0:T(8,128)(2,1)S(1)}, u32[]{:S(2)}, u32[]{:S(2)}) collective-permute-start(bf16[64,768]{1,0:T(8,128)(2,1)S(1)} %get-tuple-element.23), channel_id=1, source_target_pairs={{0,16},{16,32},{32,48},{1,17},{17,33},{33,49},{2,18},{18,34},{34,5... | collective-permute-start | bytes 294920 | tf_op jit(solution)/shard_map/ppermute | solution.py:239
  21.2 0.0 copy-start.1
  21.2 2.6 %collective-permute-start.1 = (bf16[64,768]{1,0:T(8,128)(2,1)S(1)}, bf16[64,768]{1,0:T(8,128)(2,1)S(1)}, u32[]{:S(2)}, u32[]{:S(2)}) collective-permute-start(bf16[64,768]{1,0:T(8,128)(2,1)S(1)} %get-tuple-element.24), channel_id=1, source_target_pairs={{16,0},{32,16},{48,32},{17,1},{33,17},{49,33},{18,2},{34,18},{50,3... | collective-permute-start | bytes 294920 | tf_op jit(solution)/shard_map/ppermute | solution.py:239
  23.8 0.9 shard_map.50
  24.7 0.0 copy-done.1
  24.7 0.3 reshape.33
  25.1 0.0 collective-permute-done.below_ref
  25.1 2.8 %collective-permute-done.1.above_ref = bf16[64,768]{1,0:T(8,128)(2,1)S(1)} collective-permute-done((bf16[64,768]{1,0:T(8,128)(2,1)S(1)}, bf16[64,768]{1,0:T(8,128)(2,1)S(1)}, u32[]{:S(2)}, u32[]{:S(2)}) %collective-permute-start.1) | collective-permute-done | bytes 98336 | tf_op jit(solution)/shard_map/ppermute | solution.py:239
  27.9 0.0 collective-permute-done.2.far_ref
  27.9 1.8 %shard_map.52 = f32[32,8,512]{2,1,0:T(8,128)} custom-call(s32[1]{0:T(128)} %bitcast.core_ref, bf16[64,2048]{1,0:T(8,128)(2,1)S(1)} %reshape.32.g_ref, f32[576,192]{1,0:T(8,128)S(1)} %get-tuple-element.20.gk_ref, bf16[192,1024]{1,0:T(8,128)(2,1)S(1)} %get-tuple-element.21.row_ref, bf16[192,1024]{1,0:T(8,128)(2,1)S(1)} %get-tuple-element.22.column_ref, ...), custom_call_target="tpu_custom_call" | custom-call | tf_op jit(solution)/shard_map/pallas_call | solution.py:193
  29.7 15.9 %all-to-all-start = ((f32[32,8,512]{2,1,0:T(8,128)}), f32[32,8,512]{2,1,0:T(8,128)S(1)}, u32[]{:S(2)}, u32[]{:S(2)}) async-start(f32[32,8,512]{2,1,0:T(8,128)} %shard_map.52), calls=%async_computation | async-start | bytes 1048576 | tf_op jit(solution)/shard_map/all_to_all | solution.py:275
  45.6 1.3 %collective-permute-start.3 = (bf16[64,512]{1,0:T(8,128)(2,1)S(1)}, bf16[64,512]{1,0:T(8,128)(2,1)S(1)}, u32[]{:S(2)}, u32[]{:S(2)}) collective-permute-start(bf16[64,512]{1,0:T(8,128)(2,1)S(1)} %get-tuple-element.30), channel_id=1, source_target_pairs={{1,0},{2,1},{3,2},{4,3},{5,4},{6,5},{7,6},{8,7},{9,8},{10,9},{11,1... | collective-permute-start | bytes 196616 | tf_op jit(solution)/shard_map/ppermute | solution.py:254
  46.9 9.6 %all-to-all-done = f32[32,8,512]{2,1,0:T(8,128)S(1)} async-done(((f32[32,8,512]{2,1,0:T(8,128)}), f32[32,8,512]{2,1,0:T(8,128)S(1)}, u32[]{:S(2)}, u32[]{:S(2)}) %all-to-all-start) | async-done | bytes 524320 | tf_op jit(solution)/shard_map/all_to_all | solution.py:275
  56.6 0.6 broadcast_in_dim.11
  57.3 25.2 %all-to-all-start.1 = ((f32[32,4,128]{2,1,0:T(4,128)}), f32[32,4,128]{2,1,0:T(4,128)S(1)}, u32[]{:S(2)}, u32[]{:S(2)}) async-start(f32[32,4,128]{2,1,0:T(4,128)} %bitcast.3), calls=%async_computation.1 | async-start | bytes 131072 | tf_op jit(solution)/shard_map/all_to_all | solution.py:280
  82.5 0.0 collective-permute-done.3
  82.6 3.2 %collective-permute-start.5 = (bf16[64,256]{1,0:T(8,128)(2,1)S(1)}, bf16[64,256]{1,0:T(8,128)(2,1)S(1)}, u32[]{:S(2)}, u32[]{:S(2)}) collective-permute-start(bf16[64,256]{1,0:T(8,128)(2,1)S(1)} %pad_maximum_fusion.1), channel_id=1, source_target_pairs={{16,0},{32,16},{48,32},{17,1},{33,17},{49,33},{18,2},{34,18},{50,3... | collective-permute-start | bytes 98312 | tf_op jit(solution)/shard_map/ppermute | solution.py:239
  85.8 2.7 %collective-permute-start.4 = (bf16[64,256]{1,0:T(8,128)(2,1)S(1)}, bf16[64,256]{1,0:T(8,128)(2,1)S(1)}, u32[]{:S(2)}, u32[]{:S(2)}) collective-permute-start(bf16[64,256]{1,0:T(8,128)(2,1)S(1)} %pad_maximum_fusion), channel_id=1, source_target_pairs={{0,16},{16,32},{32,48},{1,17},{17,33},{33,49},{2,18},{18,34},{34,5... | collective-permute-start | bytes 98312 | tf_op jit(solution)/shard_map/ppermute | solution.py:239
  88.5 0.0 all-to-all-done.1
  88.5 0.6 broadcast_in_dim.12
  89.1 6.7 %all-to-all-start.2 = ((f32[16,4,128]{2,1,0:T(4,128)}), f32[16,4,128]{2,1,0:T(4,128)S(1)}, u32[]{:S(2)}, u32[]{:S(2)}) async-start(f32[16,4,128]{2,1,0:T(4,128)} %broadcast_in_dim.12), calls=%async_computation.2 | async-start | bytes 65536 | tf_op jit(solution)/shard_map/all_to_all | solution.py:290
  95.8 0.2 copy.14.w_ref
  96.0 0.0 collective-permute-done.5.corner_above_ref
  96.0 0.0 collective-permute-done.4.corner_below_ref
  96.0 0.9 shard_map.53
  96.9 0.9 reshape.37
  97.8 4.3 %all-to-all-done.2 = f32[16,4,128]{2,1,0:T(4,128)S(1)} async-done(((f32[16,4,128]{2,1,0:T(4,128)}), f32[16,4,128]{2,1,0:T(4,128)S(1)}, u32[]{:S(2)}, u32[]{:S(2)}) %all-to-all-start.2) | async-done | bytes 32800 | tf_op jit(solution)/shard_map/all_to_all | solution.py:290
  102.1 0.6 slice_multiply_fusion
  (9 shorter events, 0.2 us)
Async XLA Ops:
  0.6 1.2 %copy-start = (bf16[1,64,4,4,128]{4,3,2,1,0:T(4,128)(2,1)S(1)}, bf16[1,64,4,4,128]{4,3,2,1,0:T(4,128)(2,1)}, u32[]{:S(2)}) copy-start(bf16[1,64,4,4,128]{4,3,2,1,0:T(4,128)(2,1)} %param.3) | copy-start | bytes 786436
  2.1 25.8 %collective-permute-start.2 = (bf16[64,1024]{1,0:T(8,128)(2,1)S(1)}, bf16[64,1024]{1,0:T(8,128)(2,1)S(1)}, u32[]{:S(2)}, u32[]{:S(2)}) collective-permute-start(bf16[64,1024]{1,0:T(8,128)(2,1)S(1)} %get-tuple-element.25), channel_id=1, source_target_pairs={{0,1},{1,2},{2,3},{3,4},{4,5},{5,6},{6,7},{7,8},{8,9},{9,10},{10,1... | collective-permute-start | bytes 393224 | tf_op jit(solution)/shard_map/ppermute | solution.py:254
  17.8 7.3 %collective-permute-start = (bf16[64,768]{1,0:T(8,128)(2,1)S(1)}, bf16[64,768]{1,0:T(8,128)(2,1)S(1)}, u32[]{:S(2)}, u32[]{:S(2)}) collective-permute-start(bf16[64,768]{1,0:T(8,128)(2,1)S(1)} %get-tuple-element.23), channel_id=1, source_target_pairs={{0,16},{16,32},{32,48},{1,17},{17,33},{33,49},{2,18},{18,34},{34,5... | collective-permute-start | bytes 294920 | tf_op jit(solution)/shard_map/ppermute | solution.py:239
  21.2 3.5 %copy-start.1 = (bf16[64,1728]{1,0:T(8,128)(2,1)S(1)}, bf16[64,1728]{1,0:T(8,128)(2,1)}, u32[]{:S(2)}) copy-start(bf16[64,1728]{1,0:T(8,128)(2,1)} %param.5) | copy-start | bytes 663556
  21.2 6.6 %collective-permute-start.1 = (bf16[64,768]{1,0:T(8,128)(2,1)S(1)}, bf16[64,768]{1,0:T(8,128)(2,1)S(1)}, u32[]{:S(2)}, u32[]{:S(2)}) collective-permute-start(bf16[64,768]{1,0:T(8,128)(2,1)S(1)} %get-tuple-element.24), channel_id=1, source_target_pairs={{16,0},{32,16},{48,32},{17,1},{33,17},{49,33},{18,2},{34,18},{50,3... | collective-permute-start | bytes 294920 | tf_op jit(solution)/shard_map/ppermute | solution.py:239
  29.7 26.8 %all-to-all-start = ((f32[32,8,512]{2,1,0:T(8,128)}), f32[32,8,512]{2,1,0:T(8,128)S(1)}, u32[]{:S(2)}, u32[]{:S(2)}) async-start(f32[32,8,512]{2,1,0:T(8,128)} %shard_map.52), calls=%async_computation | async-start | bytes 1048576 | tf_op jit(solution)/shard_map/all_to_all | solution.py:275
  45.6 36.9 %collective-permute-start.3 = (bf16[64,512]{1,0:T(8,128)(2,1)S(1)}, bf16[64,512]{1,0:T(8,128)(2,1)S(1)}, u32[]{:S(2)}, u32[]{:S(2)}) collective-permute-start(bf16[64,512]{1,0:T(8,128)(2,1)S(1)} %get-tuple-element.30), channel_id=1, source_target_pairs={{1,0},{2,1},{3,2},{4,3},{5,4},{6,5},{7,6},{8,7},{9,8},{10,9},{11,1... | collective-permute-start | bytes 196616 | tf_op jit(solution)/shard_map/ppermute | solution.py:254
  57.3 31.2 %all-to-all-start.1 = ((f32[32,4,128]{2,1,0:T(4,128)}), f32[32,4,128]{2,1,0:T(4,128)S(1)}, u32[]{:S(2)}, u32[]{:S(2)}) async-start(f32[32,4,128]{2,1,0:T(4,128)} %bitcast.3), calls=%async_computation.1 | async-start | bytes 131072 | tf_op jit(solution)/shard_map/all_to_all | solution.py:280
  82.6 13.4 %collective-permute-start.5 = (bf16[64,256]{1,0:T(8,128)(2,1)S(1)}, bf16[64,256]{1,0:T(8,128)(2,1)S(1)}, u32[]{:S(2)}, u32[]{:S(2)}) collective-permute-start(bf16[64,256]{1,0:T(8,128)(2,1)S(1)} %pad_maximum_fusion.1), channel_id=1, source_target_pairs={{16,0},{32,16},{48,32},{17,1},{33,17},{49,33},{18,2},{34,18},{50,3... | collective-permute-start | bytes 98312 | tf_op jit(solution)/shard_map/ppermute | solution.py:239
  85.8 10.2 %collective-permute-start.4 = (bf16[64,256]{1,0:T(8,128)(2,1)S(1)}, bf16[64,256]{1,0:T(8,128)(2,1)S(1)}, u32[]{:S(2)}, u32[]{:S(2)}) collective-permute-start(bf16[64,256]{1,0:T(8,128)(2,1)S(1)} %pad_maximum_fusion), channel_id=1, source_target_pairs={{0,16},{16,32},{32,48},{1,17},{17,33},{33,49},{2,18},{18,34},{34,5... | collective-permute-start | bytes 98312 | tf_op jit(solution)/shard_map/ppermute | solution.py:239
  89.1 12.9 %all-to-all-start.2 = ((f32[16,4,128]{2,1,0:T(4,128)}), f32[16,4,128]{2,1,0:T(4,128)S(1)}, u32[]{:S(2)}, u32[]{:S(2)}) async-start(f32[16,4,128]{2,1,0:T(4,128)} %broadcast_in_dim.12), calls=%async_computation.2 | async-start | bytes 65536 | tf_op jit(solution)/shard_map/all_to_all | solution.py:290

commit v10 on v9

--- a/solution.py
+++ b/solution.py
@@ -79,8 +79,8 @@
             gk_ref[first:last, :] += terms
 
 
-def message_kernel(
-    core_ref, g_ref, gk_ref, row_ref, column_ref, below_ref, above_ref, far_ref, msg_ref, wide_ref, rim_ref, far3_ref
+def faces_kernel(
+    core_ref, g_ref, gk_ref, row_ref, column_ref, below_ref, above_ref, sum_ref, rim_ref, own_ref
 ):
     upward = core_ref[0] == 0
 
@@ -90,31 +90,40 @@
     rim_ref[:, 0:LANES] = all_shifts(near(plane(below_ref, NY), plane(below_ref, NY + 1)))
     rim_ref[:, LANES : LANES + HALF] = near(row_ref[:, 0:HALF], row_ref[:, HALF : 2 * HALF])
     rim_ref[:, LANES + HALF : WIDE] = all_shifts(near(plane(above_ref, NY), plane(above_ref, NY + 1)))
-    for x in range(NX):
-        far3_ref[:, x * LANES : (x + 1) * LANES] = all_shifts(plane(far_ref, NX + x))
     own = [near(plane(below_ref, 0), plane(below_ref, NY - 1))]
     own += [near(plane(g_ref, x * NY), plane(g_ref, x * NY + NY - 1)) for x in range(NX)]
     own += [near(plane(above_ref, 0), plane(above_ref, NY - 1))]
+    for at, cells in enumerate(own):
+        own_ref[:, at * LANES : (at + 1) * LANES] = cells
+    for b in range(3):
+        rows = [y for y in range(NY) if 0 <= y - (b - 1) < NY]
+        of_g = (rows[0] - (b - 1)) * LANES
+        size = len(rows) * LANES
+        for a, face, side in ((0, above_ref, 1), (1, None, 0), (2, below_ref, 0)):
+            at = b * ROWS + a * CH
+            value = gk_ref[at : at + CH, :]
+            if face is not None:
+                of_a = side * HALF + rows[0] * LANES
+                value += dot_nt(face[:, of_g : of_g + size], column_ref[:, of_a : of_a + size])
+            sum_ref[at : at + CH, :] = value
+
+
+def message_kernel(core_ref, gk_ref, rim_ref, own_ref, far_ref, msg_ref, wide_ref, far3_ref):
+    upward = core_ref[0] == 0
+    for x in range(NX):
+        far3_ref[:, x * LANES : (x + 1) * LANES] = all_shifts(plane(far_ref, NX + x))
 
     def across(a):
+        at = (2 - a) * LANES
         of_far = dot_nt(far_ref[:, 0:HALF], rim_ref[:, a * LANES : a * LANES + HALF])
-        of_own = dot_nt(jnp.concatenate(own[2 - a : 2 - a + NX], axis=1), far3_ref[...])
+        of_own = dot_nt(own_ref[:, at : at + HALF], far3_ref[...])
         return jnp.where(upward, of_own, of_far), jnp.where(upward, of_far, of_own)
 
     pairs = [across(a) for a in range(3)]
 
     def block(a, b):
         value = gk_ref[b * ROWS + a * CH : b * ROWS + (a + 1) * CH, :]
-        if a != 1:
-            face, side = (above_ref, 1) if a == 0 else (below_ref, 0)
-            rows = [y for y in range(NY) if 0 <= y - (b - 1) < NY]
-            of_g = (rows[0] - (b - 1)) * LANES
-            of_a = side * HALF + rows[0] * LANES
-            size = len(rows) * LANES
-            value = value + dot_nt(face[:, of_g : of_g + size], column_ref[:, of_a : of_a + size])
-        if b != 1:
-            value = value + pairs[a][b // 2]
-        return value
+        return value if b == 1 else value + pairs[a][b // 2]
 
     pad = jnp.zeros((CH, 2 * LANES - ROWS), F32)
     lane = lax.broadcasted_iota(jnp.int32, (CH, LANES), 1)
@@ -184,23 +193,30 @@
         inner_kernel,
         (shape((3 * ROWS, ROWS), F32), shape((ROWS, 2 * HALF), BF16), shape((ROWS, 2 * HALF), BF16)),
         [pltpu.VMEM((ROWS, HALF), BF16)],
-        pl.CostEstimate(flops=20 * 10**9, transcendentals=0, bytes_accessed=2**20),
     )(*operands)
 
 
-def run_message(core, *operands):
+def with_core(body, out_shape, scratch, core, operands):
     vmem = pl.BlockSpec(memory_space=pltpu.VMEM)
     return call(
-        message_kernel,
-        jax.ShapeDtypeStruct((32, 8, HALF), F32),
-        [
-            pltpu.VMEM((16, CH, LANES), F32),
-            pltpu.VMEM((ROWS, WIDE), BF16),
-            pltpu.VMEM((ROWS, HALF), BF16),
-        ],
+        body,
+        out_shape,
+        scratch,
         in_specs=[pl.BlockSpec(memory_space=pltpu.SMEM)] + [vmem] * len(operands),
-        out_specs=vmem,
+        out_specs=jax.tree.map(lambda _: vmem, out_shape),
     )(core.reshape(1), *operands)
+
+
+def run_faces(core, *operands):
+    shape = jax.ShapeDtypeStruct
+    out_shape = (shape((3 * ROWS, ROWS), F32), shape((ROWS, WIDE), BF16), shape((CH, WIDE), BF16))
+    return with_core(faces_kernel, out_shape, (), core, operands)
+
+
+def run_message(core, *operands):
+    out_shape = jax.ShapeDtypeStruct((32, 8, HALF), F32)
+    scratch = [pltpu.VMEM((16, CH, LANES), F32), pltpu.VMEM((ROWS, HALF), BF16)]
+    return with_core(message_kernel, out_shape, scratch, core, operands)
 
 
 def rows_kernel(core_ref, g_ref, a_ref, ahead_ref, behind_ref, last_ref, first_ref):
@@ -270,7 +286,7 @@
     above = shifted_by(first_face, "px", -1)
     inner = run_inner(g, a)
     weights, *inner = lax.optimization_barrier((weights, *inner))
-    message = run_message(core, g, *inner, below, above, far)
+    message = run_message(core, *run_faces(core, g, *inner, below, above), far)
 
     parts = lax.all_to_all(message, ("core", "px", "y"), 0, 0)
     mine = jnp.sum(parts, axis=0)

time: 103 us -> 103 us (level)
  no operation moved by 1% of the time
where the time goes in v10:
time: 103 us; the launch traced here: 102 us
  starting transfers between devices  76.1 us (74%)
  waiting for transfers between devices  16.7 us (16%)
  local copies, waits for them, and re-layouts  4.09 us (4%)
  Pallas kernels  3.71 us (4%)
    all_to_all x1, starting transfers between devices, local(): lax.all_to_all(jnp.broadcast_to(mine.reshape(1, 8, 4, LANES), (4, 8, 4, L...  25.2 us
    ppermute x2, starting transfers between devices, along_y(): return lax.ppermute(x, ('core', 'y', 'zhi'), pairs)  17 us
    all_to_all x1, starting transfers between devices, local(): parts = lax.all_to_all(message, ('core', 'px', 'y'), 0, 0)  15.4 us
    ppermute x4, starting transfers between devices, shifted_by(): return lax.ppermute(x, axis, pairs)  11.8 us
    all_to_all x1, waiting for transfers between devices, local(): parts = lax.all_to_all(message, ('core', 'px', 'y'), 0, 0)  9.64 us
    all_to_all x1, starting transfers between devices, local(): lax.all_to_all(jnp.broadcast_to(mine, (16, 4, LANES)), ('px', 'y'), 0, 0)  6.66 us
    all_to_all x1, waiting for transfers between devices, local(): lax.all_to_all(jnp.broadcast_to(mine, (16, 4, LANES)), ('px', 'y'), 0, 0)  4.29 us
    ppermute x4, waiting for transfers between devices, shifted_by(): return lax.ppermute(x, axis, pairs)  2.77 us
  transfers between devices with their start and end apart: 9, of which 3 were waited for; matrix products, arithmetic and copies ran while one was open for 3% of the time, Pallas kernels for 2%

profile of v10, /device:TPU:2, one launch (start us, length us, event | category | flops | bytes accessed | tf_op | source)
XLA Modules:
  0.0 102.2 jit_solution(5195204840000388984)
XLA Ops:
  0.6 0.0 copy-start
  0.6 1.2 %reshape.33.g_ref = bf16[64,2048]{1,0:T(8,128)(2,1)S(1)} reshape(bf16[1,64,4,4,128]{4,3,2,1,0:T(4,128)(2,1)} %param.4) | data formatting | bytes 524288 | tf_op jit(solution)/shard_map/reshape | solution.py:275
  1.8 0.0 copy-done
  1.8 0.2 reshape.36.a_ref
  2.0 0.1 shard_map.51
  2.1 15.7 %collective-permute-start.2 = (bf16[64,1024]{1,0:T(8,128)(2,1)S(1)}, bf16[64,1024]{1,0:T(8,128)(2,1)S(1)}, u32[]{:S(2)}, u32[]{:S(2)}) collective-permute-start(bf16[64,1024]{1,0:T(8,128)(2,1)S(1)} %get-tuple-element.31), channel_id=1, source_target_pairs={{0,1},{1,2},{2,3},{3,4},{4,5},{5,6},{6,7},{7,8},{8,9},{9,10},{10,1... | collective-permute-start | bytes 393224 | tf_op jit(solution)/shard_map/ppermute | solution.py:270
  17.8 3.4 %collective-permute-start = (bf16[64,768]{1,0:T(8,128)(2,1)S(1)}, bf16[64,768]{1,0:T(8,128)(2,1)S(1)}, u32[]{:S(2)}, u32[]{:S(2)}) collective-permute-start(bf16[64,768]{1,0:T(8,128)(2,1)S(1)} %get-tuple-element.26), channel_id=1, source_target_pairs={{0,16},{16,32},{32,48},{1,17},{17,33},{33,49},{2,18},{18,34},{34,5... | collective-permute-start | bytes 294920 | tf_op jit(solution)/shard_map/ppermute | solution.py:255
  21.2 0.0 copy-start.1
  21.2 2.6 %collective-permute-start.1 = (bf16[64,768]{1,0:T(8,128)(2,1)S(1)}, bf16[64,768]{1,0:T(8,128)(2,1)S(1)}, u32[]{:S(2)}, u32[]{:S(2)}) collective-permute-start(bf16[64,768]{1,0:T(8,128)(2,1)S(1)} %get-tuple-element.27), channel_id=1, source_target_pairs={{16,0},{32,16},{48,32},{17,1},{33,17},{49,33},{18,2},{34,18},{50,3... | collective-permute-start | bytes 294920 | tf_op jit(solution)/shard_map/ppermute | solution.py:255
  23.8 0.9 shard_map.50
  24.7 0.0 copy-done.1
  24.7 0.3 reshape.34
  25.1 0.0 collective-permute-done.below_ref
  25.1 2.8 %collective-permute-done.1.above_ref = bf16[64,768]{1,0:T(8,128)(2,1)S(1)} collective-permute-done((bf16[64,768]{1,0:T(8,128)(2,1)S(1)}, bf16[64,768]{1,0:T(8,128)(2,1)S(1)}, u32[]{:S(2)}, u32[]{:S(2)}) %collective-permute-start.1) | collective-permute-done | bytes 98336 | tf_op jit(solution)/shard_map/ppermute | solution.py:255
  27.9 0.5 shard_map.52
  28.4 0.0 collective-permute-done.2.far_ref
  28.4 1.4 %shard_map.53 = f32[32,8,512]{2,1,0:T(8,128)} custom-call(s32[1]{0:T(128)} %bitcast.core_ref, f32[576,192]{1,0:T(8,128)S(1)} %get-tuple-element.28.gk_ref, bf16[192,768]{1,0:T(8,128)(2,1)S(1)} %get-tuple-element.29.rim_ref, bf16[64,768]{1,0:T(8,128)(2,1)S(1)} %get-tuple-element.30.own_ref, bf16[64,1024]{1,0:T(8,128)(2,1)S(1)} %collective-permute-done.2.far_ref), custom_call_target="tpu_custom_call" | custom-call | tf_op jit(solution)/shard_map/pallas_call | solution.py:201
  29.8 15.4 %all-to-all-start = ((f32[32,8,512]{2,1,0:T(8,128)}), f32[32,8,512]{2,1,0:T(8,128)S(1)}, u32[]{:S(2)}, u32[]{:S(2)}) async-start(f32[32,8,512]{2,1,0:T(8,128)} %shard_map.53), calls=%async_computation | async-start | bytes 1048576 | tf_op jit(solution)/shard_map/all_to_all | solution.py:291
  45.2 1.3 %collective-permute-start.3 = (bf16[64,512]{1,0:T(8,128)(2,1)S(1)}, bf16[64,512]{1,0:T(8,128)(2,1)S(1)}, u32[]{:S(2)}, u32[]{:S(2)}) collective-permute-start(bf16[64,512]{1,0:T(8,128)(2,1)S(1)} %get-tuple-element.36), channel_id=1, source_target_pairs={{1,0},{2,1},{3,2},{4,3},{5,4},{6,5},{7,6},{8,7},{9,8},{10,9},{11,1... | collective-permute-start | bytes 196616 | tf_op jit(solution)/shard_map/ppermute | solution.py:270
  46.5 9.6 %all-to-all-done = f32[32,8,512]{2,1,0:T(8,128)S(1)} async-done(((f32[32,8,512]{2,1,0:T(8,128)}), f32[32,8,512]{2,1,0:T(8,128)S(1)}, u32[]{:S(2)}, u32[]{:S(2)}) %all-to-all-start) | async-done | bytes 524320 | tf_op jit(solution)/shard_map/all_to_all | solution.py:291
  56.2 0.6 broadcast_in_dim.11
  56.8 25.2 %all-to-all-start.1 = ((f32[32,4,128]{2,1,0:T(4,128)}), f32[32,4,128]{2,1,0:T(4,128)S(1)}, u32[]{:S(2)}, u32[]{:S(2)}) async-start(f32[32,4,128]{2,1,0:T(4,128)} %bitcast.3), calls=%async_computation.1 | async-start | bytes 131072 | tf_op jit(solution)/shard_map/all_to_all | solution.py:296
  82.0 0.0 collective-permute-done.3
  82.1 3.2 %collective-permute-start.5 = (bf16[64,256]{1,0:T(8,128)(2,1)S(1)}, bf16[64,256]{1,0:T(8,128)(2,1)S(1)}, u32[]{:S(2)}, u32[]{:S(2)}) collective-permute-start(bf16[64,256]{1,0:T(8,128)(2,1)S(1)} %pad_maximum_fusion.1), channel_id=1, source_target_pairs={{16,0},{32,16},{48,32},{17,1},{33,17},{49,33},{18,2},{34,18},{50,3... | collective-permute-start | bytes 98312 | tf_op jit(solution)/shard_map/ppermute | solution.py:255
  85.3 2.7 %collective-permute-start.4 = (bf16[64,256]{1,0:T(8,128)(2,1)S(1)}, bf16[64,256]{1,0:T(8,128)(2,1)S(1)}, u32[]{:S(2)}, u32[]{:S(2)}) collective-permute-start(bf16[64,256]{1,0:T(8,128)(2,1)S(1)} %pad_maximum_fusion), channel_id=1, source_target_pairs={{0,16},{16,32},{32,48},{1,17},{17,33},{33,49},{2,18},{18,34},{34,5... | collective-permute-start | bytes 98312 | tf_op jit(solution)/shard_map/ppermute | solution.py:255
  88.0 0.0 all-to-all-done.1
  88.0 0.6 broadcast_in_dim.12
  88.7 6.7 %all-to-all-start.2 = ((f32[16,4,128]{2,1,0:T(4,128)}), f32[16,4,128]{2,1,0:T(4,128)S(1)}, u32[]{:S(2)}, u32[]{:S(2)}) async-start(f32[16,4,128]{2,1,0:T(4,128)} %broadcast_in_dim.12), calls=%async_computation.2 | async-start | bytes 65536 | tf_op jit(solution)/shard_map/all_to_all | solution.py:306
  95.3 0.2 copy.14.w_ref
  95.5 0.0 collective-permute-done.5.corner_above_ref
  95.5 0.0 collective-permute-done.4.corner_below_ref
  95.5 0.9 shard_map.54
  96.4 0.9 reshape.38
  97.3 4.3 %all-to-all-done.2 = f32[16,4,128]{2,1,0:T(4,128)S(1)} async-done(((f32[16,4,128]{2,1,0:T(4,128)}), f32[16,4,128]{2,1,0:T(4,128)S(1)}, u32[]{:S(2)}, u32[]{:S(2)}) %all-to-all-start.2) | async-done | bytes 32800 | tf_op jit(solution)/shard_map/all_to_all | solution.py:306
  101.6 0.6 slice_multiply_fusion
  (9 shorter events, 0.2 us)
Async XLA Ops:
  0.6 1.2 %copy-start = (bf16[1,64,4,4,128]{4,3,2,1,0:T(4,128)(2,1)S(1)}, bf16[1,64,4,4,128]{4,3,2,1,0:T(4,128)(2,1)}, u32[]{:S(2)}) copy-start(bf16[1,64,4,4,128]{4,3,2,1,0:T(4,128)(2,1)} %param.3) | copy-start | bytes 786436
  2.1 26.3 %collective-permute-start.2 = (bf16[64,1024]{1,0:T(8,128)(2,1)S(1)}, bf16[64,1024]{1,0:T(8,128)(2,1)S(1)}, u32[]{:S(2)}, u32[]{:S(2)}) collective-permute-start(bf16[64,1024]{1,0:T(8,128)(2,1)S(1)} %get-tuple-element.31), channel_id=1, source_target_pairs={{0,1},{1,2},{2,3},{3,4},{4,5},{5,6},{6,7},{7,8},{8,9},{9,10},{10,1... | collective-permute-start | bytes 393224 | tf_op jit(solution)/shard_map/ppermute | solution.py:270
  17.8 7.3 %collective-permute-start = (bf16[64,768]{1,0:T(8,128)(2,1)S(1)}, bf16[64,768]{1,0:T(8,128)(2,1)S(1)}, u32[]{:S(2)}, u32[]{:S(2)}) collective-permute-start(bf16[64,768]{1,0:T(8,128)(2,1)S(1)} %get-tuple-element.26), channel_id=1, source_target_pairs={{0,16},{16,32},{32,48},{1,17},{17,33},{33,49},{2,18},{18,34},{34,5... | collective-permute-start | bytes 294920 | tf_op jit(solution)/shard_map/ppermute | solution.py:255
  21.2 3.5 %copy-start.1 = (bf16[64,1728]{1,0:T(8,128)(2,1)S(1)}, bf16[64,1728]{1,0:T(8,128)(2,1)}, u32[]{:S(2)}) copy-start(bf16[64,1728]{1,0:T(8,128)(2,1)} %param.5) | copy-start | bytes 663556
  21.2 6.6 %collective-permute-start.1 = (bf16[64,768]{1,0:T(8,128)(2,1)S(1)}, bf16[64,768]{1,0:T(8,128)(2,1)S(1)}, u32[]{:S(2)}, u32[]{:S(2)}) collective-permute-start(bf16[64,768]{1,0:T(8,128)(2,1)S(1)} %get-tuple-element.27), channel_id=1, source_target_pairs={{16,0},{32,16},{48,32},{17,1},{33,17},{49,33},{18,2},{34,18},{50,3... | collective-permute-start | bytes 294920 | tf_op jit(solution)/shard_map/ppermute | solution.py:255
  29.8 26.3 %all-to-all-start = ((f32[32,8,512]{2,1,0:T(8,128)}), f32[32,8,512]{2,1,0:T(8,128)S(1)}, u32[]{:S(2)}, u32[]{:S(2)}) async-start(f32[32,8,512]{2,1,0:T(8,128)} %shard_map.53), calls=%async_computation | async-start | bytes 1048576 | tf_op jit(solution)/shard_map/all_to_all | solution.py:291
  45.2 36.9 %collective-permute-start.3 = (bf16[64,512]{1,0:T(8,128)(2,1)S(1)}, bf16[64,512]{1,0:T(8,128)(2,1)S(1)}, u32[]{:S(2)}, u32[]{:S(2)}) collective-permute-start(bf16[64,512]{1,0:T(8,128)(2,1)S(1)} %get-tuple-element.36), channel_id=1, source_target_pairs={{1,0},{2,1},{3,2},{4,3},{5,4},{6,5},{7,6},{8,7},{9,8},{10,9},{11,1... | collective-permute-start | bytes 196616 | tf_op jit(solution)/shard_map/ppermute | solution.py:270
  56.8 31.2 %all-to-all-start.1 = ((f32[32,4,128]{2,1,0:T(4,128)}), f32[32,4,128]{2,1,0:T(4,128)S(1)}, u32[]{:S(2)}, u32[]{:S(2)}) async-start(f32[32,4,128]{2,1,0:T(4,128)} %bitcast.3), calls=%async_computation.1 | async-start | bytes 131072 | tf_op jit(solution)/shard_map/all_to_all | solution.py:296
  82.1 13.4 %collective-permute-start.5 = (bf16[64,256]{1,0:T(8,128)(2,1)S(1)}, bf16[64,256]{1,0:T(8,128)(2,1)S(1)}, u32[]{:S(2)}, u32[]{:S(2)}) collective-permute-start(bf16[64,256]{1,0:T(8,128)(2,1)S(1)} %pad_maximum_fusion.1), channel_id=1, source_target_pairs={{16,0},{32,16},{48,32},{17,1},{33,17},{49,33},{18,2},{34,18},{50,3... | collective-permute-start | bytes 98312 | tf_op jit(solution)/shard_map/ppermute | solution.py:255
  85.3 10.2 %collective-permute-start.4 = (bf16[64,256]{1,0:T(8,128)(2,1)S(1)}, bf16[64,256]{1,0:T(8,128)(2,1)S(1)}, u32[]{:S(2)}, u32[]{:S(2)}) collective-permute-start(bf16[64,256]{1,0:T(8,128)(2,1)S(1)} %pad_maximum_fusion), channel_id=1, source_target_pairs={{0,16},{16,32},{32,48},{1,17},{17,33},{33,49},{2,18},{18,34},{34,5... | collective-permute-start | bytes 98312 | tf_op jit(solution)/shard_map/ppermute | solution.py:255
  88.7 12.9 %all-to-all-start.2 = ((f32[16,4,128]{2,1,0:T(4,128)}), f32[16,4,128]{2,1,0:T(4,128)S(1)}, u32[]{:S(2)}, u32[]{:S(2)}) async-start(f32[16,4,128]{2,1,0:T(4,128)} %broadcast_in_dim.12), calls=%async_computation.2 | async-start | bytes 65536 | tf_op jit(solution)/shard_map/all_to_all | solution.py:306
